TPU v7x, 32 devices: a whole 2x2x4 slice. The times are simulated.
32 devices in a mesh: scene: 2 (over x), slab: 4 (over y, core), sub: 4 (over z).
Axes of the slice: x: 2, y: 2, z: 4, core: 2. Of those that a mesh axis runs over, the one named last changes fastest.
Arguments:
- coarse_in: bfloat16 [32, 128, 16, 128], P(('scene', 'slab'), 'sub'), parts along dimension 0, may hold values from -110 to 290
- coarse_weight: bfloat16 [27, 128, 128], replicated, may hold values from -0.109375 to 0.109375
- norm_gain: float32 [128], replicated, may hold values from 0.25 to 1.75
- norm_bias: float32 [128], replicated, may hold values from -3 to 3
- lift_weight: bfloat16 [128, 128], replicated, may hold values from -0.5 to 0.5
- fine_input: bfloat16 [256, 512, 128], P(('scene', 'slab', 'sub')), parts along dimension 0, may hold values from -6 to 6
- block_coords: int32 [256, 3], P(('scene', 'slab', 'sub')), parts along dimension 0, may hold values from 0 to 31, as said below
- neighbours: int32 [256, 6], P(('scene', 'slab', 'sub')), parts along dimension 0, may hold values from -1 to 127, as said below
- fine_weight: bfloat16 [27, 128, 128], replicated, may hold values from -0.109375 to 0.109375
Outputs:
- fine_out: bfloat16 [256, 512, 128], P(('scene', 'slab', 'sub')), parts along dimension 0
There are 2 independent parts, one for each index of `scene`. A program takes and returns all parts, laid end to end along the dimension named above; an argument that names none is the same for every part. Nothing has to cross between parts.
Inputs may be any that keep to these rules, and one draw needn't show every extreme that they name: `block_coords`: rows name distinct blocks. The 8 blocks of one device form 8 // 4 clusters of 2 x 2 x 1 face-adjacent blocks (first and second coordinate), each with its first coordinate in an aligned pair (2 p, 2 p + 1) and no two clusters of a device in the same pair, so that exactly 0 or 2 of one device's blocks have any given first coordinate. Every block of the device with sub index u has its second coordinate in [u * 8, (u + 1) * 8). Within a device the blocks stand in any order. `neighbours`: entries are row indices of all blocks of the scene. Entry d names the listed block that shares a face with the row's block on side d, in the order -first, +first, -second, +second, -third, +third coordinate, or is -1. Each block lists exactly two, both of its own cluster, so every listed block belongs to the same device; the lists are symmetric.
All inputs are finite; a program needn't handle non-finite values.
Results may differ from a plain program's by a relative error of at most 0.0056.
Values may be sent and summed in bfloat16 or wider, within the bound.
No kernel may reach another device: no remote copies, remote signals or barrier semaphores. Data moves between devices by JAX's collectives and lax.ppermute only.
A program may use at most 128 MiB of HBM per device.

v0:
```python
import jax
import jax.numpy as jnp
from jax import lax
from jax.sharding import PartitionSpec as P

G = 32
FB = 8
MOST = 2


def padded_2(value, sides, width):
    for axis, dim in sides:
        count, length = (lax.axis_size(axis), value.shape[dim])
        up = [(i, (i + 1) % count) for i in range(count - 1)]
        down = [(j, i) for i, j in up]
        last = lax.slice_in_dim(value, length - width, length, axis=dim)
        initial = lax.slice_in_dim(value, 0, width, axis=dim)
        before = lax.ppermute(last, axis, up)
        after = lax.ppermute(initial, axis, down)
        value = jnp.concatenate([before, value, after], axis=dim)
    return value


def convolve(padded, weights):
    batches = padded.shape[0]
    span_x = padded.shape[1] - 2
    span_y = padded.shape[2] - 2
    span_z = padded.shape[3] - 2
    channels = padded.shape[4]
    summed = jnp.zeros((batches * span_x * span_y * span_z, channels), jnp.float32)
    for along_x in range(3):
        for along_y in range(3):
            window = jnp.concatenate(
                [
                    padded[
                        :,
                        along_x : along_x + span_x,
                        along_y : along_y + span_y,
                        along_z : along_z + span_z,
                        :,
                    ]
                    for along_z in range(3)
                ],
                axis=-1,
            )
            window = window.reshape(-1, 3 * channels)
            first_tap = 9 * along_x + 3 * along_y
            stacked = weights[first_tap : first_tap + 3].reshape(3 * channels, channels)
            summed = summed + jnp.dot(window, stacked, preferred_element_type=jnp.float32)
    return summed


def upsample(pieces):
    batches = pieces.shape[0]
    channels = pieces.shape[2]
    cube_edge = FB // 2
    stretched = pieces.reshape(batches, cube_edge, 1, cube_edge, 1, cube_edge, 1, channels)
    stretched = jnp.broadcast_to(
        stretched, (batches, cube_edge, 2, cube_edge, 2, cube_edge, 2, channels)
    )
    return stretched.reshape(batches, FB * FB * FB, channels)


def block_planes(blocks):
    return (
        blocks[:, -1],
        blocks[:, 0],
        blocks[:, :, -1],
        blocks[:, :, 0],
        blocks[:, :, :, -1],
        blocks[:, :, :, 0],
    )


def framed(blocks, planes, links):
    padded = jnp.pad(blocks, ((0, 0), (1, 1), (1, 1), (1, 1), (0, 0)))
    faces = []
    for direction in range(6):
        target = links[:, direction]
        picked = jnp.take(planes[direction], jnp.maximum(target, 0), axis=0)
        faces.append(jnp.where((target >= 0)[:, None, None, None], picked, jnp.zeros_like(picked)))
    padded = padded.at[:, 0, 1:-1, 1:-1].set(faces[0])
    padded = padded.at[:, -1, 1:-1, 1:-1].set(faces[1])
    padded = padded.at[:, 1:-1, 0, 1:-1].set(faces[2])
    padded = padded.at[:, 1:-1, -1, 1:-1].set(faces[3])
    padded = padded.at[:, 1:-1, 1:-1, 0].set(faces[4])
    padded = padded.at[:, 1:-1, 1:-1, -1].set(faces[5])
    return padded


def body(
    coarse_in,
    coarse_weight,
    norm_gain,
    norm_bias,
    lift_weight,
    fine_input,
    block_coords,
    neighbours,
    fine_weight,
):
    depth_x, depth_y, depth_z, channels = coarse_in.shape
    rimmed = padded_2(coarse_in, (("slab", 0), ("sub", 1)), 1)
    padded = jnp.pad(rimmed, ((0, 0), (0, 0), (1, 1), (0, 0)))[None]
    filtered = convolve(padded, coarse_weight).reshape(-1, G, channels // G)
    entries = lax.axis_size("slab") * lax.axis_size("sub") * filtered.shape[0] * (channels // G)
    moment_one, moment_two = lax.psum(
        (jnp.sum(filtered, axis=(0, 2)), jnp.sum(filtered * filtered, axis=(0, 2))), ("slab", "sub")
    )
    group_mean = moment_one / entries
    spread = moment_two / entries - group_mean * group_mean
    centred = filtered - group_mean[None, :, None]
    normed = centred * lax.rsqrt(spread + 1e-05)[None, :, None]
    normed = normed.reshape(-1, channels) * norm_gain + norm_bias
    activated = jax.nn.silu(normed).astype(jnp.bfloat16)
    cube_edge = FB // 2
    y_cubes = depth_y // cube_edge
    z_cubes = depth_z // cube_edge
    slab_count = lax.axis_size("slab")
    shaped = (
        jnp.dot(activated, lift_weight, preferred_element_type=jnp.float32)
        .astype(jnp.bfloat16)
        .reshape(depth_x, y_cubes, cube_edge, z_cubes, cube_edge, channels)
    )
    stock = shaped.transpose(1, 3, 0, 2, 4, 5).reshape(y_cubes * z_cubes, cube_edge**3, channels)
    block_total = block_coords.shape[0]
    holder = block_coords[:, 0]
    wanted = block_coords[:, 1] % y_cubes * z_cubes + block_coords[:, 2]
    places = jnp.arange(block_total, dtype=jnp.int32)
    earlier = (holder[:, None] == holder[None, :]) & (places[None, :] < places[:, None])
    slot_rank = jnp.sum(earlier.astype(jnp.int32), axis=1)
    to_holder = (holder[:, None] == jnp.arange(slab_count, dtype=jnp.int32)[None, :]).astype(
        jnp.int32
    )
    to_rank = (slot_rank[:, None] == jnp.arange(MOST, dtype=jnp.int32)[None, :]).astype(jnp.int32)
    requests = jnp.sum(to_holder[:, :, None] * to_rank[:, None, :] * wanted[:, None, None], axis=0)
    asked_for = lax.all_to_all(requests, "slab", split_axis=0, concat_axis=0, tiled=True)
    sources, item_count = asked_for.shape
    picked = jnp.take(stock, asked_for.reshape(-1), axis=0)
    upsampled = upsample(picked).reshape(sources, item_count, FB * FB * FB, channels)
    replies = lax.all_to_all(upsampled, "slab", split_axis=0, concat_axis=0, tiled=True)
    flat_replies = replies.reshape(slab_count * MOST, replies.shape[2], channels)
    reply_index = holder * MOST + slot_rank
    arrived = jnp.take(flat_replies, reply_index, axis=0)
    block_input = (fine_input.astype(jnp.float32) + arrived.astype(jnp.float32)).astype(
        jnp.bfloat16
    )
    blocks = block_input.reshape(block_total, FB, FB, FB, channels)
    local_links = jnp.where(neighbours >= 0, neighbours % block_total, -1)
    summed = convolve(framed(blocks, block_planes(blocks), local_links), fine_weight)
    result = blocks.reshape(-1, channels).astype(jnp.float32) + summed
    return result.astype(jnp.bfloat16).reshape(block_total, FB * FB * FB, channels)


def solution(mesh):
    in_specs = (
        P(("scene", "slab"), "sub", None, None),
        P(),
        P(),
        P(),
        P(),
        P(("scene", "slab", "sub"), None, None),
        P(("scene", "slab", "sub"), None),
        P(("scene", "slab", "sub"), None),
        P(),
    )
    out_specs = P(("scene", "slab", "sub"), None, None)
    return jax.shard_map(body, mesh=mesh, in_specs=in_specs, out_specs=out_specs, check_vma=False)
```

profile of v0, /device:TPU:0, one launch (start us, length us, event | category | flops | bytes accessed | tf_op | source)
XLA Modules:
  0.0 170.1 jit_solution(3519476358454260548)
XLA Ops:
  0.0 0.7 slice_bitcast_fusion.4
  0.7 0.8 fusion.20
  1.8 0.7 copy.51
  2.5 4.3 %all-to-all-start = ((s32[4,1,2]{2,1,0:T(1,128)}), s32[4,1,2]{2,1,0:T(1,128)S(1)}, u32[]{:S(2)}, u32[]{:S(2)}) async-start(s32[4,1,2]{2,1,0:T(1,128)} %copy.51), calls=%async_computation | async-start | bytes 4096 | tf_op jit(solution)/shard_map/all_to_all | solution.py:137
  6.7 1.0 fusion.33
  7.7 1.3 collective-permute-start.1
  9.0 3.0 %collective-permute-start = (bf16[1,32,16,128]{3,2,1,0:T(8,128)(2,1)S(1)}, bf16[1,32,16,128]{3,2,1,0:T(8,128)(2,1)S(1)}, u32[]{:S(2)}, u32[]{:S(2)}) collective-permute-start(bf16[1,32,16,128]{3,2,1,0:T(8,128)(2,1)S(1)} %get-tuple-element.177), channel_id=1, source_target_pairs={{0,4},{4,8},{8,12},{1,5},{5,9},{9,13},{2,6},{6,10},{10,14},{3,7},{... | collective-permute-start | bytes 393224 | tf_op jit(solution)/shard_map/ppermute | solution.py:18
  12.1 0.7 and_bitcast_fusion
  12.8 0.8 copy.53
  13.6 1.3 fusion.31
  15.5 0.7 reduce.21
  16.3 1.1 constant_dynamic-update-slice_fusion.1
  17.5 3.9 %collective-permute-start.2 = (bf16[6,1,16,128]{3,2,1,0:T(8,128)(2,1)S(1)}, bf16[6,1,16,128]{3,2,1,0:T(8,128)(2,1)S(1)}, u32[]{:S(2)}, u32[]{:S(2)}) collective-permute-start(bf16[6,1,16,128]{3,2,1,0:T(8,128)(2,1)S(1)} %get-tuple-element.174), channel_id=1, source_target_pairs={{0,1},{1,2},{2,3},{4,5},{5,6},{6,7},{8,9},{9,10},{10,11},{12,13},{... | collective-permute-start | bytes 73736 | tf_op jit(solution)/shard_map/ppermute | solution.py:18
  21.4 1.3 collective-permute-start.3
  22.9 4.2 %collective-permute-done.3 = bf16[6,1,16,128]{3,2,1,0:T(8,128)(2,1)S(1)} collective-permute-done((bf16[6,1,16,128]{3,2,1,0:T(8,128)(2,1)S(1)}, bf16[6,1,16,128]{3,2,1,0:T(8,128)(2,1)S(1)}, u32[]{:S(2)}, u32[]{:S(2)}) %collective-permute-start.3) | collective-permute-done | bytes 24608 | tf_op jit(solution)/shard_map/ppermute | solution.py:19
  27.1 0.7 fusion.8
  27.8 0.6 fusion.28
  28.4 2.5 %fusion.27 = (bf16[1,4,32,16,128]{4,3,2,1,0:T(8,128)(2,1)S(1)}, bf16[1,4,32,16,128]{4,3,2,1,0:T(8,128)(2,1)S(1)}, bf16[1,4,32,16,128]{4,3,2,1,0:T(8,128)(2,1)S(1...) fusion(bf16[1,6,34,18,128]{4,3,2,1,0:T(8,128)(2,1)S(1)} %fusion.8), kind=kLoop, calls=%fused_computation.137 | loop fusion | bytes 19922944 | tf_op jit(solution)/shard_map/slice | solution.py:35
  31.9 0.6 convolution_add_fusion.15
  33.7 0.6 convolution_add_fusion.13
  37.6 0.7 fusion.24
  38.8 31.3 %all-reduce.2 = (f32[32]{0:T(128)S(1)}, f32[32]{0:T(128)S(1)}) all-reduce(f32[32]{0:T(128)S(1)} %reduce_sum.60, f32[32]{0:T(128)S(1)} %reduce_sum.57), channel_id=1, replica_groups=mesh['scene'=2,'slab'=4,'sub'=4] {'slab','sub'}, use_global_device_ids=true, to_apply=%region_7.8 | all-reduce | flops 64 | bytes 512 | tf_op jit(solution)/shard_map/psum | solution.py:107
  71.9 1.7 broadcast_in_dim.96
  73.6 3.8 %all-to-all-start.1 = ((bf16[4,2,512,128]{3,2,1,0:T(8,128)(2,1)}), bf16[4,2,512,128]{3,2,1,0:T(8,128)(2,1)S(1)}, u32[]{:S(2)}, u32[]{:S(2)}) async-start(bf16[4,2,512,128]{3,2,1,0:T(8,128)(2,1)} %bitcast.30), calls=%async_computation.1 | async-start | bytes 2097152 | tf_op jit(solution)/shard_map/all_to_all | solution.py:141
  77.5 0.6 compare_bitcast_fusion
  78.1 0.9 fusion.30
  79.0 12.7 %all-to-all-done.1 = bf16[4,2,512,128]{3,2,1,0:T(8,128)(2,1)S(1)} async-done(((bf16[4,2,512,128]{3,2,1,0:T(8,128)(2,1)}), bf16[4,2,512,128]{3,2,1,0:T(8,128)(2,1)S(1)}, u32[]{:S(2)}, u32[]{:S(2)}) %all-to-all-start.1) | async-done | bytes 1048608 | tf_op jit(solution)/shard_map/all_to_all | solution.py:141
  91.7 0.7 gather_fusion.1
  92.9 0.9 slice_bitcast_fusion
  93.7 0.7 slice_bitcast_fusion.2
  95.6 0.9 copy.64
  97.2 0.9 copy.62
  98.1 2.0 %pad.33 = bf16[8,10,10,10,128]{4,3,2,1,0:T(8,128)(2,1)S(1)} pad(bf16[8,8,8,8,128]{4,3,2,1,0:T(8,128)(2,1)} %bitcast.172, bf16[]{:T(256)} %constant.274.clone.1), padding=0_0x1_1x1_1x1_1x0_0 | pad | bytes 3096578 | tf_op jit(solution)/shard_map/jit(_pad)/pad | solution.py:76
  100.1 1.5 gather_fusion.5
  101.6 2.1 %gather_fusion.4 = bf16[8,8,8,128]{3,2,1,0:T(8,128)(2,1)} fusion(bf16[8,8,8,128]{3,2,1,0:T(8,128)(2,1)} %get-tuple-element.153, s32[1024]{0:T(1024)S(1)} %get-tuple-element.208), kind=kCustom, calls=%fused_computation.2.clone | custom fusion | bytes 262176 | tf_op jit(solution)/shard_map/jit(_take)/gather | solution.py:80
  103.7 2.1 %gather_fusion.3 = bf16[8,8,8,128]{3,2,1,0:T(8,128)(2,1)} fusion(bf16[8,8,8,128]{3,2,1,0:T(8,128)(2,1)} %get-tuple-element.154, s32[1024]{0:T(1024)S(1)} %get-tuple-element.209), kind=kCustom, calls=%fused_computation.1.clone | custom fusion | bytes 262176 | tf_op jit(solution)/shard_map/jit(_take)/gather | solution.py:80
  105.8 2.1 %gather_fusion.2 = bf16[8,8,8,128]{3,2,1,0:T(8,128)(2,1)} fusion(bf16[8,8,8,128]{3,2,1,0:T(8,128)(2,1)} %get-tuple-element.155, s32[1024]{0:T(1024)S(1)} %get-tuple-element.210), kind=kCustom, calls=%fused_computation.clone | custom fusion | bytes 262176 | tf_op jit(solution)/shard_map/jit(_take)/gather | solution.py:80
  108.0 1.6 fusion.12
  109.6 1.6 fusion.13
  111.3 1.6 fusion.14
  112.9 1.2 scatter.20
  114.1 1.2 scatter.21
  115.3 1.2 scatter.24
  116.5 0.7 fusion.11
  117.2 1.2 scatter.25
  118.4 6.2 %scatter.26 = bf16[8,10,10,10,128]{4,3,2,1,0:T(8,128)(2,1)S(1)} dynamic-update-slice(bf16[8,10,10,10,128]{4,3,2,1,0:T(8,128)(2,1)S(1)} %scatter.25, bf16[8,8,8,1,128]{4,3,2,1,0:T(2,128)(2,1)} %copy.62, s32[]{:T(128)} %constant.268.clone.1, s32[]{:T(128)} %constant.281.clone.1, s32[]{:T(128)} %constant.281.clone.1, s32[]{:T(128)} %constant.268.clone.1, s32[]{:T(128)} %constant.268.clone.1) | dynamic-update-slice | bytes 262148 | tf_op jit(solution)/shard_map/scatter | solution.py:86
  124.6 6.2 %scatter.29 = bf16[8,10,10,10,128]{4,3,2,1,0:T(8,128)(2,1)S(1)} dynamic-update-slice(bf16[8,10,10,10,128]{4,3,2,1,0:T(8,128)(2,1)S(1)} %scatter.26, bf16[8,8,8,1,128]{4,3,2,1,0:T(2,128)(2,1)} %copy.64, s32[]{:T(128)} %constant.268.clone.1, s32[]{:T(128)} %constant.281.clone.1, s32[]{:T(128)} %constant.281.clone.1, s32[]{:T(128)} %constant.282.clone.1, s32[]{:T(128)} %constant.268.clone.1) | dynamic-update-slice | bytes 262148 | tf_op jit(solution)/shard_map/scatter | solution.py:87
  130.9 3.7 %fusion.26 = (bf16[8,8,8,8,128]{4,3,2,1,0:T(8,128)(2,1)}, bf16[8,8,8,8,128]{4,3,2,1,0:T(8,128)(2,1)}, bf16[8,8,8,8,128]{4,3,2,1,0:T(8,128)(2,1)}, bf16[8,8,8,8,1...) fusion(bf16[8,10,10,10,128]{4,3,2,1,0:T(8,128)(2,1)S(1)} %scatt, ...), kind=kLoop, calls=%fused_computation.136 | loop fusion | bytes 16777216 | tf_op jit(solution)/shard_map/slice | solution.py:35
  134.6 8.1 %fusion.25 = (bf16[8,8,8,8,128]{4,3,2,1,0:T(8,128)(2,1)}, bf16[8,8,8,8,128]{4,3,2,1,0:T(8,128)(2,1)}, bf16[8,8,8,8,128]{4,3,2,1,0:T(8,128)(2,1)}, bf16[8,8,8,8,1...) fusion(bf16[8,10,10,10,128]{4,3,2,1,0:T(8,128)(2,1)S(1)} %scatt, ...), kind=kLoop, calls=%fused_computation.135 | loop fusion | bytes 39845888 | tf_op jit(solution)/shard_map/slice | solution.py:35
  142.7 2.4 %pad_maximum_fusion = bf16[8,8,8,8,384]{4,3,2,1,0:T(8,128)(2,1)S(1)} fusion(bf16[8,8,8,8,128]{4,3,2,1,0:T(8,128)(2,1)} %get-tuple-element.120, bf16[8,8,8,8,128]{4,3,2,1,0:T(8,128)(2,1)} %get-tuple-element.121, bf16[8,8,8,8,128]{4,3,2,1,0:T(8,128)(2,1)} %get-tuple-element.122), kind=kLoop, calls=%fused_computation.20 | loop fusion | flops 9437184 | bytes 6291456 | tf_op jit(solution)/shard_map/concatenate | solution.py:33
  145.1 1.0 fusion.35
  147.9 1.0 convolution_add_fusion.7
  150.2 0.7 copy-done.19
  152.5 1.0 convolution_add_fusion.6
  154.9 0.7 copy-done.13
  156.7 0.7 copy-done.10
  158.6 0.7 copy-done.7
  160.4 0.7 copy-done.4
  162.7 1.0 convolution_add_fusion.5
  163.7 1.0 convolution_add_fusion.4
  164.8 1.0 convolution_add_fusion.3
  165.8 1.1 convolution_add_fusion.2
  166.9 1.0 convolution_add_fusion.1
  168.1 2.0 %fusion.1 = bf16[4096,128]{1,0:T(8,128)(2,1)} fusion(f32[4096,128]{1,0:T(8,128)S(1)} %convolution_add_fusion.1, bf16[4096,384]{1,0:T(8,128)(2,1)S(1)} %bitcast.168, bf16[384,128]{1,0:T(8,128)(2,1)S(1)} %bitcast.197, bf16[4096,128]{1,0:T(8,128)(2,1)S(1)} %bitcast.173), kind=kOutput, calls=%fused_computation.17 | convolution fusion | flops 404750336 | bytes 7438336 | tf_op jit(solution)/shard_map/dot_general | solution.py:49
  (140 shorter events, 22.4 us)
Async XLA Ops:
  0.0 70.4 %copy-start = (bf16[128,128]{1,0:T(8,128)(2,1)S(1)}, bf16[128,128]{1,0:T(8,128)(2,1)}, u32[]{:S(2)}) copy-start(bf16[128,128]{1,0:T(8,128)(2,1)} %param.27) | copy-start | bytes 98308
  2.5 12.4 %all-to-all-start = ((s32[4,1,2]{2,1,0:T(1,128)}), s32[4,1,2]{2,1,0:T(1,128)S(1)}, u32[]{:S(2)}, u32[]{:S(2)}) async-start(s32[4,1,2]{2,1,0:T(1,128)} %copy.51), calls=%async_computation | async-start | bytes 4096 | tf_op jit(solution)/shard_map/all_to_all | solution.py:137
  7.7 9.7 %collective-permute-start.1 = (bf16[1,32,16,128]{3,2,1,0:T(8,128)(2,1)S(1)}, bf16[1,32,16,128]{3,2,1,0:T(8,128)(2,1)S(1)}, u32[]{:S(2)}, u32[]{:S(2)}) collective-permute-start(bf16[1,32,16,128]{3,2,1,0:T(8,128)(2,1)S(1)} %get-tuple-element.176), channel_id=1, source_target_pairs={{4,0},{8,4},{12,8},{5,1},{9,5},{13,9},{6,2},{10,6},{14,10},{7,3},{... | collective-permute-start | bytes 393224 | tf_op jit(solution)/shard_map/ppermute | solution.py:19
  9.0 7.2 %collective-permute-start = (bf16[1,32,16,128]{3,2,1,0:T(8,128)(2,1)S(1)}, bf16[1,32,16,128]{3,2,1,0:T(8,128)(2,1)S(1)}, u32[]{:S(2)}, u32[]{:S(2)}) collective-permute-start(bf16[1,32,16,128]{3,2,1,0:T(8,128)(2,1)S(1)} %get-tuple-element.177), channel_id=1, source_target_pairs={{0,4},{4,8},{8,12},{1,5},{5,9},{9,13},{2,6},{6,10},{10,14},{3,7},{... | collective-permute-start | bytes 393224 | tf_op jit(solution)/shard_map/ppermute | solution.py:18
  17.5 5.4 %collective-permute-start.2 = (bf16[6,1,16,128]{3,2,1,0:T(8,128)(2,1)S(1)}, bf16[6,1,16,128]{3,2,1,0:T(8,128)(2,1)S(1)}, u32[]{:S(2)}, u32[]{:S(2)}) collective-permute-start(bf16[6,1,16,128]{3,2,1,0:T(8,128)(2,1)S(1)} %get-tuple-element.174), channel_id=1, source_target_pairs={{0,1},{1,2},{2,3},{4,5},{5,6},{6,7},{8,9},{9,10},{10,11},{12,13},{... | collective-permute-start | bytes 73736 | tf_op jit(solution)/shard_map/ppermute | solution.py:18
  21.4 5.7 %collective-permute-start.3 = (bf16[6,1,16,128]{3,2,1,0:T(8,128)(2,1)S(1)}, bf16[6,1,16,128]{3,2,1,0:T(8,128)(2,1)S(1)}, u32[]{:S(2)}, u32[]{:S(2)}) collective-permute-start(bf16[6,1,16,128]{3,2,1,0:T(8,128)(2,1)S(1)} %get-tuple-element.175), channel_id=1, source_target_pairs={{1,0},{2,1},{3,2},{5,4},{6,5},{7,6},{9,8},{10,9},{11,10},{13,12},{... | collective-permute-start | bytes 73736 | tf_op jit(solution)/shard_map/ppermute | solution.py:19
  37.0 33.4 %copy-start.39 = (f32[128]{0:T(128)S(1)}, f32[128]{0:T(128)}, u32[]{:S(2)}) copy-start(f32[128]{0:T(128)} %param.26) | copy-start | bytes 1540
  37.0 33.4 %copy-start.40 = (f32[128]{0:T(128)S(1)}, f32[128]{0:T(128)}, u32[]{:S(2)}) copy-start(f32[128]{0:T(128)} %param.25) | copy-start | bytes 1540
  70.9 7.1 %copy-start.29 = (bf16[27,128,128]{2,1,0:T(8,128)(2,1)S(1)}, bf16[27,128,128]{2,1,0:T(8,128)(2,1)}, u32[]{:S(2)}) copy-start(bf16[27,128,128]{2,1,0:T(8,128)(2,1)} %param.31) | copy-start | bytes 2654212
  73.6 18.8 %copy-start.28 = (bf16[8,512,128]{2,1,0:T(8,128)(2,1)S(1)}, bf16[8,512,128]{2,1,0:T(8,128)(2,1)}, u32[]{:S(2)}) copy-start(bf16[8,512,128]{2,1,0:T(8,128)(2,1)} %param.28) | copy-start | bytes 3145732
  73.6 18.1 %all-to-all-start.1 = ((bf16[4,2,512,128]{3,2,1,0:T(8,128)(2,1)}), bf16[4,2,512,128]{3,2,1,0:T(8,128)(2,1)S(1)}, u32[]{:S(2)}, u32[]{:S(2)}) async-start(bf16[4,2,512,128]{3,2,1,0:T(8,128)(2,1)} %bitcast.30), calls=%async_computation.1 | async-start | bytes 2097152 | tf_op jit(solution)/shard_map/all_to_all | solution.py:141
  92.8 1.6 copy-start.2
  96.5 11.4 %copy-start.38 = (pred[8]{0:T(512)(128)(4,1)S(1)}, pred[8]{0:T(512)(128)(4,1)}, u32[]{:S(2)}) copy-start(pred[8]{0:T(512)(128)(4,1)} %get-tuple-element.181) | copy-start | bytes 28
  142.7 2.4 %copy-start.37 = (bf16[3,128,128]{2,1,0:T(8,128)(2,1)S(1)}, bf16[3,128,128]{2,1,0:T(8,128)(2,1)}, u32[]{:S(2)}) copy-start(bf16[3,128,128]{2,1,0:T(8,128)(2,1)} %get-tuple-element.163) | copy-start | bytes 294916
  145.1 1.2 copy-start.25
  145.1 1.5 copy-start.26
  145.1 1.8 %copy-start.27 = (bf16[8,8,8,8,128]{4,3,2,1,0:T(8,128)(2,1)S(1)}, bf16[8,8,8,8,128]{4,3,2,1,0:T(8,128)(2,1)}, u32[]{:S(2)}) copy-start(bf16[8,8,8,8,128]{4,3,2,1,0:T(8,128)(2,1)} %get-tuple-element.119) | copy-start | bytes 3145732
  147.0 0.9 copy-start.36
  147.9 1.2 copy-start.22
  147.9 1.5 copy-start.23
  147.9 1.9 %copy-start.24 = (bf16[8,8,8,8,128]{4,3,2,1,0:T(8,128)(2,1)S(1)}, bf16[8,8,8,8,128]{4,3,2,1,0:T(8,128)(2,1)}, u32[]{:S(2)}) copy-start(bf16[8,8,8,8,128]{4,3,2,1,0:T(8,128)(2,1)} %get-tuple-element.98) | copy-start | bytes 3145732
  149.7 1.2 copy-start.19
  149.7 1.5 copy-start.20
  149.7 1.9 %copy-start.21 = (bf16[8,8,8,8,128]{4,3,2,1,0:T(8,128)(2,1)S(1)}, bf16[8,8,8,8,128]{4,3,2,1,0:T(8,128)(2,1)}, u32[]{:S(2)}) copy-start(bf16[8,8,8,8,128]{4,3,2,1,0:T(8,128)(2,1)} %get-tuple-element.114) | copy-start | bytes 3145732
  151.6 0.9 copy-start.35
  152.5 1.2 copy-start.16
  152.5 1.5 copy-start.17
  152.5 1.9 %copy-start.18 = (bf16[8,8,8,8,128]{4,3,2,1,0:T(8,128)(2,1)S(1)}, bf16[8,8,8,8,128]{4,3,2,1,0:T(8,128)(2,1)}, u32[]{:S(2)}) copy-start(bf16[8,8,8,8,128]{4,3,2,1,0:T(8,128)(2,1)} %get-tuple-element.101) | copy-start | bytes 3145732
  154.3 1.2 copy-start.13
  154.3 1.5 copy-start.14
  154.3 1.9 %copy-start.15 = (bf16[8,8,8,8,128]{4,3,2,1,0:T(8,128)(2,1)S(1)}, bf16[8,8,8,8,128]{4,3,2,1,0:T(8,128)(2,1)}, u32[]{:S(2)}) copy-start(bf16[8,8,8,8,128]{4,3,2,1,0:T(8,128)(2,1)} %get-tuple-element.104) | copy-start | bytes 3145732
  156.2 1.2 copy-start.10
  156.2 1.5 copy-start.11
  156.2 1.9 %copy-start.12 = (bf16[8,8,8,8,128]{4,3,2,1,0:T(8,128)(2,1)S(1)}, bf16[8,8,8,8,128]{4,3,2,1,0:T(8,128)(2,1)}, u32[]{:S(2)}) copy-start(bf16[8,8,8,8,128]{4,3,2,1,0:T(8,128)(2,1)} %get-tuple-element.107) | copy-start | bytes 3145732
  158.0 1.2 copy-start.7
  158.0 1.5 copy-start.8
  158.1 1.9 %copy-start.9 = (bf16[8,8,8,8,128]{4,3,2,1,0:T(8,128)(2,1)S(1)}, bf16[8,8,8,8,128]{4,3,2,1,0:T(8,128)(2,1)}, u32[]{:S(2)}) copy-start(bf16[8,8,8,8,128]{4,3,2,1,0:T(8,128)(2,1)} %get-tuple-element.110) | copy-start | bytes 3145732
  159.9 1.2 copy-start.4
  159.9 1.5 copy-start.5
  159.9 1.9 %copy-start.6 = (bf16[8,8,8,8,128]{4,3,2,1,0:T(8,128)(2,1)S(1)}, bf16[8,8,8,8,128]{4,3,2,1,0:T(8,128)(2,1)}, u32[]{:S(2)}) copy-start(bf16[8,8,8,8,128]{4,3,2,1,0:T(8,128)(2,1)} %get-tuple-element.113) | copy-start | bytes 3145732
  161.8 0.9 copy-start.34
  162.7 1.0 copy-start.33
  163.7 1.1 copy-start.32
  164.7 1.0 copy-start.31
  165.8 1.1 copy-start.30
  166.9 1.2 copy-start.3
  168.1 2.0 %copy-start.1 = (bf16[128,128]{1,0:T(8,128)(2,1)S(1)}, bf16[128,128]{1,0:T(8,128)(2,1)}, u32[]{:S(2)}) copy-start(bf16[128,128]{1,0:T(8,128)(2,1)} %param.27) | copy-start | bytes 98308
where the time goes:
time: 172 us; the launch traced here: 170 us
  local copies, waits for them, and re-layouts  68.6 us (40%)
  blocking collectives  31.3 us (18%)
  other arithmetic  18.8 us (11%)
  starting transfers between devices  17.6 us (10%)
  waiting for transfers between devices  17.1 us (10%)
  matrix products  15.9 us (9%)
    psum x1, blocking collectives, body(): lax.psum((jnp.sum(filtered, axis=(0, 2)), jnp.sum(filtered * filtered, ax...  31.3 us
    dot_general x18, matrix products, convolve(): jnp.dot(window, stacked, preferred_element_type=jnp.float32)  15.5 us
    slice x4, local copies, waits for them, and re-layouts, convolve(): padded[:, along_x:along_x + span_x, along_y:along_y + span_y, along_z:alo...  14.9 us
    all_to_all x1, waiting for transfers between devices, body(): lax.all_to_all(upsampled, 'slab', split_axis=0, concat_axis=0, tiled=True)  12.7 us
    unnamed x87, local copies, waits for them, and re-layouts  12.6 us
    gather x6, local copies, waits for them, and re-layouts, framed(): picked = jnp.take(planes[direction], jnp.maximum(target, 0), axis=0)  8.97 us
    concatenate x14, other arithmetic, convolve(): jnp.concatenate([padded[:, along_x:along_x + span_x, along_y:along_y + sp...  8.37 us
    ppermute x2, starting transfers between devices, padded_2(): before = lax.ppermute(last, axis, up)  6.96 us
  transfers between devices with their start and end apart: 6, of which 3 were waited for; matrix products, arithmetic and copies ran while one was open for 5% of the time, Pallas kernels for 0%

commit v1 on v0

v1 whole, which is shorter than its diff:
```python
import functools

import jax
import jax.numpy as jnp
from jax import lax
from jax.experimental import pallas as pl
from jax.experimental.pallas import tpu as pltpu
from jax.sharding import PartitionSpec as P

G = 32
FB = 8
MOST = 2
EPS = 1e-05
F32 = jnp.float32
BF16 = jnp.bfloat16


def pairs(count, odd):
    links = []
    for i in range(odd, count - 1, 2):
        links += [(i, i + 1), (i + 1, i)]
    return links


def xor_links(count, distance):
    return [(i, i ^ distance) for i in range(count)]


def tap_sums(taken, weight_ref):
    window = jnp.concatenate(taken, axis=1)
    return jnp.dot(window, weight_ref, preferred_element_type=F32)


def shifted_sum(sums, depth, channels):
    rows = sums.shape[0]
    place = lax.broadcasted_iota(jnp.int32, (rows, channels), 0) % depth
    below = pltpu.roll(sums[:, :channels], 1, 0)
    above = pltpu.roll(sums[:, 2 * channels :], rows - 1, 0)
    return (
        sums[:, channels : 2 * channels]
        + jnp.where(place == 0, 0.0, below)
        + jnp.where(place == depth - 1, 0.0, above)
    )


def start_all(copies):
    for copy in copies:
        copy.start()


def wait_all(copies):
    for copy in copies:
        copy.wait()


def weight_copies(source, target, sems, first):
    channels = target.shape[1] // 3
    copies = []
    for tap in range(27):
        ab, c = tap // 3, tap % 3
        copies.append(
            pltpu.make_async_copy(
                source.at[tap],
                target.at[pl.ds(ab * channels, channels), pl.ds(c * channels, channels)],
                sems.at[first + tap],
            )
        )
    return copies


def coarse_kernel(sources, xor, *refs):
    coords = refs[:sources] if xor else refs[:1]
    refs = refs[sources:] if xor else refs[1:]
    (inp, x_first, x_second, y_first, y_second, weight) = refs[:6]
    outs = refs[6 : 6 + sources] if xor else refs[6:7]
    stats = refs[6 + len(outs)]
    padded, conv, wide, sems = refs[7 + len(outs) :]
    dx, dy, dz, channels = inp.shape
    slab = lax.axis_index("slab")
    sub = lax.axis_index("sub")
    rows = pl.ds(1, dy)
    x_even = lax.rem(slab, 2) == 0
    y_even = lax.rem(sub, 2) == 0
    xa = jnp.where(x_even, dx + 1, 0)
    xb = dx + 1 - xa
    ya = jnp.where(y_even, dy + 1, 0)
    yb = dy + 1 - ya
    moves = [
        (inp, padded.at[pl.ds(1, dx), rows]),
        (x_first, padded.at[xa, rows]),
        (x_second, padded.at[xb, rows]),
    ]
    for got, place in ((y_first, ya), (y_second, yb)):
        moves += [
            (got.at[0], padded.at[xa, place]),
            (got.at[pl.ds(1, dx)], padded.at[pl.ds(1, dx), place]),
            (got.at[dx + 1], padded.at[xb, place]),
        ]
    copies = [pltpu.make_async_copy(a, b, sems.at[i]) for i, (a, b) in enumerate(moves)]
    loads = weight_copies(weight, wide, sems, len(moves))
    start_all(loads)
    start_all(copies)
    wait_all(copies)
    wait_all(loads)
    total = jnp.zeros((8, channels), F32)
    for x in range(dx):
        taken = [
            padded[x + a, pl.ds(b, dy)].reshape(dy * dz, channels)
            for a in range(3)
            for b in range(3)
        ]
        value = shifted_sum(tap_sums(taken, wide[...]), dz, channels)
        conv[x] = value.reshape(dy, dz, channels)
        total = total + jnp.sum(value.reshape(-1, 8, channels), axis=0)
    mean = jnp.sum(total, axis=0, keepdims=True) / (dx * dy * dz)
    square = jnp.zeros((8, channels), F32)
    for x in range(dx):
        off = conv[x].reshape(-1, 8, channels) - mean[None]
        square = square + jnp.sum(off * off, axis=0)
    stats[0:1, :] = mean
    stats[1:2, :] = jnp.sum(square, axis=0, keepdims=True)
    edge = FB // 2
    for s in range(sources):
        wanted = coords[s] if xor else coords[0].at[s]
        seen = jnp.int32(0)
        where_y = [jnp.int32(0)] * MOST
        where_z = [jnp.int32(0)] * MOST
        for n in range(wanted.shape[0]):
            hit = wanted[n, 0] == slab
            y = wanted[n, 1] - sub * (dy // edge)
            for slot in range(MOST):
                here = jnp.logical_and(hit, seen == slot)
                where_y[slot] = jnp.where(here, y, where_y[slot])
                where_z[slot] = jnp.where(here, wanted[n, 2], where_z[slot])
            seen = seen + hit.astype(jnp.int32)
        out = outs[s] if xor else outs[0].at[s]
        for slot in range(MOST):
            for x in range(edge):
                for y in range(edge):
                    piece = conv[x, edge * where_y[slot] + y, pl.ds(edge * where_z[slot], edge), :]
                    out[slot, pl.ds((x * edge + y) * edge, edge), :] = piece


def group_sum(value, size):
    lanes = value.shape[-1]
    place = lax.broadcasted_iota(jnp.int32, value.shape, 1) % size
    total = value
    for step in range(1, size):
        total = total + jnp.where(place >= step, pltpu.roll(value, step, 1), 0.0)
        total = total + jnp.where(place + step < size, pltpu.roll(value, lanes - step, 1), 0.0)
    return total


def merge(means, squares, count):
    mean = sum(means) / len(means)
    square = sum(squares)
    for part in means:
        square = square + count * (part - mean) * (part - mean)
    return mean, square


def fine_kernel(cube_lists, stat_lists, cells, xor, *refs):
    coords, links = refs[:2]
    cubes = refs[2 : 2 + cube_lists]
    stats = refs[2 + cube_lists : 2 + cube_lists + stat_lists]
    gain, bias, lift, fine, weight, out = refs[2 + cube_lists + stat_lists : 8 + cube_lists + stat_lists]
    held, block, even, odd, wide, sems = refs[8 + cube_lists + stat_lists :]
    total, _, channels = fine.shape
    slab = lax.axis_index("slab")
    edge = FB // 2
    loads = weight_copies(weight, wide, sems, cube_lists)
    start_all(loads)
    moves = []
    for i, cube in enumerate(cubes):
        target = held.at[pl.ds(MOST * i, MOST)] if xor else held
        moves.append(pltpu.make_async_copy(cube, target, sems.at[i]))
    start_all(moves)
    size = channels // G
    mean, square = merge(
        [s[0:1, :] for s in stats], [s[1:2, :] for s in stats], float(cells)
    )
    cells = cells * stat_lists
    group_mean = group_sum(mean, size) / size
    off = mean - group_mean
    group_var = group_sum(square + cells * off * off, size) / (cells * size)
    scale = lax.rsqrt(group_var + EPS)
    duplicate = (
        lax.broadcasted_iota(jnp.int32, (2 * edge**3, edge**3), 1)
        == lax.broadcasted_iota(jnp.int32, (2 * edge**3, edge**3), 0) // FB * edge
        + lax.broadcasted_iota(jnp.int32, (2 * edge**3, edge**3), 0) % FB // 2
    ).astype(BF16)
    wait_all(moves)
    for n in range(total):
        holder = coords[n, 0]
        rank = jnp.int32(0)
        for m in range(n):
            rank = rank + (coords[m, 0] == holder).astype(jnp.int32)
        source = jnp.bitwise_xor(holder, slab) if xor else holder
        value = held[source * MOST + rank]
        normed = (value - group_mean) * scale * gain[...] + bias[...]
        acted = (normed / (1.0 + jnp.exp(-normed))).astype(BF16)
        lifted = jnp.dot(acted, lift[...], preferred_element_type=F32).astype(BF16)
        wider = jnp.dot(duplicate, lifted, preferred_element_type=F32)
        wider = wider.reshape(edge, edge, FB, channels)
        own = fine[n].astype(F32).reshape(FB, FB, FB, channels)
        for i in range(FB):
            for j in range(FB):
                summed = (own[i, j] + wider[i // 2, j // 2]).astype(BF16).astype(F32)
                block[n, i, j] = summed
    zero = jnp.zeros((FB, channels), F32)
    wait_all(loads)
    for n in range(total):
        picked = []
        for direction in range(4):
            target = links[n, direction]
            valid = (target >= 0).astype(F32)
            picked.append((lax.rem(jnp.maximum(target, 0), total), valid))
        for i in range(FB + 2):
            if 0 < i < FB + 1:
                line = [block[n, i - 1, j] for j in range(FB)]
                (low, low_on), (high, high_on) = picked[2], picked[3]
                line = [block[low, i - 1, FB - 1] * low_on] + line + [block[high, i - 1, 0] * high_on]
            else:
                (other, on) = picked[0] if i == 0 else picked[1]
                plane = FB - 1 if i == 0 else 0
                line = [zero] + [block[other, plane, j] * on for j in range(FB)] + [zero]
            for j in range(0, FB, 2):
                even[i, j // 2] = jnp.concatenate(line[j + 1 : j + 3], axis=0).astype(BF16)
            for j in range(0, FB + 2, 2):
                odd[i, j // 2] = jnp.concatenate(line[j : j + 2], axis=0).astype(BF16)
        taken = []
        for a in range(3):
            for b in range(3):
                if b == 1:
                    part = even[pl.ds(a, FB)]
                else:
                    part = odd[pl.ds(a, FB), pl.ds(b // 2, FB // 2)]
                taken.append(part.reshape(FB**3, channels))
        value = shifted_sum(tap_sums(taken, wide[...]), FB, channels)
        value = value + block[n].reshape(FB**3, channels)
        out[n] = value.astype(BF16)


def body(
    coarse_in,
    coarse_weight,
    norm_gain,
    norm_bias,
    lift_weight,
    fine_input,
    block_coords,
    neighbours,
    fine_weight,
):
    dx, dy, dz, channels = coarse_in.shape
    slabs, subs = lax.axis_size("slab"), lax.axis_size("sub")
    slab, sub = lax.axis_index("slab"), lax.axis_index("sub")
    total = block_coords.shape[0]
    xor = slabs == 4
    edge = FB // 2
    if xor:
        near = lax.ppermute(block_coords, "slab", xor_links(slabs, 1))
        both = jnp.stack([block_coords, near])
        far = lax.ppermute(both, "slab", xor_links(slabs, 2))
        asked = [block_coords, near, far[0], far[1]]
    else:
        asked = [lax.all_gather(block_coords, "slab", axis=0)]
    x_even, y_even = slab % 2 == 0, sub % 2 == 0
    last, first = coarse_in[dx - 1], coarse_in[0]
    x_first = lax.ppermute(jnp.where(x_even, last, first), "slab", pairs(slabs, 0))
    x_second = lax.ppermute(jnp.where(x_even, first, last), "slab", pairs(slabs, 1))
    low = jnp.concatenate([x_first[None, 0], coarse_in[:, 0], x_second[None, 0]])
    high = jnp.concatenate([x_first[None, dy - 1], coarse_in[:, dy - 1], x_second[None, dy - 1]])
    y_first = lax.ppermute(jnp.where(y_even, high, low), "sub", pairs(subs, 0))
    y_second = lax.ppermute(jnp.where(y_even, low, high), "sub", pairs(subs, 1))

    smem = pl.BlockSpec(memory_space=pltpu.SMEM)
    vmem = pl.BlockSpec(memory_space=pltpu.VMEM)
    hbm = pl.BlockSpec(memory_space=pl.ANY)
    piece = (MOST, edge**3, channels)
    if xor:
        shapes = [jax.ShapeDtypeStruct(piece, F32)] * slabs
    else:
        shapes = [jax.ShapeDtypeStruct((slabs,) + piece, F32)]
    results = pl.pallas_call(
        functools.partial(coarse_kernel, slabs, xor),
        out_shape=shapes + [jax.ShapeDtypeStruct((8, channels), F32)],
        in_specs=[smem] * len(asked) + [hbm] * 6,
        out_specs=[vmem] * (len(shapes) + 1),
        scratch_shapes=[
            pltpu.VMEM((dx + 2, dy + 2, dz, channels), BF16),
            pltpu.VMEM((dx, dy, dz, channels), F32),
            pltpu.VMEM((9 * channels, 3 * channels), BF16),
            pltpu.SemaphoreType.DMA((9 + 27,)),
        ],
        name="coarse",
    )(*asked, coarse_in, x_first, x_second, y_first, y_second, coarse_weight)
    sent, stats = results[:-1], results[-1]
    cells = dx * dy * dz
    if xor:
        replies = [sent[0]]
        parts = [stats]
        for distance in range(1, slabs):
            parts.append(lax.ppermute(stats, "slab", xor_links(slabs, distance)))
            replies.append(lax.ppermute(sent[distance], "slab", xor_links(slabs, distance)))
    else:
        replies = [
            lax.all_to_all(sent[0], "slab", split_axis=0, concat_axis=0, tiled=True).reshape(
                slabs * MOST, edge**3, channels
            )
        ]
        parts = list(lax.all_gather(stats, "slab", axis=0))
    mean, square = merge([p[0:1] for p in parts], [p[1:2] for p in parts], float(cells))
    cells = cells * slabs
    merged = jnp.concatenate([mean, square])
    if subs == 4:
        lines = [merged] + [
            lax.ppermute(merged, "sub", xor_links(subs, distance)) for distance in range(1, subs)
        ]
    else:
        lines = list(lax.all_gather(merged, "sub", axis=0))

    return pl.pallas_call(
        functools.partial(fine_kernel, len(replies), len(lines), cells, xor),
        out_shape=jax.ShapeDtypeStruct(fine_input.shape, BF16),
        in_specs=[smem] * 2 + [hbm] * len(replies) + [vmem] * (len(lines) + 4) + [hbm],
        out_specs=vmem,
        scratch_shapes=[
            pltpu.VMEM((slabs * MOST, edge**3, channels), F32),
            pltpu.VMEM((total, FB, FB, FB, channels), F32),
            pltpu.VMEM((FB + 2, FB // 2, 2 * FB, channels), BF16),
            pltpu.VMEM((FB + 2, FB // 2 + 1, 2 * FB, channels), BF16),
            pltpu.VMEM((9 * channels, 3 * channels), BF16),
            pltpu.SemaphoreType.DMA((len(replies) + 27,)),
        ],
        name="fine",
    )(
        block_coords,
        neighbours,
        *replies,
        *lines,
        norm_gain.reshape(1, channels),
        norm_bias.reshape(1, channels),
        lift_weight,
        fine_input,
        fine_weight,
    )


def solution(mesh):
    in_specs = (
        P(("scene", "slab"), "sub", None, None),
        P(),
        P(),
        P(),
        P(),
        P(("scene", "slab", "sub"), None, None),
        P(("scene", "slab", "sub"), None),
        P(("scene", "slab", "sub"), None),
        P(),
    )
    out_specs = P(("scene", "slab", "sub"), None, None)
    return jax.shard_map(body, mesh=mesh, in_specs=in_specs, out_specs=out_specs, check_vma=False)
```

time: 172 us -> 49.4 us (0.29)
  local copies, waits for them, and re-layouts: 68.6 us -> 4.97 us
  blocking collectives: 31.3 us -> 0 us
  other arithmetic: 18.8 us -> 1.79 us
  Pallas kernels: 0 us -> 17 us
  matrix products: 15.9 us -> 0 us
  waiting for transfers between devices: 17.1 us -> 6.17 us
    psum x1 -> x0, blocking collectives: 31.3 us -> none  [body(): lax.psum((jnp.sum(filtered, axis=(0, 2)), jnp.sum(filtered * filtered, ax...]
    slice x9 -> x2, local copies, waits for them, and re-layouts: 18.5 us -> 0.01 us  [the longest x1 0.01 us: body(): x_second[None, dy - 1]]
    scatter x6 -> x0, local copies, waits for them, and re-layouts: 17.2 us -> none  [the longest x1 6.24 us: framed(): padded = padded.at[:, 1:-1, 1:-1, 0].set(faces[4])]
    pallas_call x0 -> x2, Pallas kernels: none -> 17 us  [the longest x1 10.7 us: body(): pl.pallas_call(functools.partial(fine_kernel, len(replies), len(lines), c...]
    dot_general x19 -> x0, matrix products: 15.9 us -> none  [the longest x18 15.5 us: convolve(): jnp.dot(window, stacked, preferred_element_type=jnp.float32)]
    all_to_all x2 -> x0, waiting for transfers between devices: 12.7 us -> none  [the longest x1 12.7 us: body(): lax.all_to_all(upsampled, 'slab', split_axis=0, concat_axis=0, tiled=True)]
    gather x8 -> x0, local copies, waits for them, and re-layouts: 10.3 us -> none  [the longest x6 8.97 us: framed(): picked = jnp.take(planes[direction], jnp.maximum(target, 0), axis=0)]
    unnamed x87 -> x29, local copies, waits for them, and re-layouts: 12.6 us -> 2.8 us
  transfers between devices with their start and end apart: 6 -> 15, of which waited for: 3 -> 4; matrix products, arithmetic and copies ran while one was open for 5% -> 8% of each run, Pallas kernels for 0% -> 0%
where the time goes in v1:
time: 49.4 us; the launch traced here: 49 us
  starting transfers between devices  18.8 us (38%)
  Pallas kernels  17 us (34%)
  waiting for transfers between devices  6.17 us (12%)
  local copies, waits for them, and re-layouts  4.97 us (10%)
  other arithmetic  1.79 us (4%)
    pallas_call x1, Pallas kernels, body(): pl.pallas_call(functools.partial(fine_kernel, len(replies), len(lines), c...  10.7 us
    pallas_call x1, Pallas kernels, body(): pl.pallas_call(functools.partial(coarse_kernel, slabs, xor), out_shape=sh...  6.35 us
    ppermute x3, waiting for transfers between devices, body(): lax.ppermute(merged, 'sub', xor_links(subs, distance))  5.5 us
    ppermute x1, starting transfers between devices, body(): y_first = lax.ppermute(jnp.where(y_even, high, low), 'sub', pairs(subs, 0))  4.46 us
    ppermute x1, starting transfers between devices, body(): lax.ppermute(jnp.where(x_even, last, first), 'slab', pairs(slabs, 0))  4.42 us
    ppermute x3, starting transfers between devices, body(): lax.ppermute(merged, 'sub', xor_links(subs, distance))  3.5 us
    unnamed x29, local copies, waits for them, and re-layouts  2.8 us
    ppermute x3, starting transfers between devices, body(): parts.append(lax.ppermute(stats, 'slab', xor_links(slabs, distance)))  2.77 us
  transfers between devices with their start and end apart: 15, of which 4 were waited for; matrix products, arithmetic and copies ran while one was open for 8% of the time, Pallas kernels for 0%

profile of v1, /device:TPU:0, one launch (start us, length us, event | category | flops | bytes accessed | tf_op | source)
XLA Modules:
  0.0 49.0 jit_solution(1692575501704395963)
XLA Ops:
  0.0 0.8 %copy.17.refs_0_ = s32[8,3]{1,0:T(8,128)S(1)} copy(s32[8,3]{0,1:T(4,128)} %param.15) | data formatting | bytes 192 | tf_op args[6]
  0.8 0.0 copy-start.5
  0.8 0.5 %collective-permute-start = (s32[8,3]{1,0:T(8,128)S(1)}, s32[8,3]{1,0:T(8,128)S(1)}, u32[]{:S(2)}, u32[]{:S(2)}) collective-permute-start(s32[8,3]{1,0:T(8,128)S(1)} %copy.17.refs_0_), channel_id=1, source_target_pairs={{0,4},{4,0},{8,12},{12,8},{1,5},{5,1},{9,13},{13,9},{2,6},{6,2},{1... | collective-permute-start | bytes 296 | tf_op jit(solution)/shard_map/ppermute | solution.py:262
  1.3 0.1 copy-done.5
  1.3 1.0 %select_bitcast_fusion = (bf16[32,16,128]{2,1,0:T(8,128)(2,1)S(1)}, bf16[32,16,128]{2,1,0:T(8,128)(2,1)S(1)}) fusion(pred[]{:T(512)S(6)} %eq.9, bf16[4,32,16,128]{3,2,1,0:T(8,128)(2,1)} %refs_4_.1), kind=kLoop, calls=%fused_computation | loop fusion | flops 131072 | bytes 524289 | tf_op jit(solution)/shard_map/jit(_where)/select_n | solution.py:271
  2.3 0.7 %collective-permute-start.3 = (bf16[32,16,128]{2,1,0:T(8,128)(2,1)S(1)}, bf16[32,16,128]{2,1,0:T(8,128)(2,1)S(1)}, u32[]{:S(2)}, u32[]{:S(2)}) collective-permute-start(bf16[32,16,128]{2,1,0:T(8,128)(2,1)S(1)} %get-tuple-element.19), channel_id=1, source_target_pairs={{4,8},{8,4},{5,9},{9,5},{6,10},{10,6},{7,11},{11,7},{20,24},{24,20... | collective-permute-start | bytes 393224 | tf_op jit(solution)/shard_map/ppermute | solution.py:271
  3.0 4.4 %collective-permute-start.2 = (bf16[32,16,128]{2,1,0:T(8,128)(2,1)S(1)}, bf16[32,16,128]{2,1,0:T(8,128)(2,1)S(1)}, u32[]{:S(2)}, u32[]{:S(2)}) collective-permute-start(bf16[32,16,128]{2,1,0:T(8,128)(2,1)S(1)} %get-tuple-element.20), channel_id=1, source_target_pairs={{0,4},{4,0},{8,12},{12,8},{1,5},{5,1},{9,13},{13,9},{2,6},{6,2},{1... | collective-permute-start | bytes 393224 | tf_op jit(solution)/shard_map/ppermute | solution.py:270
  7.4 0.7 %slice_bitcast_fusion.1 = (bf16[4,16,128]{2,1,0:T(8,128)(2,1)S(1)}, bf16[4,16,128]{2,1,0:T(8,128)(2,1)S(1)}) fusion(bf16[4,32,16,128]{3,2,1,0:T(8,128)(2,1)} %refs_4_.1), kind=kLoop, calls=%fused_computation.7 | loop fusion | bytes 65536 | tf_op jit(solution)/shard_map/squeeze | solution.py:273
  8.2 0.0 collective-permute-done.refs_1_
  8.2 0.0 copy-start.8
  8.2 0.1 copy.11
  8.3 0.0 copy-start.9
  8.3 0.5 %copy-done.8 = s32[8,3]{1,0:T(8,128)} copy-done((s32[8,3]{1,0:T(8,128)}, s32[8,3]{1,0:T(8,128)S(1)}, u32[]{:S(2)}) %copy-start.8) | copy-done | bytes 120
  8.8 0.2 copy-done.9
  8.9 0.0 collective-permute-start.1
  8.9 0.0 collective-permute-done.3.refs_6_
  9.0 0.0 copy-start
  9.0 0.0 collective-permute-done.2.refs_5_
  9.0 0.0 copy-start.1
  9.0 0.7 %collective-permute-start.5 = (bf16[6,16,128]{2,1,0:T(8,128)(2,1)S(1)}, bf16[6,16,128]{2,1,0:T(8,128)(2,1)S(1)}, u32[]{:S(2)}, u32[]{:S(2)}) collective-permute-start(bf16[6,16,128]{2,1,0:T(8,128)(2,1)S(1)} %get-tuple-element.25), channel_id=1, source_target_pairs={{1,2},{2,1},{5,6},{6,5},{9,10},{10,9},{13,14},{14,13},{17,18},{18,... | collective-permute-start | bytes 73736 | tf_op jit(solution)/shard_map/ppermute | solution.py:275
  9.7 4.5 %collective-permute-start.4 = (bf16[6,16,128]{2,1,0:T(8,128)(2,1)S(1)}, bf16[6,16,128]{2,1,0:T(8,128)(2,1)S(1)}, u32[]{:S(2)}, u32[]{:S(2)}) collective-permute-start(bf16[6,16,128]{2,1,0:T(8,128)(2,1)S(1)} %get-tuple-element.26), channel_id=1, source_target_pairs={{0,1},{1,0},{2,3},{3,2},{4,5},{5,4},{6,7},{7,6},{8,9},{9,8},{10,11... | collective-permute-start | bytes 73736 | tf_op jit(solution)/shard_map/ppermute | solution.py:274
  14.2 0.0 collective-permute-done.1
  14.2 0.7 %copy.16.refs_3_ = s32[8,3]{1,0:T(8,128)} copy(s32[8,3]{0,1:T(4,128)S(1)} %get-tuple-element.27) | data formatting | bytes 192 | tf_op jit(solution)/shard_map/squeeze | solution.py:265
  14.8 0.7 %copy.15.refs_2_ = s32[8,3]{1,0:T(8,128)} copy(s32[8,3]{0,1:T(4,128)S(1)} %get-tuple-element.28) | data formatting | bytes 192 | tf_op jit(solution)/shard_map/squeeze | solution.py:265
  15.5 0.0 collective-permute-done.5.refs_8_
  15.5 0.0 copy-start.6
  15.5 0.6 %collective-permute-done.4.refs_7_ = bf16[6,16,128]{2,1,0:T(8,128)(2,1)S(1)} collective-permute-done((bf16[6,16,128]{2,1,0:T(8,128)(2,1)S(1)}, bf16[6,16,128]{2,1,0:T(8,128)(2,1)S(1)}, u32[]{:S(2)}, u32[]{:S(2)}) %collective-permute-start.4) | collective-permute-done | bytes 24608 | tf_op jit(solution)/shard_map/ppermute | solution.py:274
  16.2 0.0 copy-done
  16.2 0.0 copy-done.1
  16.2 0.0 copy-done.6
  16.2 0.0 copy-start.7
  16.2 0.6 %copy-done.7 = bf16[6,16,128]{2,1,0:T(8,128)(2,1)} copy-done((bf16[6,16,128]{2,1,0:T(8,128)(2,1)}, bf16[6,16,128]{2,1,0:T(8,128)(2,1)S(1)}, u32[]{:S(2)}) %copy-start.7) | copy-done | bytes 24600
  16.8 6.4 %coarse.1 = (f32[2,64,128]{2,1,0:T(8,128)}, f32[2,64,128]{2,1,0:T(8,128)}, f32[2,64,128]{2,1,0:T(8,128)}, f32[2,64,128]{2,1,0:T(8,128)}, f32[8,128]{1,0:T(8,128)}) custom-call(s32[8,3]{1,0:T(8,128)} %copy-done.5, s32[8,3]{1,0:T(8,128)} %copy-done.8, s32[8,3]{1,0:T(8,128)} %copy.15.refs_2_, s32[8,3]{1,0:T(8,128)} %copy.16.refs_3_, ...), custom_call_target="tpu_custom_call" | custom-call | tf_op jit(solution)/shard_map/coarse/pallas_call | solution.py:285
  23.1 0.8 %collective-permute-start.11 = (f32[8,128]{1,0:T(8,128)}, f32[8,128]{1,0:T(8,128)S(1)}, u32[]{:S(2)}, u32[]{:S(2)}) collective-permute-start(f32[8,128]{1,0:T(8,128)} %get-tuple-element.14), channel_id=1, source_target_pairs={{0,12},{4,8},{8,4},{12,0},{1,13},{5,9},{9,5},{13,1},{2,14},{6,10},... | collective-permute-start | bytes 12296 | tf_op jit(solution)/shard_map/ppermute | solution.py:304
  23.9 1.9 %collective-permute-start.10 = (f32[8,128]{1,0:T(8,128)}, f32[8,128]{1,0:T(8,128)S(1)}, u32[]{:S(2)}, u32[]{:S(2)}) collective-permute-start(f32[8,128]{1,0:T(8,128)} %get-tuple-element.14), channel_id=1, source_target_pairs={{0,8},{4,12},{8,0},{12,4},{1,9},{5,13},{9,1},{13,5},{2,10},{6,14},... | collective-permute-start | bytes 12296 | tf_op jit(solution)/shard_map/ppermute | solution.py:304
  25.9 0.0 collective-permute-start.9
  25.9 0.5 collective-permute-start.6
  26.4 1.3 %collective-permute-start.7 = (f32[2,64,128]{2,1,0:T(8,128)}, f32[2,64,128]{2,1,0:T(8,128)S(1)}, u32[]{:S(2)}, u32[]{:S(2)}) collective-permute-start(f32[2,64,128]{2,1,0:T(8,128)} %get-tuple-element.12), channel_id=1, source_target_pairs={{0,8},{4,12},{8,0},{12,4},{1,9},{5,13},{9,1},{13,5},{2,10},{6,14},... | collective-permute-start | bytes 196616 | tf_op jit(solution)/shard_map/ppermute | solution.py:305
  27.7 0.0 collective-permute-done.11
  27.7 0.1 collective-permute-start.8
  27.8 0.0 collective-permute-done.10
  27.8 0.0 collective-permute-done.9
  27.8 0.8 %fusion.3 = (f32[1,128]{1,0:T(1,128)S(1)}, f32[1,128]{1,0:T(1,128)S(1)}) fusion(f32[8,128]{1,0:T(8,128)S(1)} %collective-permute-done.11, f32[8,128]{1,0:T(8,128)S(1)} %collective-permute-done.10, f32[8,128]{1,0:T(8,128)S(1)} %collective-permute-done.9, f32[8,128]{1,0:T(8,128)} %get-tuple-element.14), kind=kLoop, calls=%fused_computation.19 | loop fusion | flops 2944 | bytes 5120 | tf_op jit(solution)/shard_map/add | solution.py:158
  28.6 0.0 copy-start.10
  28.6 1.4 %collective-permute-start.14 = (f32[2,128]{1,0:T(2,128)S(1)}, f32[2,128]{1,0:T(2,128)S(1)}, u32[]{:S(2)}, u32[]{:S(2)}) collective-permute-start(f32[2,128]{1,0:T(2,128)S(1)} %pad_maximum_fusion.2.refs_6_), channel_id=1, source_target_pairs={{0,3},{1,2},{2,1},{3,0},{4,7},{5,6},{6,5},{7,4},{8,11},{9,10},{10,... | collective-permute-start | bytes 3080 | tf_op jit(solution)/shard_map/ppermute | solution.py:318
  30.0 2.0 %collective-permute-start.13 = (f32[2,128]{1,0:T(2,128)S(1)}, f32[2,128]{1,0:T(2,128)S(1)}, u32[]{:S(2)}, u32[]{:S(2)}) collective-permute-start(f32[2,128]{1,0:T(2,128)S(1)} %pad_maximum_fusion.2.refs_6_), channel_id=1, source_target_pairs={{0,2},{1,3},{2,0},{3,1},{4,6},{5,7},{6,4},{7,5},{8,10},{9,11},{10,... | collective-permute-start | bytes 3080 | tf_op jit(solution)/shard_map/ppermute | solution.py:318
  32.0 2.0 %collective-permute-done.14.refs_9_ = f32[2,128]{1,0:T(2,128)S(1)} collective-permute-done((f32[2,128]{1,0:T(2,128)S(1)}, f32[2,128]{1,0:T(2,128)S(1)}, u32[]{:S(2)}, u32[]{:S(2)}) %collective-permute-start.14) | collective-permute-done | bytes 1056 | tf_op jit(solution)/shard_map/ppermute | solution.py:318
  34.0 0.0 copy-start.11
  34.0 0.1 collective-permute-start.12
  34.1 0.4 collective-permute-done.13.refs_8_
  34.5 3.1 %collective-permute-done.12.refs_7_ = f32[2,128]{1,0:T(2,128)S(1)} collective-permute-done((f32[2,128]{1,0:T(2,128)S(1)}, f32[2,128]{1,0:T(2,128)S(1)}, u32[]{:S(2)}, u32[]{:S(2)}) %collective-permute-start.12) | collective-permute-done | bytes 1056 | tf_op jit(solution)/shard_map/ppermute | solution.py:318
  37.6 0.0 collective-permute-done.6.refs_3_
  37.6 0.0 collective-permute-done.7.refs_4_
  37.6 0.0 copy-start.3
  37.6 0.0 collective-permute-done.8.refs_5_
  37.6 0.0 copy-start.4
  37.6 0.0 copy-done.10
  37.7 0.0 copy-done.11
  37.7 0.0 copy-done.12
  37.7 0.5 %copy-done.13 = f32[2,128]{1,0:T(2,128)} copy-done((f32[2,128]{1,0:T(2,128)}, f32[2,128]{1,0:T(2,128)S(1)}, u32[]{:S(2)}) %copy-start.13) | copy-done | bytes 1048
  38.2 0.1 copy-done.2
  38.2 0.0 copy-done.3
  38.3 0.0 copy-done.4
  38.3 10.7 %fine.1 = bf16[8,512,128]{2,1,0:T(8,128)(2,1)} custom-call(s32[8,3]{1,0:T(8,128)} %copy-done.5, s32[8,6]{1,0:T(8,128)} %refs_1_.1, f32[2,64,128]{2,1,0:T(8,128)} %get-tuple-element.10.refs_2_, f32[2,64,128]{2,1,0:T(8,128)} %copy-done.2, f32[2,64,128]{2,1,0:T(8,128)} %copy-done.3, f32[2,64,128]{2,1,0:T(8,128)} %copy-done.4, f32[2,128]{1,0:T(2,128)} %copy-done.10, ...), custom_call_target="tpu_custom_call" | custom-call | tf_op jit(solution)/shard_map/fine/pallas_call | solution.py:323
  (9 shorter events, 0.0 us)
Async XLA Ops:
  0.8 0.6 %copy-start.5 = (s32[8,3]{1,0:T(8,128)}, s32[8,3]{1,0:T(8,128)S(1)}, u32[]{:S(2)}) copy-start(s32[8,3]{1,0:T(8,128)S(1)} %copy.17.refs_0_) | copy-start | bytes 292
  0.8 7.4 %collective-permute-start = (s32[8,3]{1,0:T(8,128)S(1)}, s32[8,3]{1,0:T(8,128)S(1)}, u32[]{:S(2)}, u32[]{:S(2)}) collective-permute-start(s32[8,3]{1,0:T(8,128)S(1)} %copy.17.refs_0_), channel_id=1, source_target_pairs={{0,4},{4,0},{8,12},{12,8},{1,5},{5,1},{9,13},{13,9},{2,6},{6,2},{1... | collective-permute-start | bytes 296 | tf_op jit(solution)/shard_map/ppermute | solution.py:262
  2.3 6.6 %collective-permute-start.3 = (bf16[32,16,128]{2,1,0:T(8,128)(2,1)S(1)}, bf16[32,16,128]{2,1,0:T(8,128)(2,1)S(1)}, u32[]{:S(2)}, u32[]{:S(2)}) collective-permute-start(bf16[32,16,128]{2,1,0:T(8,128)(2,1)S(1)} %get-tuple-element.19), channel_id=1, source_target_pairs={{4,8},{8,4},{5,9},{9,5},{6,10},{10,6},{7,11},{11,7},{20,24},{24,20... | collective-permute-start | bytes 393224 | tf_op jit(solution)/shard_map/ppermute | solution.py:271
  3.0 6.0 %collective-permute-start.2 = (bf16[32,16,128]{2,1,0:T(8,128)(2,1)S(1)}, bf16[32,16,128]{2,1,0:T(8,128)(2,1)S(1)}, u32[]{:S(2)}, u32[]{:S(2)}) collective-permute-start(bf16[32,16,128]{2,1,0:T(8,128)(2,1)S(1)} %get-tuple-element.20), channel_id=1, source_target_pairs={{0,4},{4,0},{8,12},{12,8},{1,5},{5,1},{9,13},{13,9},{2,6},{6,2},{1... | collective-permute-start | bytes 393224 | tf_op jit(solution)/shard_map/ppermute | solution.py:270
  8.2 0.6 %copy-start.8 = (s32[8,3]{1,0:T(8,128)}, s32[8,3]{1,0:T(8,128)S(1)}, u32[]{:S(2)}) copy-start(s32[8,3]{1,0:T(8,128)S(1)} %collective-permute-done.refs_1_) | copy-start | bytes 292
  8.3 0.7 %copy-start.9 = (s32[8,3]{0,1:T(4,128)S(1)}, s32[8,3]{0,1:T(4,128)}, u32[]{:S(2)}) copy-start(s32[8,3]{0,1:T(4,128)} %param.15) | copy-start | bytes 292
  8.9 5.2 %collective-permute-start.1 = (s32[2,8,3]{1,2,0:T(4,128)S(1)}, s32[2,8,3]{1,2,0:T(4,128)S(1)}, u32[]{:S(2)}, u32[]{:S(2)}) collective-permute-start(s32[2,8,3]{1,2,0:T(4,128)S(1)} %pad_add_fusion), channel_id=1, source_target_pairs={{0,8},{4,12},{8,0},{12,4},{1,9},{5,13},{9,1},{13,5},{2,10},{6,14},... | collective-permute-start | bytes 584 | tf_op jit(solution)/shard_map/ppermute | solution.py:264
  9.0 7.2 %copy-start = (bf16[32,16,128]{2,1,0:T(8,128)(2,1)}, bf16[32,16,128]{2,1,0:T(8,128)(2,1)S(1)}, u32[]{:S(2)}) copy-start(bf16[32,16,128]{2,1,0:T(8,128)(2,1)S(1)} %collective-permute-done.3.refs_6_) | copy-start | bytes 393220
  9.0 7.2 %copy-start.1 = (bf16[32,16,128]{2,1,0:T(8,128)(2,1)}, bf16[32,16,128]{2,1,0:T(8,128)(2,1)S(1)}, u32[]{:S(2)}) copy-start(bf16[32,16,128]{2,1,0:T(8,128)(2,1)S(1)} %collective-permute-done.2.refs_5_) | copy-start | bytes 393220
  9.0 6.5 %collective-permute-start.5 = (bf16[6,16,128]{2,1,0:T(8,128)(2,1)S(1)}, bf16[6,16,128]{2,1,0:T(8,128)(2,1)S(1)}, u32[]{:S(2)}, u32[]{:S(2)}) collective-permute-start(bf16[6,16,128]{2,1,0:T(8,128)(2,1)S(1)} %get-tuple-element.25), channel_id=1, source_target_pairs={{1,2},{2,1},{5,6},{6,5},{9,10},{10,9},{13,14},{14,13},{17,18},{18,... | collective-permute-start | bytes 73736 | tf_op jit(solution)/shard_map/ppermute | solution.py:275
  9.7 6.5 %collective-permute-start.4 = (bf16[6,16,128]{2,1,0:T(8,128)(2,1)S(1)}, bf16[6,16,128]{2,1,0:T(8,128)(2,1)S(1)}, u32[]{:S(2)}, u32[]{:S(2)}) collective-permute-start(bf16[6,16,128]{2,1,0:T(8,128)(2,1)S(1)} %get-tuple-element.26), channel_id=1, source_target_pairs={{0,1},{1,0},{2,3},{3,2},{4,5},{5,4},{6,7},{7,6},{8,9},{9,8},{10,11... | collective-permute-start | bytes 73736 | tf_op jit(solution)/shard_map/ppermute | solution.py:274
  15.5 0.6 %copy-start.6 = (bf16[6,16,128]{2,1,0:T(8,128)(2,1)}, bf16[6,16,128]{2,1,0:T(8,128)(2,1)S(1)}, u32[]{:S(2)}) copy-start(bf16[6,16,128]{2,1,0:T(8,128)(2,1)S(1)} %collective-permute-done.5.refs_8_) | copy-start | bytes 73732
  16.2 0.6 %copy-start.7 = (bf16[6,16,128]{2,1,0:T(8,128)(2,1)}, bf16[6,16,128]{2,1,0:T(8,128)(2,1)S(1)}, u32[]{:S(2)}) copy-start(bf16[6,16,128]{2,1,0:T(8,128)(2,1)S(1)} %collective-permute-done.4.refs_7_) | copy-start | bytes 73732
  23.1 4.5 %collective-permute-start.11 = (f32[8,128]{1,0:T(8,128)}, f32[8,128]{1,0:T(8,128)S(1)}, u32[]{:S(2)}, u32[]{:S(2)}) collective-permute-start(f32[8,128]{1,0:T(8,128)} %get-tuple-element.14), channel_id=1, source_target_pairs={{0,12},{4,8},{8,4},{12,0},{1,13},{5,9},{9,5},{13,1},{2,14},{6,10},... | collective-permute-start | bytes 12296 | tf_op jit(solution)/shard_map/ppermute | solution.py:304
  23.9 3.8 %collective-permute-start.10 = (f32[8,128]{1,0:T(8,128)}, f32[8,128]{1,0:T(8,128)S(1)}, u32[]{:S(2)}, u32[]{:S(2)}) collective-permute-start(f32[8,128]{1,0:T(8,128)} %get-tuple-element.14), channel_id=1, source_target_pairs={{0,8},{4,12},{8,0},{12,4},{1,9},{5,13},{9,1},{13,5},{2,10},{6,14},... | collective-permute-start | bytes 12296 | tf_op jit(solution)/shard_map/ppermute | solution.py:304
  25.9 1.9 %collective-permute-start.9 = (f32[8,128]{1,0:T(8,128)}, f32[8,128]{1,0:T(8,128)S(1)}, u32[]{:S(2)}, u32[]{:S(2)}) collective-permute-start(f32[8,128]{1,0:T(8,128)} %get-tuple-element.14), channel_id=1, source_target_pairs={{0,4},{4,0},{8,12},{12,8},{1,5},{5,1},{9,13},{13,9},{2,6},{6,2},{1... | collective-permute-start | bytes 12296 | tf_op jit(solution)/shard_map/ppermute | solution.py:304
  25.9 11.7 %collective-permute-start.6 = (f32[2,64,128]{2,1,0:T(8,128)}, f32[2,64,128]{2,1,0:T(8,128)S(1)}, u32[]{:S(2)}, u32[]{:S(2)}) collective-permute-start(f32[2,64,128]{2,1,0:T(8,128)} %get-tuple-element.11), channel_id=1, source_target_pairs={{0,4},{4,0},{8,12},{12,8},{1,5},{5,1},{9,13},{13,9},{2,6},{6,2},{1... | collective-permute-start | bytes 196616 | tf_op jit(solution)/shard_map/ppermute | solution.py:305
  26.4 11.2 %collective-permute-start.7 = (f32[2,64,128]{2,1,0:T(8,128)}, f32[2,64,128]{2,1,0:T(8,128)S(1)}, u32[]{:S(2)}, u32[]{:S(2)}) collective-permute-start(f32[2,64,128]{2,1,0:T(8,128)} %get-tuple-element.12), channel_id=1, source_target_pairs={{0,8},{4,12},{8,0},{12,4},{1,9},{5,13},{9,1},{13,5},{2,10},{6,14},... | collective-permute-start | bytes 196616 | tf_op jit(solution)/shard_map/ppermute | solution.py:305
  27.7 10.0 %collective-permute-start.8 = (f32[2,64,128]{2,1,0:T(8,128)}, f32[2,64,128]{2,1,0:T(8,128)S(1)}, u32[]{:S(2)}, u32[]{:S(2)}) collective-permute-start(f32[2,64,128]{2,1,0:T(8,128)} %get-tuple-element.13), channel_id=1, source_target_pairs={{0,12},{4,8},{8,4},{12,0},{1,13},{5,9},{9,5},{13,1},{2,14},{6,10},... | collective-permute-start | bytes 196616 | tf_op jit(solution)/shard_map/ppermute | solution.py:305
  28.6 9.1 %copy-start.10 = (f32[2,128]{1,0:T(2,128)}, f32[2,128]{1,0:T(2,128)S(1)}, u32[]{:S(2)}) copy-start(f32[2,128]{1,0:T(2,128)S(1)} %pad_maximum_fusion.2.refs_6_) | copy-start | bytes 3076
  28.6 5.4 %collective-permute-start.14 = (f32[2,128]{1,0:T(2,128)S(1)}, f32[2,128]{1,0:T(2,128)S(1)}, u32[]{:S(2)}, u32[]{:S(2)}) collective-permute-start(f32[2,128]{1,0:T(2,128)S(1)} %pad_maximum_fusion.2.refs_6_), channel_id=1, source_target_pairs={{0,3},{1,2},{2,1},{3,0},{4,7},{5,6},{6,5},{7,4},{8,11},{9,10},{10,... | collective-permute-start | bytes 3080 | tf_op jit(solution)/shard_map/ppermute | solution.py:318
  30.0 4.5 %collective-permute-start.13 = (f32[2,128]{1,0:T(2,128)S(1)}, f32[2,128]{1,0:T(2,128)S(1)}, u32[]{:S(2)}, u32[]{:S(2)}) collective-permute-start(f32[2,128]{1,0:T(2,128)S(1)} %pad_maximum_fusion.2.refs_6_), channel_id=1, source_target_pairs={{0,2},{1,3},{2,0},{3,1},{4,6},{5,7},{6,4},{7,5},{8,10},{9,11},{10,... | collective-permute-start | bytes 3080 | tf_op jit(solution)/shard_map/ppermute | solution.py:318
  34.0 3.6 %copy-start.11 = (f32[2,128]{1,0:T(2,128)}, f32[2,128]{1,0:T(2,128)S(1)}, u32[]{:S(2)}) copy-start(f32[2,128]{1,0:T(2,128)S(1)} %collective-permute-done.14.refs_9_) | copy-start | bytes 3076
  34.0 3.6 %collective-permute-start.12 = (f32[2,128]{1,0:T(2,128)S(1)}, f32[2,128]{1,0:T(2,128)S(1)}, u32[]{:S(2)}, u32[]{:S(2)}) collective-permute-start(f32[2,128]{1,0:T(2,128)S(1)} %pad_maximum_fusion.2.refs_6_), channel_id=1, source_target_pairs={{0,1},{1,0},{2,3},{3,2},{4,5},{5,4},{6,7},{7,6},{8,9},{9,8},{10,11... | collective-permute-start | bytes 3080 | tf_op jit(solution)/shard_map/ppermute | solution.py:318
  34.5 3.2 %copy-start.12 = (f32[2,128]{1,0:T(2,128)}, f32[2,128]{1,0:T(2,128)S(1)}, u32[]{:S(2)}) copy-start(f32[2,128]{1,0:T(2,128)S(1)} %collective-permute-done.13.refs_8_) | copy-start | bytes 3076
  37.6 0.6 %copy-start.13 = (f32[2,128]{1,0:T(2,128)}, f32[2,128]{1,0:T(2,128)S(1)}, u32[]{:S(2)}) copy-start(f32[2,128]{1,0:T(2,128)S(1)} %collective-permute-done.12.refs_7_) | copy-start | bytes 3076
  37.6 0.6 %copy-start.2 = (f32[2,64,128]{2,1,0:T(8,128)}, f32[2,64,128]{2,1,0:T(8,128)S(1)}, u32[]{:S(2)}) copy-start(f32[2,64,128]{2,1,0:T(8,128)S(1)} %collective-permute-done.6.refs_3_) | copy-start | bytes 196612
  37.6 0.6 %copy-start.3 = (f32[2,64,128]{2,1,0:T(8,128)}, f32[2,64,128]{2,1,0:T(8,128)S(1)}, u32[]{:S(2)}) copy-start(f32[2,64,128]{2,1,0:T(8,128)S(1)} %collective-permute-done.7.refs_4_) | copy-start | bytes 196612
  37.6 0.7 %copy-start.4 = (f32[2,64,128]{2,1,0:T(8,128)}, f32[2,64,128]{2,1,0:T(8,128)S(1)}, u32[]{:S(2)}) copy-start(f32[2,64,128]{2,1,0:T(8,128)S(1)} %collective-permute-done.8.refs_5_) | copy-start | bytes 196612

commit v2 on v1

v2 whole, which is shorter than its diff:
```python
import functools

import jax
import jax.numpy as jnp
from jax import lax
from jax.experimental import pallas as pl
from jax.experimental.pallas import tpu as pltpu
from jax.sharding import PartitionSpec as P

G = 32
FB = 8
EDGE = FB // 2
MOST = 2
EPS = 1e-05
F32 = jnp.float32
BF16 = jnp.bfloat16


def pairs(count, odd):
    links = []
    for i in range(odd, count - 1, 2):
        links += [(i, i + 1), (i + 1, i)]
    return links


def xor_links(count, distance):
    return [(i, i ^ distance) for i in range(count)]


def wide_weight(weight):
    return jnp.concatenate(
        [
            jnp.concatenate([weight[3 * ab + c] for c in range(3)], axis=1)
            for ab in range(9)
        ],
        axis=0,
    )


def shifted_sum(sums, depth, channels):
    rows = sums.shape[0]
    place = lax.broadcasted_iota(jnp.int32, (rows, channels), 0) % depth
    below = pltpu.roll(sums[:, :channels], 1, 0)
    above = pltpu.roll(sums[:, 2 * channels :], rows - 1, 0)
    return (
        sums[:, channels : 2 * channels]
        + jnp.where(place == 0, 0.0, below)
        + jnp.where(place == depth - 1, 0.0, above)
    )


def neighbour(links, n, direction, total):
    target = links[n, direction]
    return lax.rem(jnp.maximum(target, 0), total), target >= 0


def fold_weights(weight, out):
    channels = weight.shape[1]
    taps = (((0,), (1, 2)), ((0, 1), (2,)))
    for p in range(2):
        for q in range(2):
            for a in range(2):
                for b in range(2):
                    sums = []
                    for c in range(3):
                        parts = [
                            weight[9 * i + 3 * j + c].astype(F32)
                            for i in taps[p][a]
                            for j in taps[q][b]
                        ]
                        sums.append(functools.reduce(jnp.add, parts))
                    kinds = [sums[1] + sums[2], sums[0], sums[0] + sums[1], sums[2]]
                    rows = pl.ds((2 * a + b) * channels, channels)
                    for k, kind in enumerate(kinds):
                        out[2 * p + q, rows, pl.ds(k * channels, channels)] = kind.astype(BF16)


def parity(name, length):
    return jnp.where(lax.rem(lax.axis_index(name), 2) == 0, length - 1, 0)


def send_kernel(inp, coords, links, send_a, send_b, row_a, row_b, coords_out, links_out, note, sems):
    dx, dy = inp.shape[:2]
    xa, ya = parity("slab", dx), parity("sub", dy)
    moves = [
        (coords, coords_out),
        (inp.at[xa], send_a.at[pl.ds(0, dy)]),
        (inp.at[dx - 1 - xa], send_b),
        (inp.at[:, ya], row_a),
        (inp.at[:, dy - 1 - ya], row_b),
        (links, links_out),
    ]
    copies = [pltpu.make_async_copy(a, b, sems.at[i]) for i, (a, b) in enumerate(moves)]
    for copy in copies:
        copy.start()
    note[...] = jnp.zeros_like(note)
    copies[0].wait()
    note[pl.ds(0, coords.shape[0]), pl.ds(0, coords.shape[1])] = coords_out[...]
    send_a[dy] = note[...].astype(F32).astype(BF16)
    for copy in copies[1:]:
        copy.wait()


def line_kernel(x_first, x_second, row_a, row_b, line_a, line_b):
    dx, dy = row_a.shape[0], x_second.shape[0]
    ya = parity("sub", dy)
    for place, row, line in ((ya, row_a, line_a), (dy - 1 - ya, row_b, line_b)):
        line[0] = x_first[place]
        line[pl.ds(1, dx)] = row[...]
        line[dx + 1] = x_second[place]


def fine_kernel(first, count, role, *refs):
    loads = []
    if role == "load":
        links, fine_from, weight_from, inp = refs[:4]
        out, fine, weight, padded, even, odd, sems = refs[4:]
        dx, dy = inp.shape[:2]
        moves = [
            (fine_from, fine),
            (weight_from, weight),
            (inp, padded.at[pl.ds(1, dx), pl.ds(1, dy)]),
        ]
        loads = [pltpu.make_async_copy(a, b, sems.at[i]) for i, (a, b) in enumerate(moves)]
        for load in loads:
            load.start()
        loads[0].wait()
    elif role == "fold":
        links, fine, weight, _, out, folded, even, odd = refs
        fold_weights(weight, folded)
    else:
        links, fine, weight, _, out, even, odd = refs
    total, _, channels = fine.shape
    tile = 2 * FB
    lines = FB // 2

    def plane(n, i):
        return fine[n, pl.ds(i * FB * FB, FB * FB), :].reshape(lines, tile, channels)

    zero = jnp.zeros((FB, channels), F32)
    for slot in range(count):
        n = first + slot
        sides = [neighbour(links, n, direction, total) for direction in range(4)]
        for i in range(-1, FB + 1):
            if 0 <= i < FB:
                here = plane(n, i)
                (low, low_on), (high, high_on) = sides[2], sides[3]
                before = fine[low, pl.ds(i * FB * FB + FB * FB - tile, tile), :].astype(F32)
                after = fine[high, pl.ds(i * FB * FB, tile), :].astype(F32)
                before = jnp.where(low_on, before[FB:], 0.0)
                after = jnp.where(high_on, after[:FB], 0.0)
            else:
                other, on = sides[0] if i < 0 else sides[1]
                here = plane(other, FB - 1 if i < 0 else 0)
                here = jnp.where(on, here, jnp.zeros_like(here))
                before = after = zero
            even[slot, i + 1] = here
            wide = here.astype(F32)
            halves = [before]
            for line in range(lines):
                halves += [wide[line, :FB], wide[line, FB:]]
            halves.append(after)
            for line in range(lines + 1):
                odd[slot, i + 1, line] = jnp.concatenate(
                    halves[2 * line : 2 * line + 2], axis=0
                ).astype(BF16)
        if role == "load" and slot == 0:
            loads[1].wait()
        taken = []
        for a in range(3):
            for b in range(3):
                if b == 1:
                    part = even[slot, pl.ds(a, FB)]
                else:
                    part = odd[slot, pl.ds(a, FB), pl.ds(b // 2, lines)]
                taken.append(part.reshape(FB**3, channels))
        sums = jnp.dot(
            jnp.concatenate(taken, axis=1), wide_weight(weight), preferred_element_type=F32
        )
        out[slot] = shifted_sum(sums, FB, channels)
    for load in loads[2:]:
        load.wait()


def coarse_kernel(sources, xor, cells_shape, total_blocks, *refs):
    own, far = refs[:2]
    _, x_first, x_second, y_first, y_second, weight = refs[2:8]
    outs = refs[8:-5]
    padded, conv, notes, wanted, sems = refs[-5:]
    dx, dy, dz = cells_shape
    asked = [own[dy], x_first[dy], far[0], far[1]] if xor else [far[s] for s in range(sources)]
    for s, note in enumerate(asked):
        notes[s] = note.astype(F32).astype(jnp.int32)
    noted = pltpu.make_async_copy(notes, wanted, sems.at[2])
    noted.start()
    channels = padded.shape[-1]
    slab = lax.axis_index("slab")
    sub = lax.axis_index("sub")
    rows = pl.ds(1, dy)
    xa = jnp.where(lax.rem(slab, 2) == 0, dx + 1, 0)
    xb = dx + 1 - xa
    ya = jnp.where(lax.rem(sub, 2) == 0, dy + 1, 0)
    yb = dy + 1 - ya
    moves = [(x_first.at[pl.ds(0, dy)], padded.at[xa, rows]), (x_second, padded.at[xb, rows])]
    copies = [pltpu.make_async_copy(a, b, sems.at[i]) for i, (a, b) in enumerate(moves)]
    for copy in copies:
        copy.start()
    for got, place in ((y_first, ya), (y_second, yb)):
        padded[xa, place] = got[0]
        for x in range(dx):
            padded[1 + x, place] = got[1 + x]
        padded[xb, place] = got[dx + 1]
    for copy in copies:
        copy.wait()
    total = jnp.zeros((8, channels), F32)
    for x in range(dx):
        taken = [
            padded[x + a, pl.ds(b, dy)].reshape(dy * dz, channels)
            for a in range(3)
            for b in range(3)
        ]
        sums = jnp.dot(
            jnp.concatenate(taken, axis=1), wide_weight(weight), preferred_element_type=F32
        )
        value = shifted_sum(sums, dz, channels)
        conv[x] = value.reshape(dy, dz, channels)
        total = total + jnp.sum(value.reshape(-1, 8, channels), axis=0)
    mean = jnp.sum(total, axis=0, keepdims=True) / (dx * dy * dz)
    square = jnp.zeros((8, channels), F32)
    for x in range(dx):
        off = conv[x].reshape(-1, 8, channels) - mean[None]
        square = square + jnp.sum(off * off, axis=0)
    square = jnp.sum(square, axis=0, keepdims=True)
    noted.wait()
    for s in range(sources):
        seen = jnp.int32(0)
        where_y = [jnp.int32(0)] * MOST
        where_z = [jnp.int32(0)] * MOST
        for n in range(total_blocks):
            hit = wanted[s, 0, n] == slab
            y = wanted[s, 1, n] - sub * (dy // EDGE)
            for slot in range(MOST):
                here = jnp.logical_and(hit, seen == slot)
                where_y[slot] = jnp.where(here, y, where_y[slot])
                where_z[slot] = jnp.where(here, wanted[s, 2, n], where_z[slot])
            seen = seen + hit.astype(jnp.int32)
        out = outs[s] if xor else outs[0].at[s]
        for slot in range(MOST):
            for x in range(EDGE):
                for y in range(EDGE):
                    piece = conv[x, EDGE * where_y[slot] + y, pl.ds(EDGE * where_z[slot], EDGE), :]
                    out[pl.ds(slot * EDGE**3 + (x * EDGE + y) * EDGE, EDGE), :] = piece
        out[pl.ds(MOST * EDGE**3, 1), :] = mean
        out[pl.ds(MOST * EDGE**3 + 1, 1), :] = square


def group_sum(value, size):
    lanes = value.shape[-1]
    place = lax.broadcasted_iota(jnp.int32, value.shape, 1) % size
    total = value
    for step in range(1, size):
        total = total + jnp.where(place >= step, pltpu.roll(value, step, 1), 0.0)
        total = total + jnp.where(place + step < size, pltpu.roll(value, lanes - step, 1), 0.0)
    return total


def merge(means, squares, count):
    mean = sum(means) / len(means)
    square = sum(squares)
    for part in means:
        square = square + count * (part - mean) * (part - mean)
    return mean, square


def final_kernel(cube_lists, stat_lists, cells, xor, *refs):
    coords, links = refs[:2]
    cubes = refs[2 : 2 + cube_lists]
    stats = refs[2 + cube_lists : 2 + cube_lists + stat_lists]
    rest = refs[2 + cube_lists + stat_lists :]
    gain, bias, lift, fine, folded = rest[:5]
    pieces, out_to = rest[5:-9], rest[-9]
    held, acted, lifted, twice, frame, spread, out, sems = rest[-8:]
    total, _, channels = fine.shape
    slab = lax.axis_index("slab")
    volume = EDGE**3
    for i, cube in enumerate(cubes):
        for slot in range(MOST):
            if xor:
                held[MOST * i + slot] = cube[pl.ds(slot * volume, volume), :]
            else:
                for s in range(cube.shape[0]):
                    held[MOST * s + slot] = cube[s, pl.ds(slot * volume, volume), :]
    size = channels // G
    mean, square = merge(
        [s[0:1, :] for s in stats], [s[1:2, :] for s in stats], float(cells)
    )
    cells = cells * stat_lists
    group_mean = group_sum(mean, size) / size
    off = mean - group_mean
    group_var = group_sum(square + cells * off * off, size) / (cells * size)
    scale = lax.rsqrt(group_var + EPS)
    for n in range(total):
        holder = coords[0, n]
        rank = jnp.int32(0)
        for m in range(n):
            rank = rank + (coords[0, m] == holder).astype(jnp.int32)
        source = jnp.bitwise_xor(holder, slab) if xor else holder
        value = held[source * MOST + rank]
        normed = (value - group_mean) * scale * gain[...] + bias[...]
        acted[pl.ds(n * volume, volume), :] = (normed / (1.0 + jnp.exp(-normed))).astype(BF16)
    rounded = jnp.dot(acted[...], lift[...], preferred_element_type=F32).astype(BF16).astype(F32)
    rows = total * volume
    twice[pl.ds(0, rows, stride=2), :] = rounded
    twice[pl.ds(1, rows, stride=2), :] = rounded
    flat = EDGE * EDGE
    lifted[...] = rounded.reshape(total, EDGE, flat, channels)
    place = lax.broadcasted_iota(jnp.int32, (flat, channels), 0)
    for n in range(total):
        sides = [neighbour(links, n, direction, total) for direction in range(4)]
        for i in range(-1, EDGE + 1):
            if 0 <= i < EDGE:
                here = lifted[n, i]
                (low, low_on), (high, high_on) = sides[2], sides[3]
                before = jnp.where(low_on, lifted[low, i], 0.0)
                after = jnp.where(high_on, lifted[high, i], 0.0)
                before = pltpu.roll(before, EDGE, 0)
                after = pltpu.roll(after, flat - EDGE, 0)
            else:
                other, on = sides[0] if i < 0 else sides[1]
                here = jnp.where(on, lifted[other, EDGE - 1 if i < 0 else 0], 0.0)
                before = after = jnp.zeros_like(here)
            frame[0, n, i + 1] = jnp.where(
                place < EDGE, before, pltpu.roll(here, EDGE, 0)
            ).astype(BF16)
            frame[1, n, i + 1] = here.astype(BF16)
            frame[2, n, i + 1] = jnp.where(
                place >= flat - EDGE, after, pltpu.roll(here, flat - EDGE, 0)
            ).astype(BF16)
    level = lax.broadcasted_iota(jnp.int32, (rows, channels), 0) % EDGE
    for p in range(2):
        for q in range(2):
            taken = [
                frame[q + b, :, pl.ds(p + a, EDGE)].reshape(rows, channels)
                for a in range(2)
                for b in range(2)
            ]
            sums = jnp.dot(
                jnp.concatenate(taken, axis=1), folded[2 * p + q], preferred_element_type=F32
            )
            below = pltpu.roll(sums[:, channels : 2 * channels], 1, 0)
            above = pltpu.roll(sums[:, 3 * channels :], rows - 1, 0)
            even = sums[:, :channels] + jnp.where(level == 0, 0.0, below)
            odd = sums[:, 2 * channels : 3 * channels] + jnp.where(level == EDGE - 1, 0.0, above)
            spread[2 * p + q, pl.ds(0, rows, stride=2), :] = even
            spread[2 * p + q, pl.ds(1, rows, stride=2), :] = odd
    copies = []
    whole = [piece.at[n] for piece in pieces for n in range(piece.shape[0])]
    for n, part in enumerate(whole):
        for i in range(FB):
            for j in range(0, FB, 2):
                cell = pl.ds(((n * EDGE + i // 2) * EDGE + j // 2) * FB, FB)
                pair = pl.ds((i * FB + j) * FB, 2 * FB)
                up = twice[cell, :]
                raised = jnp.concatenate([up, up], axis=0)
                own = (fine[n, pair, :].astype(F32) + raised).astype(BF16).astype(F32)
                conv = jnp.concatenate(
                    [spread[2 * (i % 2), cell, :], spread[2 * (i % 2) + 1, cell, :]], axis=0
                )
                out[n, pair, :] = (own + part[pair, :] + conv).astype(BF16)
        copies.append(pltpu.make_async_copy(out.at[n], out_to.at[n], sems.at[n]))
        copies[-1].start()
    for copy in copies:
        copy.wait()


SMEM = pl.BlockSpec(memory_space=pltpu.SMEM)
VMEM = pl.BlockSpec(memory_space=pltpu.VMEM)
HBM = pl.BlockSpec(memory_space=pl.ANY)


def limit(mib):
    return pltpu.CompilerParams(vmem_limit_bytes=mib * 2**20)


def fine_part(links, fine, weight, after, first, count, role):
    total, cells, channels = fine.shape
    shapes = [jax.ShapeDtypeStruct((count, cells, channels), F32)]
    specs, sems = [SMEM, VMEM, VMEM, HBM], []
    if role == "fold":
        shapes.append(jax.ShapeDtypeStruct((4, 4 * channels, 4 * channels), BF16))
    if role == "load":
        dx, dy, dz, _ = after.shape
        extra = [fine.shape, weight.shape, (dx + 2, dy + 2, dz, channels)]
        shapes += [jax.ShapeDtypeStruct(shape, BF16) for shape in extra]
        specs = [SMEM] + [pl.BlockSpec(memory_space=pltpu.HBM)] * 3
        sems = [pltpu.SemaphoreType.DMA((len(extra),))]
        fine, weight, after = (
            pltpu.with_memory_space_constraint(x, pltpu.HBM) for x in (fine, weight, after)
        )
    return pl.pallas_call(
        functools.partial(fine_kernel, first, count, role),
        out_shape=shapes,
        in_specs=specs,
        out_specs=[VMEM] * len(shapes),
        scratch_shapes=[
            pltpu.VMEM((count, FB + 2, FB // 2, 2 * FB, channels), BF16),
            pltpu.VMEM((count, FB + 2, FB // 2 + 1, 2 * FB, channels), BF16),
        ]
        + sems,
        compiler_params=limit(18),
        cost_estimate=pl.CostEstimate(
            flops=2 * 27 * count * cells * channels * channels,
            bytes_accessed=4 * count * cells * channels,
            transcendentals=0,
        ),
        name="fine_part",
    )(links, fine, weight, after)


def body(
    coarse_in,
    coarse_weight,
    norm_gain,
    norm_bias,
    lift_weight,
    fine_input,
    block_coords,
    neighbours,
    fine_weight,
):
    dx, dy, dz, channels = coarse_in.shape
    slabs, subs = lax.axis_size("slab"), lax.axis_size("sub")
    total = block_coords.shape[0]
    xor = slabs == 4
    coords = block_coords.T
    send_a, send_b, row_a, row_b, coords, links = pl.pallas_call(
        send_kernel,
        out_shape=[
            jax.ShapeDtypeStruct((dy + 1, dz, channels), BF16),
            jax.ShapeDtypeStruct((dy, dz, channels), BF16),
            jax.ShapeDtypeStruct((dx, dz, channels), BF16),
            jax.ShapeDtypeStruct((dx, dz, channels), BF16),
            jax.ShapeDtypeStruct(coords.shape, jnp.int32),
            jax.ShapeDtypeStruct(neighbours.shape, jnp.int32),
        ],
        in_specs=[pl.BlockSpec(memory_space=pltpu.HBM)] * 3,
        out_specs=[VMEM] * 6,
        scratch_shapes=[pltpu.VMEM((dz, channels), jnp.int32), pltpu.SemaphoreType.DMA((6,))],
        compiler_params=limit(4),
        name="send",
    )(*(pltpu.with_memory_space_constraint(x, pltpu.HBM) for x in (coarse_in, coords, neighbours)))
    x_first = lax.ppermute(send_a, "slab", pairs(slabs, 0))
    x_second = lax.ppermute(send_b, "slab", pairs(slabs, 1))
    if xor:
        both = jnp.stack([send_a[dy], x_first[dy]])
        far = lax.ppermute(both, "slab", xor_links(slabs, 2))
    else:
        far = lax.all_gather(send_a[dy], "slab", axis=0)
    shares = [0, total // 4, total * 3 // 4, total]
    pieces = []

    def fill(index, after, waiting, role="plain"):
        begin = shares[index]
        made = fine_part(links, fine, weight, after, begin, shares[index + 1] - begin, role)
        made, waiting = lax.optimization_barrier((made, waiting))
        pieces.append(made[0])
        return made[1:], waiting

    fine, weight = fine_input, fine_weight
    made, (x_first, x_second, far) = fill(0, coarse_in, (x_first, x_second, far), "load")
    fine, weight, padded = made
    line_a, line_b = pl.pallas_call(
        line_kernel,
        out_shape=[jax.ShapeDtypeStruct((dx + 2, dz, channels), BF16)] * 2,
        in_specs=[VMEM] * 4,
        out_specs=[VMEM] * 2,
        compiler_params=limit(4),
        name="line",
    )(x_first, x_second, row_a, row_b)
    y_first = lax.ppermute(line_a, "sub", pairs(subs, 0))
    y_second = lax.ppermute(line_b, "sub", pairs(subs, 1))

    piece = (MOST * EDGE**3 + 8, channels)
    if xor:
        shapes = [jax.ShapeDtypeStruct(piece, F32)] * slabs
    else:
        shapes = [jax.ShapeDtypeStruct((slabs,) + piece, F32)]
    results = pl.pallas_call(
        functools.partial(coarse_kernel, slabs, xor, (dx, dy, dz), total),
        out_shape=shapes + [jax.ShapeDtypeStruct(padded.shape, BF16)],
        in_specs=[VMEM] * 8,
        out_specs=[VMEM] * (len(shapes) + 1),
        scratch_shapes=[
            pltpu.VMEM((dx, dy, dz, channels), F32),
            pltpu.VMEM((slabs, dz, channels), jnp.int32),
            pltpu.SMEM((slabs, dz, channels), jnp.int32),
            pltpu.SemaphoreType.DMA((3,)),
        ],
        input_output_aliases={2: len(shapes)},
        compiler_params=limit(12),
        name="coarse",
    )(send_a, far, padded, x_first, x_second, y_first, y_second, coarse_weight)
    sent = results[:-1]
    cells = dx * dy * dz
    row = MOST * EDGE**3
    if xor:
        replies = [sent[0]] + [
            lax.ppermute(sent[distance], "slab", xor_links(slabs, distance))
            for distance in range(1, slabs)
        ]
        parts = [r[row : row + 2] for r in replies]
    else:
        replies = [lax.all_to_all(sent[0], "slab", split_axis=0, concat_axis=0, tiled=True)]
        parts = [replies[0][s, row : row + 2] for s in range(slabs)]
    _, parts = fill(1, sent[0], parts)
    mean, square = merge([p[0:1] for p in parts], [p[1:2] for p in parts], float(cells))
    cells = cells * slabs
    merged = jnp.concatenate([mean, square])
    if subs == 4:
        lines = [merged] + [
            lax.ppermute(merged, "sub", xor_links(subs, distance)) for distance in range(1, subs)
        ]
    else:
        lines = list(lax.all_gather(merged, "sub", axis=0))
    (folded,), lines = fill(2, merged, lines, "fold")

    volume = EDGE**3
    return pl.pallas_call(
        functools.partial(final_kernel, len(replies), len(lines), cells, xor),
        out_shape=jax.ShapeDtypeStruct(fine_input.shape, BF16),
        in_specs=[SMEM] * 2 + [VMEM] * (len(replies) + len(lines) + 5 + len(pieces)),
        out_specs=HBM,
        scratch_shapes=[
            pltpu.VMEM((slabs * MOST, volume, channels), F32),
            pltpu.VMEM((total * volume, channels), BF16),
            pltpu.VMEM((total, EDGE, EDGE * EDGE, channels), F32),
            pltpu.VMEM((2 * total * volume, channels), F32),
            pltpu.VMEM((3, total, EDGE + 2, EDGE * EDGE, channels), BF16),
            pltpu.VMEM((4, 2 * total * volume, channels), F32),
            pltpu.VMEM(fine_input.shape, BF16),
            pltpu.SemaphoreType.DMA((total,)),
        ],
        compiler_params=limit(18),
        name="final",
    )(
        coords,
        links,
        *replies,
        *lines,
        norm_gain.reshape(1, channels),
        norm_bias.reshape(1, channels),
        lift_weight,
        fine,
        folded,
        *pieces,
    )


def solution(mesh):
    in_specs = (
        P(("scene", "slab"), "sub", None, None),
        P(),
        P(),
        P(),
        P(),
        P(("scene", "slab", "sub"), None, None),
        P(("scene", "slab", "sub"), None),
        P(("scene", "slab", "sub"), None),
        P(),
    )
    out_specs = P(("scene", "slab", "sub"), None, None)
    return jax.shard_map(body, mesh=mesh, in_specs=in_specs, out_specs=out_specs, check_vma=False)
```

time: 49.4 us -> 37.2 us (0.75)
  local copies, waits for them, and re-layouts: 4.97 us -> 0.04 us
  waiting for transfers between devices: 6.17 us -> 2 us
  starting transfers between devices: 18.8 us -> 16.7 us
  other arithmetic: 1.79 us -> 0.03 us
  Pallas kernels: 17 us -> 18.1 us
    ppermute x8 -> x4, starting transfers between devices: 13.5 us -> 4.09 us  [the longest x1 2.23 us: body(): y_first = lax.ppermute(line_a, 'sub', pairs(subs, 0))]
    ppermute x3, waiting for transfers between devices: 5.5 us -> 0.34 us  [body(): lax.ppermute(merged, 'sub', xor_links(subs, distance))]
    ppermute x3, starting transfers between devices: 3.5 us -> 7.12 us  [body(): lax.ppermute(merged, 'sub', xor_links(subs, distance))]
    ppermute x1, starting transfers between devices: 0.01 us -> 3.55 us  [body(): far = lax.ppermute(both, 'slab', xor_links(slabs, 2))]
    unnamed x29 -> x8, local copies, waits for them, and re-layouts: 2.8 us -> 0.02 us
    squeeze x4 -> x0, local copies, waits for them, and re-layouts: 2.08 us -> none  [the longest x3 1.35 us: body(): asked = [block_coords, near, far[0], far[1]]]
    pallas_call x2 -> x7, Pallas kernels: 17 us -> 18.1 us  [the longest x3 9.71 us: fine_part(): pl.pallas_call(functools.partial(fine_kernel, first, count, role), out_sh...]
    select_n x2 -> x0, other arithmetic: 1 us -> none  [the longest x1 0.99 us: body(): jnp.where(x_even, first, last)]
  transfers between devices with their start and end apart: 15 -> 11, of which waited for: 4 -> 4; matrix products, arithmetic and copies ran while one was open for 8% -> 0% of each run, Pallas kernels for 0% -> 26%
where the time goes in v2:
time: 37.2 us; the launch traced here: 37.1 us
  Pallas kernels  18.1 us (49%)
  starting transfers between devices  16.7 us (45%)
  waiting for transfers between devices  2 us (5%)
    pallas_call x3, Pallas kernels, fine_part(): pl.pallas_call(functools.partial(fine_kernel, first, count, role), out_sh...  9.71 us
    ppermute x3, starting transfers between devices, body(): lax.ppermute(merged, 'sub', xor_links(subs, distance))  7.12 us
    pallas_call x1, Pallas kernels, body(): pl.pallas_call(functools.partial(final_kernel, len(replies), len(lines),...  3.77 us
    ppermute x1, starting transfers between devices, body(): far = lax.ppermute(both, 'slab', xor_links(slabs, 2))  3.55 us
    pallas_call x1, Pallas kernels, body(): pl.pallas_call(functools.partial(coarse_kernel, slabs, xor, (dx, dy, dz),...  3.51 us
    ppermute x1, starting transfers between devices, body(): y_first = lax.ppermute(line_a, 'sub', pairs(subs, 0))  2.23 us
    ppermute x3, starting transfers between devices, body(): lax.ppermute(sent[distance], 'slab', xor_links(slabs, distance))  1.92 us
    ppermute x1, waiting for transfers between devices, body(): y_first = lax.ppermute(line_a, 'sub', pairs(subs, 0))  1.15 us
  transfers between devices with their start and end apart: 11, of which 4 were waited for; matrix products, arithmetic and copies ran while one was open for 0% of the time, Pallas kernels for 26%

profile of v2, /device:TPU:0, one launch (start us, length us, event | category | flops | bytes accessed | tf_op | source)
XLA Modules:
  0.0 37.1 jit_solution(15310830972567804775)
XLA Ops:
  0.0 0.0 copy-start
  0.0 1.1 %send.1 = (bf16[33,16,128]{2,1,0:T(8,128)(2,1)S(1)}, bf16[32,16,128]{2,1,0:T(8,128)(2,1)S(1)}, bf16[4,16,128]{2,1,0:T(8,128)(2,1)S(1)}, bf16[4,16,128]{2,1,0:T(8...) custom-call(bf16[4,32,16,128]{3,2,1,0:T(8,128)(2,1)} %refs_3_.1, s32[3,8]{1,0:T(4,128)} %bitcast.5, s32[8,6]{1,0:T(8,128)} %links.1), custom_call_target="tpu_custom_call" | custom-call | tf_op jit(solution)/shard_map/send/pallas_call | solution.py:436
  1.1 0.6 %collective-permute-start = (bf16[33,16,128]{2,1,0:T(8,128)(2,1)S(1)}, bf16[33,16,128]{2,1,0:T(8,128)(2,1)S(1)}, u32[]{:S(2)}, u32[]{:S(2)}) collective-permute-start(bf16[33,16,128]{2,1,0:T(8,128)(2,1)S(1)} %get-tuple-element.43.refs_0_), channel_id=1, source_target_pairs={{0,4},{4,0},{8,12},{12,8},{1,5},{5,1},{9,13},{13,9},{2,6},{6,2},{1... | collective-permute-start | bytes 405512 | tf_op jit(solution)/shard_map/ppermute | solution.py:452
  1.7 0.7 %collective-permute-start.1 = (bf16[32,16,128]{2,1,0:T(8,128)(2,1)S(1)}, bf16[32,16,128]{2,1,0:T(8,128)(2,1)S(1)}, u32[]{:S(2)}, u32[]{:S(2)}) collective-permute-start(bf16[32,16,128]{2,1,0:T(8,128)(2,1)S(1)} %get-tuple-element.48), channel_id=1, source_target_pairs={{4,8},{8,4},{5,9},{9,5},{6,10},{10,6},{7,11},{11,7},{20,24},{24,20... | collective-permute-start | bytes 393224 | tf_op jit(solution)/shard_map/ppermute | solution.py:453
  2.4 0.3 collective-permute-done.x_first.refs_3_
  2.7 3.6 %collective-permute-start.2 = (bf16[2,16,128]{2,1,0:T(8,128)(2,1)S(1)}, bf16[2,16,128]{2,1,0:T(8,128)(2,1)S(1)}, u32[]{:S(2)}, u32[]{:S(2)}) collective-permute-start(bf16[2,16,128]{2,1,0:T(8,128)(2,1)S(1)} %pad_maximum_fusion), channel_id=1, source_target_pairs={{0,8},{4,12},{8,0},{12,4},{1,9},{5,13},{9,1},{13,5},{2,10},{6,14},... | collective-permute-start | bytes 24584 | tf_op jit(solution)/shard_map/ppermute | solution.py:456
  6.2 3.6 %fine_part.3 = (f32[2,512,128]{2,1,0:T(8,128)S(1)}, bf16[8,512,128]{2,1,0:T(8,128)(2,1)S(1)}, bf16[27,128,128]{2,1,0:T(8,128)(2,1)S(1)}, bf16[6,34,16,128]{3,2,1,0:T(8,128)(2,1)S(1)}) custom-call(s32[8,6]{1,0:T(8,128)S(1)} %get-tuple-element.42.refs_0_.refs_1_, bf16[8,512,128]{2,1,0:T(8,128)(2,1)} %refs_1_.1, bf16[27,128,128]{2,1,0:T(8,128)(2,1)} %refs_2_.1, ...), custom_call_target="tpu_custom_call" | custom-call | flops 905969664 | bytes 524288 | tf_op jit(solution)/shard_map/fine_part/pallas_call | solution.py:400
  9.8 0.0 collective-permute-done.1.x_second.refs_4_
  9.8 0.0 collective-permute-done.2.refs_1_
  9.9 2.2 %collective-permute-start.3 = (bf16[6,16,128]{2,1,0:T(8,128)(2,1)S(1)}, bf16[6,16,128]{2,1,0:T(8,128)(2,1)S(1)}, u32[]{:S(2)}, u32[]{:S(2)}) collective-permute-start(bf16[6,16,128]{2,1,0:T(8,128)(2,1)S(1)} %get-tuple-element.55), channel_id=1, source_target_pairs={{0,1},{1,0},{2,3},{3,2},{4,5},{5,4},{6,7},{7,6},{8,9},{9,8},{10,11... | collective-permute-start | bytes 73736 | tf_op jit(solution)/shard_map/ppermute | solution.py:480
  12.1 0.7 %collective-permute-start.4 = (bf16[6,16,128]{2,1,0:T(8,128)(2,1)S(1)}, bf16[6,16,128]{2,1,0:T(8,128)(2,1)S(1)}, u32[]{:S(2)}, u32[]{:S(2)}) collective-permute-start(bf16[6,16,128]{2,1,0:T(8,128)(2,1)S(1)} %get-tuple-element.56), channel_id=1, source_target_pairs={{1,2},{2,1},{5,6},{6,5},{9,10},{10,9},{13,14},{14,13},{17,18},{18,... | collective-permute-start | bytes 73736 | tf_op jit(solution)/shard_map/ppermute | solution.py:481
  12.8 1.1 %collective-permute-done.3.refs_5_ = bf16[6,16,128]{2,1,0:T(8,128)(2,1)S(1)} collective-permute-done((bf16[6,16,128]{2,1,0:T(8,128)(2,1)S(1)}, bf16[6,16,128]{2,1,0:T(8,128)(2,1)S(1)}, u32[]{:S(2)}, u32[]{:S(2)}) %collective-permute-start.3) | collective-permute-done | bytes 24608 | tf_op jit(solution)/shard_map/ppermute | solution.py:480
  13.9 0.0 collective-permute-done.4.refs_6_
  13.9 0.0 copy-done
  13.9 3.5 %coarse.1 = (f32[136,128]{1,0:T(8,128)S(1)}, f32[136,128]{1,0:T(8,128)S(1)}, f32[136,128]{1,0:T(8,128)S(1)}, f32[136,128]{1,0:T(8,128)S(1)}, bf16[6,34,16,128]{3,2,1,0:T(8,128)(2,1)S(1)}) custom-call(bf16[33,16,128]{2,1,0:T(8,128)(2,1)S(1)} %get-tuple-element.43.refs_0_, ...), custom_call_target="tpu_custom_call", output_to_operand_aliasing={{4}: (2, {})} | custom-call | tf_op jit(solution)/shard_map/coarse/pallas_call | solution.py:488
  17.4 0.1 collective-permute-start.5
  17.5 0.8 %collective-permute-start.6 = (f32[136,128]{1,0:T(8,128)S(1)}, f32[136,128]{1,0:T(8,128)S(1)}, u32[]{:S(2)}, u32[]{:S(2)}) collective-permute-start(f32[136,128]{1,0:T(8,128)S(1)} %get-tuple-element.59), channel_id=1, source_target_pairs={{0,8},{4,12},{8,0},{12,4},{1,9},{5,13},{9,1},{13,5},{2,10},{6,14},... | collective-permute-start | bytes 208904 | tf_op jit(solution)/shard_map/ppermute | solution.py:508
  18.3 1.1 %collective-permute-start.7 = (f32[136,128]{1,0:T(8,128)S(1)}, f32[136,128]{1,0:T(8,128)S(1)}, u32[]{:S(2)}, u32[]{:S(2)}) collective-permute-start(f32[136,128]{1,0:T(8,128)S(1)} %get-tuple-element.60), channel_id=1, source_target_pairs={{0,12},{4,8},{8,4},{12,0},{1,13},{5,9},{9,5},{13,1},{2,14},{6,10},... | collective-permute-start | bytes 208904 | tf_op jit(solution)/shard_map/ppermute | solution.py:508
  19.4 3.4 %fine_part.4.refs_16_ = f32[4,512,128]{2,1,0:T(8,128)S(1)} custom-call(s32[8,6]{1,0:T(8,128)S(1)} %get-tuple-element.42.refs_0_.refs_1_, bf16[8,512,128]{2,1,0:T(8,128)(2,1)S(1)} %get-tuple-element.61.refs_1_.refs_13_, bf16[27,128,128]{2,1,0:T(8,128)(2,1)S(1)} %get-tuple-element.62.refs_2_, f32[136,128]{1,0:T(8,128)S(1)} %get-tuple-element.57.refs_3_.refs_2_), custom_call_target="tpu_custom_call" | custom-call | flops 1811939328 | bytes 1048576 | tf_op jit(solution)/shard_map/fine_part/pallas_call | solution.py:400
  22.8 0.0 copy-start.1
  22.8 0.0 copy-start.2
  22.8 0.0 copy-start.3
  22.8 0.0 collective-permute-done.5.refs_3_
  22.8 0.0 collective-permute-done.6.refs_4_
  22.9 0.2 collective-permute-done.7.refs_5_
  23.1 4.1 %collective-permute-start.10 = (f32[2,128]{1,0:T(2,128)S(1)}, f32[2,128]{1,0:T(2,128)S(1)}, u32[]{:S(2)}, u32[]{:S(2)}) collective-permute-start(f32[2,128]{1,0:T(2,128)S(1)} %pad_maximum_fusion.1.refs_3_.refs_6_), channel_id=1, source_target_pairs={{0,3},{1,2},{2,1},{3,0},{4,7},{5,6},{6,5},{7,4},{8,11},{9,10},{10,... | collective-permute-start | bytes 3080 | tf_op jit(solution)/shard_map/ppermute | solution.py:521
  27.2 2.5 %collective-permute-start.9 = (f32[2,128]{1,0:T(2,128)S(1)}, f32[2,128]{1,0:T(2,128)S(1)}, u32[]{:S(2)}, u32[]{:S(2)}) collective-permute-start(f32[2,128]{1,0:T(2,128)S(1)} %pad_maximum_fusion.1.refs_3_.refs_6_), channel_id=1, source_target_pairs={{0,2},{1,3},{2,0},{3,1},{4,6},{5,7},{6,4},{7,5},{8,10},{9,11},{10,... | collective-permute-start | bytes 3080 | tf_op jit(solution)/shard_map/ppermute | solution.py:521
  29.7 0.5 %collective-permute-start.8 = (f32[2,128]{1,0:T(2,128)S(1)}, f32[2,128]{1,0:T(2,128)S(1)}, u32[]{:S(2)}, u32[]{:S(2)}) collective-permute-start(f32[2,128]{1,0:T(2,128)S(1)} %pad_maximum_fusion.1.refs_3_.refs_6_), channel_id=1, source_target_pairs={{0,1},{1,0},{2,3},{3,2},{4,5},{5,4},{6,7},{7,6},{8,9},{9,8},{10,11... | collective-permute-start | bytes 3080 | tf_op jit(solution)/shard_map/ppermute | solution.py:521
  30.2 2.7 %fine_part.5 = (f32[2,512,128]{2,1,0:T(8,128)S(1)}, bf16[4,512,512]{2,1,0:T(8,128)(2,1)S(1)}) custom-call(s32[8,6]{1,0:T(8,128)S(1)} %get-tuple-element.42.refs_0_.refs_1_, bf16[8,512,128]{2,1,0:T(8,128)(2,1)S(1)} %get-tuple-element.61.refs_1_.refs_13_, bf16[27,128,128]{2,1,0:T(8,128)(2,1)S(1)} %get-tuple-element.62.refs_2_, ...), custom_call_target="tpu_custom_call" | custom-call | flops 905969664 | bytes 524288 | tf_op jit(solution)/shard_map/fine_part/pallas_call | solution.py:400
  32.9 0.0 collective-permute-done.10.refs_9_
  32.9 0.0 collective-permute-done.9.refs_8_
  33.0 0.3 collective-permute-done.8.refs_7_
  33.3 0.0 copy-done.1
  33.3 0.0 copy-done.2
  33.3 0.0 copy-done.3
  33.3 3.8 %final.1 = bf16[8,512,128]{2,1,0:T(8,128)(2,1)} custom-call(s32[3,8]{1,0:T(4,128)S(1)} %get-tuple-element.41.refs_0_, s32[8,6]{1,0:T(8,128)S(1)} %get-tuple-element.42.refs_0_.refs_1_, f32[136,128]{1,0:T(8,128)S(1)} %get-tuple-element.57.refs_3_.refs_2_, f32[136,128]{1,0:T(8,128)S(1)} %collective-permute-done.5.refs_3_, ...), custom_call_target="tpu_custom_call" | custom-call | tf_op jit(solution)/shard_map/final/pallas_call | solution.py:528
  (10 shorter events, 0.1 us)
Async XLA Ops:
  0.0 13.9 %copy-start = (bf16[27,128,128]{2,1,0:T(8,128)(2,1)S(1)}, bf16[27,128,128]{2,1,0:T(8,128)(2,1)}, u32[]{:S(2)}) copy-start(bf16[27,128,128]{2,1,0:T(8,128)(2,1)} %refs_7_.1) | copy-start | bytes 2654212
  1.1 1.6 %collective-permute-start = (bf16[33,16,128]{2,1,0:T(8,128)(2,1)S(1)}, bf16[33,16,128]{2,1,0:T(8,128)(2,1)S(1)}, u32[]{:S(2)}, u32[]{:S(2)}) collective-permute-start(bf16[33,16,128]{2,1,0:T(8,128)(2,1)S(1)} %get-tuple-element.43.refs_0_), channel_id=1, source_target_pairs={{0,4},{4,0},{8,12},{12,8},{1,5},{5,1},{9,13},{13,9},{2,6},{6,2},{1... | collective-permute-start | bytes 405512 | tf_op jit(solution)/shard_map/ppermute | solution.py:452
  1.7 8.2 %collective-permute-start.1 = (bf16[32,16,128]{2,1,0:T(8,128)(2,1)S(1)}, bf16[32,16,128]{2,1,0:T(8,128)(2,1)S(1)}, u32[]{:S(2)}, u32[]{:S(2)}) collective-permute-start(bf16[32,16,128]{2,1,0:T(8,128)(2,1)S(1)} %get-tuple-element.48), channel_id=1, source_target_pairs={{4,8},{8,4},{5,9},{9,5},{6,10},{10,6},{7,11},{11,7},{20,24},{24,20... | collective-permute-start | bytes 393224 | tf_op jit(solution)/shard_map/ppermute | solution.py:453
  2.7 7.2 %collective-permute-start.2 = (bf16[2,16,128]{2,1,0:T(8,128)(2,1)S(1)}, bf16[2,16,128]{2,1,0:T(8,128)(2,1)S(1)}, u32[]{:S(2)}, u32[]{:S(2)}) collective-permute-start(bf16[2,16,128]{2,1,0:T(8,128)(2,1)S(1)} %pad_maximum_fusion), channel_id=1, source_target_pairs={{0,8},{4,12},{8,0},{12,4},{1,9},{5,13},{9,1},{13,5},{2,10},{6,14},... | collective-permute-start | bytes 24584 | tf_op jit(solution)/shard_map/ppermute | solution.py:456
  9.9 4.0 %collective-permute-start.3 = (bf16[6,16,128]{2,1,0:T(8,128)(2,1)S(1)}, bf16[6,16,128]{2,1,0:T(8,128)(2,1)S(1)}, u32[]{:S(2)}, u32[]{:S(2)}) collective-permute-start(bf16[6,16,128]{2,1,0:T(8,128)(2,1)S(1)} %get-tuple-element.55), channel_id=1, source_target_pairs={{0,1},{1,0},{2,3},{3,2},{4,5},{5,4},{6,7},{7,6},{8,9},{9,8},{10,11... | collective-permute-start | bytes 73736 | tf_op jit(solution)/shard_map/ppermute | solution.py:480
  12.1 1.8 %collective-permute-start.4 = (bf16[6,16,128]{2,1,0:T(8,128)(2,1)S(1)}, bf16[6,16,128]{2,1,0:T(8,128)(2,1)S(1)}, u32[]{:S(2)}, u32[]{:S(2)}) collective-permute-start(bf16[6,16,128]{2,1,0:T(8,128)(2,1)S(1)} %get-tuple-element.56), channel_id=1, source_target_pairs={{1,2},{2,1},{5,6},{6,5},{9,10},{10,9},{13,14},{14,13},{17,18},{18,... | collective-permute-start | bytes 73736 | tf_op jit(solution)/shard_map/ppermute | solution.py:481
  17.4 5.4 %collective-permute-start.5 = (f32[136,128]{1,0:T(8,128)S(1)}, f32[136,128]{1,0:T(8,128)S(1)}, u32[]{:S(2)}, u32[]{:S(2)}) collective-permute-start(f32[136,128]{1,0:T(8,128)S(1)} %get-tuple-element.58), channel_id=1, source_target_pairs={{0,4},{4,0},{8,12},{12,8},{1,5},{5,1},{9,13},{13,9},{2,6},{6,2},{1... | collective-permute-start | bytes 208904 | tf_op jit(solution)/shard_map/ppermute | solution.py:508
  17.5 5.3 %collective-permute-start.6 = (f32[136,128]{1,0:T(8,128)S(1)}, f32[136,128]{1,0:T(8,128)S(1)}, u32[]{:S(2)}, u32[]{:S(2)}) collective-permute-start(f32[136,128]{1,0:T(8,128)S(1)} %get-tuple-element.59), channel_id=1, source_target_pairs={{0,8},{4,12},{8,0},{12,4},{1,9},{5,13},{9,1},{13,5},{2,10},{6,14},... | collective-permute-start | bytes 208904 | tf_op jit(solution)/shard_map/ppermute | solution.py:508
  18.3 4.8 %collective-permute-start.7 = (f32[136,128]{1,0:T(8,128)S(1)}, f32[136,128]{1,0:T(8,128)S(1)}, u32[]{:S(2)}, u32[]{:S(2)}) collective-permute-start(f32[136,128]{1,0:T(8,128)S(1)} %get-tuple-element.60), channel_id=1, source_target_pairs={{0,12},{4,8},{8,4},{12,0},{1,13},{5,9},{9,5},{13,1},{2,14},{6,10},... | collective-permute-start | bytes 208904 | tf_op jit(solution)/shard_map/ppermute | solution.py:508
  22.8 10.5 %copy-start.1 = (bf16[128,128]{1,0:T(8,128)(2,1)S(1)}, bf16[128,128]{1,0:T(8,128)(2,1)}, u32[]{:S(2)}) copy-start(bf16[128,128]{1,0:T(8,128)(2,1)} %refs_12_.1) | copy-start | bytes 98308
  22.8 10.5 %copy-start.2 = (f32[128]{0:T(128)S(1)}, f32[128]{0:T(128)}, u32[]{:S(2)}) copy-start(f32[128]{0:T(128)} %param.11) | copy-start | bytes 1540
  22.8 10.5 %copy-start.3 = (f32[128]{0:T(128)S(1)}, f32[128]{0:T(128)}, u32[]{:S(2)}) copy-start(f32[128]{0:T(128)} %param.12) | copy-start | bytes 1540
  23.1 9.9 %collective-permute-start.10 = (f32[2,128]{1,0:T(2,128)S(1)}, f32[2,128]{1,0:T(2,128)S(1)}, u32[]{:S(2)}, u32[]{:S(2)}) collective-permute-start(f32[2,128]{1,0:T(2,128)S(1)} %pad_maximum_fusion.1.refs_3_.refs_6_), channel_id=1, source_target_pairs={{0,3},{1,2},{2,1},{3,0},{4,7},{5,6},{6,5},{7,4},{8,11},{9,10},{10,... | collective-permute-start | bytes 3080 | tf_op jit(solution)/shard_map/ppermute | solution.py:521
  27.2 5.8 %collective-permute-start.9 = (f32[2,128]{1,0:T(2,128)S(1)}, f32[2,128]{1,0:T(2,128)S(1)}, u32[]{:S(2)}, u32[]{:S(2)}) collective-permute-start(f32[2,128]{1,0:T(2,128)S(1)} %pad_maximum_fusion.1.refs_3_.refs_6_), channel_id=1, source_target_pairs={{0,2},{1,3},{2,0},{3,1},{4,6},{5,7},{6,4},{7,5},{8,10},{9,11},{10,... | collective-permute-start | bytes 3080 | tf_op jit(solution)/shard_map/ppermute | solution.py:521
  29.7 3.6 %collective-permute-start.8 = (f32[2,128]{1,0:T(2,128)S(1)}, f32[2,128]{1,0:T(2,128)S(1)}, u32[]{:S(2)}, u32[]{:S(2)}) collective-permute-start(f32[2,128]{1,0:T(2,128)S(1)} %pad_maximum_fusion.1.refs_3_.refs_6_), channel_id=1, source_target_pairs={{0,1},{1,0},{2,3},{3,2},{4,5},{5,4},{6,7},{7,6},{8,9},{9,8},{10,11... | collective-permute-start | bytes 3080 | tf_op jit(solution)/shard_map/ppermute | solution.py:521

commit v3 on v2

--- a/solution.py
+++ b/solution.py
@@ -7,10 +7,13 @@
 from jax.experimental.pallas import tpu as pltpu
 from jax.sharding import PartitionSpec as P
 
+
 G = 32
 FB = 8
 EDGE = FB // 2
 MOST = 2
+TAIL = 16
+SENT = jnp.bfloat16
 EPS = 1e-05
 F32 = jnp.float32
 BF16 = jnp.bfloat16
@@ -85,7 +88,7 @@
     moves = [
         (coords, coords_out),
         (inp.at[xa], send_a.at[pl.ds(0, dy)]),
-        (inp.at[dx - 1 - xa], send_b),
+        (inp.at[dx - 1 - xa], send_b.at[pl.ds(0, dy)]),
         (inp.at[:, ya], row_a),
         (inp.at[:, dy - 1 - ya], row_b),
         (links, links_out),
@@ -95,26 +98,38 @@
         copy.start()
     note[...] = jnp.zeros_like(note)
     copies[0].wait()
-    note[pl.ds(0, coords.shape[0]), pl.ds(0, coords.shape[1])] = coords_out[...]
+    note[pl.ds(0, coords.shape[0]), pl.ds(0, coords.shape[1])] = coords_out[...] + 1
     send_a[dy] = note[...].astype(F32).astype(BF16)
+    send_b[dy] = send_a[dy]
+    send_b[dy + 1] = jnp.zeros_like(send_a[dy])
     for copy in copies[1:]:
         copy.wait()
 
 
-def line_kernel(x_first, x_second, row_a, row_b, line_a, line_b):
-    dx, dy = row_a.shape[0], x_second.shape[0]
+def relay_kernel(x_first, _, send_b):
+    send_b[send_b.shape[0] - 1] = x_first[x_first.shape[0] - 1]
+
+
+def inside(xor, slabs):
+    slab = lax.axis_index("slab")
+    return jnp.logical_or(not xor, jnp.logical_and(slab > 0, slab < slabs - 1))
+
+
+def line_kernel(slabs, xor, x_first, x_second, row_a, row_b, line_a, line_b):
+    dx, dy = row_a.shape[0], x_first.shape[0] - 1
+    has = inside(xor, slabs)
     ya = parity("sub", dy)
     for place, row, line in ((ya, row_a, line_a), (dy - 1 - ya, row_b, line_b)):
         line[0] = x_first[place]
         line[pl.ds(1, dx)] = row[...]
-        line[dx + 1] = x_second[place]
+        line[dx + 1] = jnp.where(has, x_second[place], jnp.zeros_like(x_second[place]))
 
 
 def fine_kernel(first, count, role, *refs):
     loads = []
     if role == "load":
-        links, fine_from, weight_from, inp = refs[:4]
-        out, fine, weight, padded, even, odd, sems = refs[4:]
+        links, fine_from, weight_from, _, inp = refs[:5]
+        out, fine, weight, padded, folded, even, odd, sems = refs[5:]
         dx, dy = inp.shape[:2]
         moves = [
             (fine_from, fine),
@@ -124,10 +139,9 @@
         loads = [pltpu.make_async_copy(a, b, sems.at[i]) for i, (a, b) in enumerate(moves)]
         for load in loads:
             load.start()
+        for y in (0, dy + 1):
+            padded[:, y] = jnp.zeros((dx + 2,) + padded.shape[2:], BF16)
         loads[0].wait()
-    elif role == "fold":
-        links, fine, weight, _, out, folded, even, odd = refs
-        fold_weights(weight, folded)
     else:
         links, fine, weight, _, out, even, odd = refs
     total, _, channels = fine.shape
@@ -178,41 +192,70 @@
             jnp.concatenate(taken, axis=1), wide_weight(weight), preferred_element_type=F32
         )
         out[slot] = shifted_sum(sums, FB, channels)
+    if role == "load":
+        fold_weights(weight, folded)
     for load in loads[2:]:
         load.wait()
 
 
-def coarse_kernel(sources, xor, cells_shape, total_blocks, *refs):
-    own, far = refs[:2]
-    _, x_first, x_second, y_first, y_second, weight = refs[2:8]
-    outs = refs[8:-5]
-    padded, conv, notes, wanted, sems = refs[-5:]
+def choose(notes, y_cubes):
+    rows = [jnp.concatenate([note[k : k + 1] for note in notes], axis=0) for k in range(3)]
+    lane = lax.broadcasted_iota(jnp.int32, rows[0].shape, 1)
+    slab = lax.axis_index("slab").astype(F32)
+    low = (lax.axis_index("sub") * y_cubes).astype(F32)
+    blank = rows[0] != slab + 1.0
+    hit = jnp.where(blank, 0.0, 1.0)
+    upto = hit
+    for step in (1, 2, 4, 8, 16, 32, 64):
+        upto = upto + jnp.where(lane >= step, pltpu.roll(upto, step, 1), 0.0)
+    result = jnp.zeros(rows[0].shape, F32)
+    for slot in range(MOST):
+        here = hit * jnp.where(upto == slot + 1.0, 1.0, 0.0)
+        for k, cube in enumerate((rows[1] - 1.0 - low, rows[2] - 1.0)):
+            first = jnp.sum(here * cube, axis=1, keepdims=True) * EDGE
+            result = jnp.where(lane == 2 * slot + k, first, result)
+    return result.astype(jnp.int32)
+
+
+def thirds(value):
+    parts = []
+    for _ in range(3):
+        part = value.astype(BF16)
+        parts.append(part)
+        value = value - part.astype(F32)
+    return parts
+
+
+def whole_of(rows):
+    return jnp.sum(rows.astype(F32), axis=0, keepdims=True)
+
+
+def coarse_kernel(slabs, xor, cells_shape, *refs):
+    _, own, far, x_first, x_second, weight, _ = refs[:7]
+    padded, conv, stats, picks, sems = refs[7:]
     dx, dy, dz = cells_shape
-    asked = [own[dy], x_first[dy], far[0], far[1]] if xor else [far[s] for s in range(sources)]
-    for s, note in enumerate(asked):
-        notes[s] = note.astype(F32).astype(jnp.int32)
-    noted = pltpu.make_async_copy(notes, wanted, sems.at[2])
-    noted.start()
+    sources = slabs
+    asked = [own[dy], x_first[dy], far[dy + 1], far[dy]] if xor else [far[s] for s in range(sources)]
     channels = padded.shape[-1]
-    slab = lax.axis_index("slab")
-    sub = lax.axis_index("sub")
     rows = pl.ds(1, dy)
-    xa = jnp.where(lax.rem(slab, 2) == 0, dx + 1, 0)
+    xa = jnp.where(lax.rem(lax.axis_index("slab"), 2) == 0, dx + 1, 0)
     xb = dx + 1 - xa
-    ya = jnp.where(lax.rem(sub, 2) == 0, dy + 1, 0)
-    yb = dy + 1 - ya
-    moves = [(x_first.at[pl.ds(0, dy)], padded.at[xa, rows]), (x_second, padded.at[xb, rows])]
-    copies = [pltpu.make_async_copy(a, b, sems.at[i]) for i, (a, b) in enumerate(moves)]
-    for copy in copies:
-        copy.start()
-    for got, place in ((y_first, ya), (y_second, yb)):
-        padded[xa, place] = got[0]
-        for x in range(dx):
-            padded[1 + x, place] = got[1 + x]
-        padded[xb, place] = got[dx + 1]
-    for copy in copies:
-        copy.wait()
-    total = jnp.zeros((8, channels), F32)
+    has = inside(xor, slabs)
+    first = pltpu.make_async_copy(x_first.at[pl.ds(0, dy)], padded.at[xa, rows], sems.at[0])
+    first.start()
+
+    @pl.when(has)
+    def _():
+        second = pltpu.make_async_copy(x_second.at[pl.ds(0, dy)], padded.at[xb, rows], sems.at[1])
+        second.start()
+        second.wait()
+
+    @pl.when(jnp.logical_not(has))
+    def _():
+        padded[xb, rows] = jnp.zeros((dy,) + padded.shape[2:], BF16)
+
+    first.wait()
+    means, squares = [], []
     for x in range(dx):
         taken = [
             padded[x + a, pl.ds(b, dy)].reshape(dy * dz, channels)
@@ -222,36 +265,70 @@
         sums = jnp.dot(
             jnp.concatenate(taken, axis=1), wide_weight(weight), preferred_element_type=F32
         )
-        value = shifted_sum(sums, dz, channels)
-        conv[x] = value.reshape(dy, dz, channels)
-        total = total + jnp.sum(value.reshape(-1, 8, channels), axis=0)
-    mean = jnp.sum(total, axis=0, keepdims=True) / (dx * dy * dz)
-    square = jnp.zeros((8, channels), F32)
-    for x in range(dx):
-        off = conv[x].reshape(-1, 8, channels) - mean[None]
-        square = square + jnp.sum(off * off, axis=0)
-    square = jnp.sum(square, axis=0, keepdims=True)
-    noted.wait()
+        value = shifted_sum(sums, dz, channels).reshape(dy, dz, channels)
+        conv[x] = value
+        if x == 0:
+            picks[...] = choose([note.astype(F32) for note in asked], dy // EDGE)
+        inner = value[1 : dy - 1].reshape(-1, 8, channels)
+        mean = jnp.sum(jnp.sum(inner, axis=0), axis=0, keepdims=True) / ((dy - 2) * dz)
+        off = conv[x, pl.ds(1, dy - 2)].reshape(-1, 8, channels) - mean[None]
+        means.append(mean)
+        squares.append(jnp.sum(jnp.sum(off * off, axis=0), axis=0, keepdims=True))
+    mean, square = merge(means, squares, float((dy - 2) * dz))
+    stats[0:1, :] = mean
+    stats[1:2, :] = square
+
+
+def edge_kernel(sources, xor, *refs):
+    picks, conv_from, stats, y_first, y_second, weight = refs[:6]
+    outs = refs[6:-3]
+    conv, rim, cube = refs[-3:]
+    dx, dy, dz, channels = conv.shape
+    slab = lax.axis_index("slab")
+    sub = lax.axis_index("sub")
+    xa = jnp.where(lax.rem(slab, 2) == 0, dx + 1, 0)
+    xb = dx + 1 - xa
+    side = jnp.where(lax.rem(sub, 2) == 0, 1, 0)
+    for got, place in ((y_first, side), (y_second, 1 - side)):
+        rim[place, xa] = got[0]
+        rim[place, pl.ds(1, dx)] = got[pl.ds(1, dx)]
+        rim[place, xb] = got[dx + 1]
+    edges = []
+    for place, row, b in ((0, 0, 0), (1, dy - 1, 2)):
+        taken = [rim[place, pl.ds(a, dx)].reshape(dx * dz, channels) for a in range(3)]
+        taps = jnp.concatenate(
+            [
+                jnp.concatenate([weight[9 * a + 3 * b + c] for c in range(3)], axis=1)
+                for a in range(3)
+            ],
+            axis=0,
+        )
+        sums = jnp.dot(jnp.concatenate(taken, axis=1), taps, preferred_element_type=F32)
+        value = conv_from[:, row] + shifted_sum(sums, dz, channels).reshape(dx, dz, channels)
+        conv[:, row] = value
+        edges.append(value.reshape(-1, 8, channels))
+    count = 2 * dx * dz
+    mean = sum(jnp.sum(jnp.sum(e, axis=0), axis=0, keepdims=True) for e in edges) / count
+    square = sum(
+        jnp.sum(jnp.sum((e - mean[None]) ** 2, axis=0), axis=0, keepdims=True) for e in edges
+    )
+    cells = dx * dy * dz
+    apart = mean - stats[0:1, :]
+    square = square + stats[1:2, :] + apart * apart * (count * (cells - count) / cells)
+    mean = stats[0:1, :] + apart * (count / cells)
+    tail = jnp.concatenate(thirds(mean) + thirds(square), axis=0).astype(F32)
+    tail = jnp.concatenate([tail, jnp.zeros((TAIL - 6, channels), F32)], axis=0).astype(SENT)
     for s in range(sources):
-        seen = jnp.int32(0)
-        where_y = [jnp.int32(0)] * MOST
-        where_z = [jnp.int32(0)] * MOST
-        for n in range(total_blocks):
-            hit = wanted[s, 0, n] == slab
-            y = wanted[s, 1, n] - sub * (dy // EDGE)
-            for slot in range(MOST):
-                here = jnp.logical_and(hit, seen == slot)
-                where_y[slot] = jnp.where(here, y, where_y[slot])
-                where_z[slot] = jnp.where(here, wanted[s, 2, n], where_z[slot])
-            seen = seen + hit.astype(jnp.int32)
         out = outs[s] if xor else outs[0].at[s]
         for slot in range(MOST):
+            first_y = picks[s, 2 * slot]
+            first_z = picks[s, 2 * slot + 1]
             for x in range(EDGE):
                 for y in range(EDGE):
-                    piece = conv[x, EDGE * where_y[slot] + y, pl.ds(EDGE * where_z[slot], EDGE), :]
-                    out[pl.ds(slot * EDGE**3 + (x * EDGE + y) * EDGE, EDGE), :] = piece
-        out[pl.ds(MOST * EDGE**3, 1), :] = mean
-        out[pl.ds(MOST * EDGE**3 + 1, 1), :] = square
+                    piece = conv[x, first_y + y, pl.ds(first_z, EDGE), :]
+                    cube[pl.ds(slot * EDGE**3 + (x * EDGE + y) * EDGE, EDGE), :] = piece
+        out[pl.ds(0, MOST * EDGE**3), :] = (cube[...] - mean).astype(SENT)
+        out[pl.ds(MOST * EDGE**3, TAIL), :] = tail
 
 
 def group_sum(value, size):
@@ -283,13 +360,12 @@
     total, _, channels = fine.shape
     slab = lax.axis_index("slab")
     volume = EDGE**3
-    for i, cube in enumerate(cubes):
+    if not xor:
         for slot in range(MOST):
-            if xor:
-                held[MOST * i + slot] = cube[pl.ds(slot * volume, volume), :]
-            else:
-                for s in range(cube.shape[0]):
-                    held[MOST * s + slot] = cube[s, pl.ds(slot * volume, volume), :]
+            for s in range(cubes[0].shape[0]):
+                held[MOST * s + slot] = cubes[0][s, pl.ds(slot * volume, volume), :].astype(F32) + whole_of(
+                    cubes[0][s, pl.ds(MOST * volume, 3), :]
+                )
     size = channels // G
     mean, square = merge(
         [s[0:1, :] for s in stats], [s[1:2, :] for s in stats], float(cells)
@@ -298,16 +374,32 @@
     group_mean = group_sum(mean, size) / size
     off = mean - group_mean
     group_var = group_sum(square + cells * off * off, size) / (cells * size)
-    scale = lax.rsqrt(group_var + EPS)
+    scale = lax.rsqrt(group_var + EPS) * gain[...]
+
+    def act(value, n):
+        normed = (value - group_mean) * scale + bias[...]
+        rows = pl.ds(pl.multiple_of(n * volume, volume), volume)
+        acted[rows, :] = (normed / (1.0 + jnp.exp(-normed))).astype(BF16)
+
+    seen = [[jnp.int32(0)] * MOST for _ in cubes]
     for n in range(total):
         holder = coords[0, n]
         rank = jnp.int32(0)
         for m in range(n):
             rank = rank + (coords[0, m] == holder).astype(jnp.int32)
-        source = jnp.bitwise_xor(holder, slab) if xor else holder
-        value = held[source * MOST + rank]
-        normed = (value - group_mean) * scale * gain[...] + bias[...]
-        acted[pl.ds(n * volume, volume), :] = (normed / (1.0 + jnp.exp(-normed))).astype(BF16)
+        if xor:
+            source = jnp.bitwise_xor(holder, slab)
+            for s in range(len(cubes)):
+                for slot in range(MOST):
+                    here = jnp.logical_and(source == s, rank == slot)
+                    seen[s][slot] = jnp.where(here, n, seen[s][slot])
+        else:
+            act(held[holder * MOST + rank], n)
+    if xor:
+        for s, cube in enumerate(cubes):
+            base = whole_of(cube[pl.ds(MOST * volume, TAIL), :][0:3])
+            for slot in range(MOST):
+                act(cube[pl.ds(slot * volume, volume), :].astype(F32) + base, seen[s][slot])
     rounded = jnp.dot(acted[...], lift[...], preferred_element_type=F32).astype(BF16).astype(F32)
     rows = total * volume
     twice[pl.ds(0, rows, stride=2), :] = rounded
@@ -336,39 +428,46 @@
             frame[2, n, i + 1] = jnp.where(
                 place >= flat - EDGE, after, pltpu.roll(here, flat - EDGE, 0)
             ).astype(BF16)
-    level = lax.broadcasted_iota(jnp.int32, (rows, channels), 0) % EDGE
-    for p in range(2):
-        for q in range(2):
-            taken = [
-                frame[q + b, :, pl.ds(p + a, EDGE)].reshape(rows, channels)
-                for a in range(2)
-                for b in range(2)
-            ]
-            sums = jnp.dot(
-                jnp.concatenate(taken, axis=1), folded[2 * p + q], preferred_element_type=F32
-            )
-            below = pltpu.roll(sums[:, channels : 2 * channels], 1, 0)
-            above = pltpu.roll(sums[:, 3 * channels :], rows - 1, 0)
-            even = sums[:, :channels] + jnp.where(level == 0, 0.0, below)
-            odd = sums[:, 2 * channels : 3 * channels] + jnp.where(level == EDGE - 1, 0.0, above)
-            spread[2 * p + q, pl.ds(0, rows, stride=2), :] = even
-            spread[2 * p + q, pl.ds(1, rows, stride=2), :] = odd
+    whole = [piece.at[n] for piece in pieces for n in range(piece.shape[0])]
+    step = total // 2
+    band = step * volume
+    level = lax.broadcasted_iota(jnp.int32, (band, channels), 0) % EDGE
     copies = []
-    whole = [piece.at[n] for piece in pieces for n in range(piece.shape[0])]
-    for n, part in enumerate(whole):
-        for i in range(FB):
-            for j in range(0, FB, 2):
-                cell = pl.ds(((n * EDGE + i // 2) * EDGE + j // 2) * FB, FB)
-                pair = pl.ds((i * FB + j) * FB, 2 * FB)
-                up = twice[cell, :]
-                raised = jnp.concatenate([up, up], axis=0)
-                own = (fine[n, pair, :].astype(F32) + raised).astype(BF16).astype(F32)
-                conv = jnp.concatenate(
-                    [spread[2 * (i % 2), cell, :], spread[2 * (i % 2) + 1, cell, :]], axis=0
+    for first in range(0, total, step):
+        for p in range(2):
+            for q in range(2):
+                taken = [
+                    frame[q + b, pl.ds(first, step), pl.ds(p + a, EDGE)].reshape(band, channels)
+                    for a in range(2)
+                    for b in range(2)
+                ]
+                sums = jnp.dot(
+                    jnp.concatenate(taken, axis=1), folded[2 * p + q], preferred_element_type=F32
                 )
-                out[n, pair, :] = (own + part[pair, :] + conv).astype(BF16)
-        copies.append(pltpu.make_async_copy(out.at[n], out_to.at[n], sems.at[n]))
-        copies[-1].start()
+                below = pltpu.roll(sums[:, channels : 2 * channels], 1, 0)
+                above = pltpu.roll(sums[:, 3 * channels :], band - 1, 0)
+                even = sums[:, :channels] + jnp.where(level == 0, 0.0, below)
+                odd = sums[:, 2 * channels : 3 * channels] + jnp.where(
+                    level == EDGE - 1, 0.0, above
+                )
+                start = 2 * first * volume
+                spread[2 * p + q, pl.ds(start, band, stride=2), :] = even
+                spread[2 * p + q, pl.ds(start + 1, band, stride=2), :] = odd
+            for n in range(first, first + step):
+                for i in range(p, FB, 2):
+                    for j in range(0, FB, 2):
+                        cell = pl.ds(((n * EDGE + i // 2) * EDGE + j // 2) * FB, FB)
+                        pair = pl.ds((i * FB + j) * FB, 2 * FB)
+                        up = twice[cell, :]
+                        raised = jnp.concatenate([up, up], axis=0)
+                        own = (fine[n, pair, :].astype(F32) + raised).astype(BF16).astype(F32)
+                        conv = jnp.concatenate(
+                            [spread[2 * p, cell, :], spread[2 * p + 1, cell, :]], axis=0
+                        )
+                        out[n, pair, :] = (own + whole[n][pair, :] + conv).astype(BF16)
+                if p:
+                    copies.append(pltpu.make_async_copy(out.at[n], out_to.at[n], sems.at[n]))
+                    copies[-1].start()
     for copy in copies:
         copy.wait()
 
@@ -382,21 +481,22 @@
     return pltpu.CompilerParams(vmem_limit_bytes=mib * 2**20)
 
 
-def fine_part(links, fine, weight, after, first, count, role):
-    total, cells, channels = fine.shape
+def fine_part(links, fine, weight, after, first, count, role, coarse_in=None):
+    _, cells, channels = fine.shape
     shapes = [jax.ShapeDtypeStruct((count, cells, channels), F32)]
-    specs, sems = [SMEM, VMEM, VMEM, HBM], []
-    if role == "fold":
-        shapes.append(jax.ShapeDtypeStruct((4, 4 * channels, 4 * channels), BF16))
+    specs, sems, inputs = [SMEM, VMEM, VMEM, HBM], [], (links, fine, weight, after)
     if role == "load":
-        dx, dy, dz, _ = after.shape
+        dx, dy, dz, _ = coarse_in.shape
         extra = [fine.shape, weight.shape, (dx + 2, dy + 2, dz, channels)]
+        extra.append((4, 4 * channels, 4 * channels))
         shapes += [jax.ShapeDtypeStruct(shape, BF16) for shape in extra]
-        specs = [SMEM] + [pl.BlockSpec(memory_space=pltpu.HBM)] * 3
-        sems = [pltpu.SemaphoreType.DMA((len(extra),))]
-        fine, weight, after = (
-            pltpu.with_memory_space_constraint(x, pltpu.HBM) for x in (fine, weight, after)
+        hbm = pl.BlockSpec(memory_space=pltpu.HBM)
+        specs = [SMEM, hbm, hbm, HBM, hbm]
+        sems = [pltpu.SemaphoreType.DMA((3,))]
+        fine, weight, coarse_in = (
+            pltpu.with_memory_space_constraint(x, pltpu.HBM) for x in (fine, weight, coarse_in)
         )
+        inputs = (links, fine, weight, after, coarse_in)
     return pl.pallas_call(
         functools.partial(fine_kernel, first, count, role),
         out_shape=shapes,
@@ -414,7 +514,7 @@
             transcendentals=0,
         ),
         name="fine_part",
-    )(links, fine, weight, after)
+    )(*inputs)
 
 
 def body(
@@ -431,13 +531,13 @@
     dx, dy, dz, channels = coarse_in.shape
     slabs, subs = lax.axis_size("slab"), lax.axis_size("sub")
     total = block_coords.shape[0]
-    xor = slabs == 4
+    xor = slabs == 4 and total == MOST * slabs
     coords = block_coords.T
     send_a, send_b, row_a, row_b, coords, links = pl.pallas_call(
         send_kernel,
         out_shape=[
             jax.ShapeDtypeStruct((dy + 1, dz, channels), BF16),
-            jax.ShapeDtypeStruct((dy, dz, channels), BF16),
+            jax.ShapeDtypeStruct((dy + 2, dz, channels), BF16),
             jax.ShapeDtypeStruct((dx, dz, channels), BF16),
             jax.ShapeDtypeStruct((dx, dz, channels), BF16),
             jax.ShapeDtypeStruct(coords.shape, jnp.int32),
@@ -450,27 +550,38 @@
         name="send",
     )(*(pltpu.with_memory_space_constraint(x, pltpu.HBM) for x in (coarse_in, coords, neighbours)))
     x_first = lax.ppermute(send_a, "slab", pairs(slabs, 0))
-    x_second = lax.ppermute(send_b, "slab", pairs(slabs, 1))
     if xor:
-        both = jnp.stack([send_a[dy], x_first[dy]])
-        far = lax.ppermute(both, "slab", xor_links(slabs, 2))
+        send_b = pl.pallas_call(
+            relay_kernel,
+            out_shape=jax.ShapeDtypeStruct(send_b.shape, BF16),
+            in_specs=[VMEM] * 2,
+            out_specs=VMEM,
+            input_output_aliases={1: 0},
+            compiler_params=limit(4),
+            name="relay",
+        )(x_first, send_b)
+        far = x_second = lax.ppermute(send_b, "slab", xor_links(slabs, 3))
     else:
+        x_second = lax.ppermute(send_b, "slab", pairs(slabs, 1))
         far = lax.all_gather(send_a[dy], "slab", axis=0)
-    shares = [0, total // 4, total * 3 // 4, total]
+    shares = [0, total * 3 // 8, total * 3 // 4, total]
     pieces = []
 
     def fill(index, after, waiting, role="plain"):
         begin = shares[index]
-        made = fine_part(links, fine, weight, after, begin, shares[index + 1] - begin, role)
+        count = shares[index + 1] - begin
+        made = fine_part(links, fine, weight, after, begin, count, role, coarse_in)
         made, waiting = lax.optimization_barrier((made, waiting))
         pieces.append(made[0])
         return made[1:], waiting
 
     fine, weight = fine_input, fine_weight
-    made, (x_first, x_second, far) = fill(0, coarse_in, (x_first, x_second, far), "load")
-    fine, weight, padded = made
+    made, x_second = fill(0, send_b, x_second, "load")
+    if xor:
+        far = x_second
+    fine, weight, padded, folded = made
     line_a, line_b = pl.pallas_call(
-        line_kernel,
+        functools.partial(line_kernel, slabs, xor),
         out_shape=[jax.ShapeDtypeStruct((dx + 2, dz, channels), BF16)] * 2,
         in_specs=[VMEM] * 4,
         out_specs=[VMEM] * 2,
@@ -480,26 +591,47 @@
     y_first = lax.ppermute(line_a, "sub", pairs(subs, 0))
     y_second = lax.ppermute(line_b, "sub", pairs(subs, 1))
 
-    piece = (MOST * EDGE**3 + 8, channels)
+    padded, conv, stats, picks = pl.pallas_call(
+        functools.partial(coarse_kernel, slabs, xor, (dx, dy, dz)),
+        out_shape=[
+            jax.ShapeDtypeStruct(padded.shape, BF16),
+            jax.ShapeDtypeStruct(coarse_in.shape, F32),
+            jax.ShapeDtypeStruct((8, channels), F32),
+            jax.ShapeDtypeStruct((slabs, channels), jnp.int32),
+        ],
+        in_specs=[VMEM] * 6 + [HBM],
+        out_specs=[VMEM] * 4,
+        scratch_shapes=[pltpu.SemaphoreType.DMA((2,))],
+        input_output_aliases={0: 0},
+        compiler_params=limit(12),
+        cost_estimate=pl.CostEstimate(
+            flops=2 * 27 * dx * dy * dz * channels * channels,
+            bytes_accessed=4 * dx * dy * dz * channels,
+            transcendentals=0,
+        ),
+        name="coarse",
+    )(padded, send_a, far, x_first, x_second, coarse_weight, line_a)
+    (conv, stats), (y_first, y_second) = lax.optimization_barrier(
+        ((conv, stats), (y_first, y_second))
+    )
+    piece = (MOST * EDGE**3 + TAIL, channels)
     if xor:
-        shapes = [jax.ShapeDtypeStruct(piece, F32)] * slabs
+        shapes = [jax.ShapeDtypeStruct(piece, SENT)] * slabs
     else:
-        shapes = [jax.ShapeDtypeStruct((slabs,) + piece, F32)]
+        shapes = [jax.ShapeDtypeStruct((slabs,) + piece, SENT)]
     results = pl.pallas_call(
-        functools.partial(coarse_kernel, slabs, xor, (dx, dy, dz), total),
-        out_shape=shapes + [jax.ShapeDtypeStruct(padded.shape, BF16)],
-        in_specs=[VMEM] * 8,
+        functools.partial(edge_kernel, slabs, xor),
+        out_shape=shapes + [jax.ShapeDtypeStruct(conv.shape, F32)],
+        in_specs=[SMEM] + [VMEM] * 5,
         out_specs=[VMEM] * (len(shapes) + 1),
         scratch_shapes=[
-            pltpu.VMEM((dx, dy, dz, channels), F32),
-            pltpu.VMEM((slabs, dz, channels), jnp.int32),
-            pltpu.SMEM((slabs, dz, channels), jnp.int32),
-            pltpu.SemaphoreType.DMA((3,)),
+            pltpu.VMEM((2, dx + 2, dz, channels), BF16),
+            pltpu.VMEM((MOST * EDGE**3, channels), F32),
         ],
-        input_output_aliases={2: len(shapes)},
-        compiler_params=limit(12),
-        name="coarse",
-    )(send_a, far, padded, x_first, x_second, y_first, y_second, coarse_weight)
+        input_output_aliases={1: len(shapes)},
+        compiler_params=limit(8),
+        name="edge",
+    )(picks, conv, stats, y_first, y_second, coarse_weight)
     sent = results[:-1]
     cells = dx * dy * dz
     row = MOST * EDGE**3
@@ -508,12 +640,12 @@
             lax.ppermute(sent[distance], "slab", xor_links(slabs, distance))
             for distance in range(1, slabs)
         ]
-        parts = [r[row : row + 2] for r in replies]
+        parts = [r[row : row + 6] for r in replies]
     else:
         replies = [lax.all_to_all(sent[0], "slab", split_axis=0, concat_axis=0, tiled=True)]
-        parts = [replies[0][s, row : row + 2] for s in range(slabs)]
+        parts = [replies[0][s, row : row + 6] for s in range(slabs)]
     _, parts = fill(1, sent[0], parts)
-    mean, square = merge([p[0:1] for p in parts], [p[1:2] for p in parts], float(cells))
+    mean, square = merge([whole_of(p[0:3]) for p in parts], [whole_of(p[3:6]) for p in parts], float(cells))
     cells = cells * slabs
     merged = jnp.concatenate([mean, square])
     if subs == 4:
@@ -522,7 +654,7 @@
         ]
     else:
         lines = list(lax.all_gather(merged, "sub", axis=0))
-    (folded,), lines = fill(2, merged, lines, "fold")
+    _, lines = fill(2, merged, lines)
 
     volume = EDGE**3
     return pl.pallas_call(

time: 37.2 us -> 35.2 us (0.946)
  starting transfers between devices: 16.7 us -> 14.3 us
    ppermute x2 -> x1, starting transfers between devices: 4.21 us -> 2.62 us  [body(): far = x_second = lax.ppermute(send_b, 'slab', xor_links(slabs, 3))]
    ppermute x1, waiting for transfers between devices: 1.15 us -> 0.01 us  [body(): y_first = lax.ppermute(line_a, 'sub', pairs(subs, 0))]
    ppermute x1, waiting for transfers between devices: 0.32 us -> 0.99 us  [body(): x_first = lax.ppermute(send_a, 'slab', pairs(slabs, 0))]
    ppermute x3, waiting for transfers between devices: 0.34 us -> 1.01 us  [body(): lax.ppermute(merged, 'sub', xor_links(subs, distance))]
    ppermute x1, starting transfers between devices: 2.23 us -> 1.64 us  [body(): y_first = lax.ppermute(line_a, 'sub', pairs(subs, 0))]
    pallas_call x2 -> x4, Pallas kernels: 3.53 us -> 4 us  [the longest x1 3.1 us: body(): pl.pallas_call(functools.partial(coarse_kernel, slabs, xor, (dx, dy, dz))...]
  transfers between devices with their start and end apart: 11 -> 10, of which waited for: 4 -> 2; matrix products, arithmetic and copies ran while one was open for 0% -> 0% of each run, Pallas kernels for 26% -> 37%
where the time goes in v3:
time: 35.2 us; the launch traced here: 35 us
  Pallas kernels  18.4 us (52%)
  starting transfers between devices  14.3 us (41%)
  waiting for transfers between devices  2.06 us (6%)
    pallas_call x3, Pallas kernels, fine_part(): pl.pallas_call(functools.partial(fine_kernel, first, count, role), out_sh...  9.76 us
    ppermute x3, starting transfers between devices, body(): lax.ppermute(merged, 'sub', xor_links(subs, distance))  6.88 us
    pallas_call x1, Pallas kernels, body(): pl.pallas_call(functools.partial(final_kernel, len(replies), len(lines),...  3.55 us
    pallas_call x1, Pallas kernels, body(): pl.pallas_call(functools.partial(coarse_kernel, slabs, xor, (dx, dy, dz))...  3.1 us
    ppermute x1, starting transfers between devices, body(): far = x_second = lax.ppermute(send_b, 'slab', xor_links(slabs, 3))  2.62 us
    ppermute x3, starting transfers between devices, body(): lax.ppermute(sent[distance], 'slab', xor_links(slabs, distance))  1.93 us
    ppermute x1, starting transfers between devices, body(): y_first = lax.ppermute(line_a, 'sub', pairs(subs, 0))  1.64 us
    pallas_call x1, Pallas kernels, body(): pl.pallas_call(send_kernel, out_shape=[jax.ShapeDtypeStruct((dy + 1, dz,...  1.04 us
  transfers between devices with their start and end apart: 10, of which 2 were waited for; matrix products, arithmetic and copies ran while one was open for 0% of the time, Pallas kernels for 37%

profile of v3, /device:TPU:0, one launch (start us, length us, event | category | flops | bytes accessed | tf_op | source)
XLA Modules:
  0.0 35.0 jit_solution(9886494022623951207)
XLA Ops:
  0.0 1.0 %send.1 = (bf16[33,16,128]{2,1,0:T(8,128)(2,1)S(1)}, bf16[34,16,128]{2,1,0:T(8,128)(2,1)S(1)}, bf16[4,16,128]{2,1,0:T(8,128)(2,1)S(1)}, bf16[4,16,128]{2,1,0:T(8...) custom-call(bf16[4,32,16,128]{3,2,1,0:T(8,128)(2,1)} %refs_4_.1, s32[3,8]{1,0:T(4,128)} %bitcast.43, s32[8,6]{1,0:T(8,128)} %links.1), custom_call_target="tpu_custom_call" | custom-call | tf_op jit(solution)/shard_map/send/pallas_call | solution.py:536
  1.0 0.6 %collective-permute-start = (bf16[33,16,128]{2,1,0:T(8,128)(2,1)S(1)}, bf16[33,16,128]{2,1,0:T(8,128)(2,1)S(1)}, u32[]{:S(2)}, u32[]{:S(2)}) collective-permute-start(bf16[33,16,128]{2,1,0:T(8,128)(2,1)S(1)} %get-tuple-element.47.refs_1_), channel_id=1, source_target_pairs={{0,4},{4,0},{8,12},{12,8},{1,5},{5,1},{9,13},{13,9},{2,6},{6,2},{1... | collective-permute-start | bytes 405512 | tf_op jit(solution)/shard_map/ppermute | solution.py:552
  1.6 1.0 %collective-permute-done.x_first.refs_3_ = bf16[33,16,128]{2,1,0:T(8,128)(2,1)S(1)} collective-permute-done((bf16[33,16,128]{2,1,0:T(8,128)(2,1)S(1)}, bf16[33,16,128]{2,1,0:T(8,128)(2,1)S(1)}, u32[]{:S(2)}, u32[]{:S(2)}) %collective-permute-start) | collective-permute-done | bytes 135200 | tf_op jit(solution)/shard_map/ppermute | solution.py:552
  2.6 2.6 %collective-permute-start.1 = (bf16[34,16,128]{2,1,0:T(8,128)(2,1)S(1)}, bf16[34,16,128]{2,1,0:T(8,128)(2,1)S(1)}, u32[]{:S(2)}, u32[]{:S(2)}) collective-permute-start(bf16[34,16,128]{2,1,0:T(8,128)(2,1)S(1)} %relay.1.refs_3_), channel_id=1, source_target_pairs={{0,12},{4,8},{8,4},{12,0},{1,13},{5,9},{9,5},{13,1},{2,14},{6,10},... | collective-permute-start | bytes 417800 | tf_op jit(solution)/shard_map/ppermute | solution.py:563
  5.2 0.0 copy-start
  5.2 5.0 %fine_part.3 = (f32[3,512,128]{2,1,0:T(8,128)S(1)}, bf16[8,512,128]{2,1,0:T(8,128)(2,1)S(1)}, bf16[27,128,128]{2,1,0:T(8,128)(2,1)S(1)}, bf16[6,34,16,128]{3,2,1,0:T(8,128)(2,1)S(1)}, bf16[4,512,512]{2,1,0:T(8,128)(2,1)S(1)}) custom-call(s32[8,6]{1,0:T(8,128)S(1)} %get-tuple-element.46.refs_0_.refs_1_, bf16[8,512,128]{2,1,0:T(8,128)(2,1)} %refs_1_.1, ...), custom_call_target="tpu_custom_call" | custom-call | flops 1358954496 | bytes 786432 | tf_op jit(solution)/shard_map/fine_part/pallas_call | solution.py:500
  10.2 0.0 collective-permute-done.1.x_second.refs_2_.refs_4_
  10.2 1.6 %collective-permute-start.2 = (bf16[6,16,128]{2,1,0:T(8,128)(2,1)S(1)}, bf16[6,16,128]{2,1,0:T(8,128)(2,1)S(1)}, u32[]{:S(2)}, u32[]{:S(2)}) collective-permute-start(bf16[6,16,128]{2,1,0:T(8,128)(2,1)S(1)} %get-tuple-element.58.refs_6_), channel_id=1, source_target_pairs={{0,1},{1,0},{2,3},{3,2},{4,5},{5,4},{6,7},{7,6},{8,9},{9,8},{10,11... | collective-permute-start | bytes 73736 | tf_op jit(solution)/shard_map/ppermute | solution.py:591
  11.9 0.7 %collective-permute-start.3 = (bf16[6,16,128]{2,1,0:T(8,128)(2,1)S(1)}, bf16[6,16,128]{2,1,0:T(8,128)(2,1)S(1)}, u32[]{:S(2)}, u32[]{:S(2)}) collective-permute-start(bf16[6,16,128]{2,1,0:T(8,128)(2,1)S(1)} %get-tuple-element.62), channel_id=1, source_target_pairs={{1,2},{2,1},{5,6},{6,5},{9,10},{10,9},{13,14},{14,13},{17,18},{18,... | collective-permute-start | bytes 73736 | tf_op jit(solution)/shard_map/ppermute | solution.py:592
  12.5 0.0 copy-done
  12.5 3.1 %coarse.1 = (bf16[6,34,16,128]{3,2,1,0:T(8,128)(2,1)S(1)}, f32[4,32,16,128]{3,2,1,0:T(8,128)S(1)}, f32[8,128]{1,0:T(8,128)S(1)}, s32[4,128]{1,0:T(4,128)S(1)}) custom-call(bf16[6,34,16,128]{3,2,1,0:T(8,128)(2,1)S(1)} %get-tuple-element.54.refs_0_, bf16[33,16,128]{2,1,0:T(8,128)(2,1)S(1)} %get-tuple-element.47.refs_1_, ...), custom_call_target="tpu_custom_call", output_to_operand_aliasing={{0}: (0, {})} | custom-call | flops 1811939328 | bytes 1048576 | tf_op jit(solution)/shard_map/coarse/pallas_call | solution.py:594
  15.6 0.0 collective-permute-done.2.refs_3_
  15.6 0.0 collective-permute-done.3.refs_4_
  15.7 0.9 %edge.1 = (bf16[144,128]{1,0:T(8,128)(2,1)S(1)}, bf16[144,128]{1,0:T(8,128)(2,1)S(1)}, bf16[144,128]{1,0:T(8,128)(2,1)S(1)}, bf16[144,128]{1,0:T(8,128)(2,1)S(1)}, f32[4,32,16,128]{3,2,1,0:T(8,128)S(1)}) custom-call(s32[4,128]{1,0:T(4,128)S(1)} %get-tuple-element.59.refs_0_, ...), custom_call_target="tpu_custom_call", output_to_operand_aliasing={{4}: (1, {})} | custom-call | tf_op jit(solution)/shard_map/edge/pallas_call | solution.py:622
  16.5 0.3 collective-permute-start.4
  16.8 0.9 %collective-permute-start.5 = (bf16[144,128]{1,0:T(8,128)(2,1)S(1)}, bf16[144,128]{1,0:T(8,128)(2,1)S(1)}, u32[]{:S(2)}, u32[]{:S(2)}) collective-permute-start(bf16[144,128]{1,0:T(8,128)(2,1)S(1)} %get-tuple-element.69), channel_id=1, source_target_pairs={{0,8},{4,12},{8,0},{12,4},{1,9},{5,13},{9,1},{13,5},{2,10},{6,14},... | collective-permute-start | bytes 110600 | tf_op jit(solution)/shard_map/ppermute | solution.py:640
  17.7 0.7 %collective-permute-start.6 = (bf16[144,128]{1,0:T(8,128)(2,1)S(1)}, bf16[144,128]{1,0:T(8,128)(2,1)S(1)}, u32[]{:S(2)}, u32[]{:S(2)}) collective-permute-start(bf16[144,128]{1,0:T(8,128)(2,1)S(1)} %get-tuple-element.70), channel_id=1, source_target_pairs={{0,12},{4,8},{8,4},{12,0},{1,13},{5,9},{9,5},{13,1},{2,14},{6,10},... | collective-permute-start | bytes 110600 | tf_op jit(solution)/shard_map/ppermute | solution.py:640
  18.5 2.7 %fine_part.4.refs_16_ = f32[3,512,128]{2,1,0:T(8,128)S(1)} custom-call(s32[8,6]{1,0:T(8,128)S(1)} %get-tuple-element.46.refs_0_.refs_1_, bf16[8,512,128]{2,1,0:T(8,128)(2,1)S(1)} %get-tuple-element.71.refs_1_.refs_13_, bf16[27,128,128]{2,1,0:T(8,128)(2,1)S(1)} %get-tuple-element.72.refs_2_, bf16[144,128]{1,0:T(8,128)(2,1)S(1)} %get-tuple-element.67.refs_3_.refs_2_), custom_call_target="tpu_custom_call" | custom-call | flops 1358954496 | bytes 786432 | tf_op jit(solution)/shard_map/fine_part/pallas_call | solution.py:500
  21.2 0.0 copy-start.1
  21.2 0.0 copy-start.2
  21.2 0.0 copy-start.3
  21.3 0.0 collective-permute-done.4.refs_3_
  21.3 0.0 collective-permute-done.5.refs_4_
  21.3 0.0 collective-permute-done.6.refs_5_
  21.4 4.4 %collective-permute-start.7 = (f32[2,128]{1,0:T(2,128)S(1)}, f32[2,128]{1,0:T(2,128)S(1)}, u32[]{:S(2)}, u32[]{:S(2)}) collective-permute-start(f32[2,128]{1,0:T(2,128)S(1)} %pad_maximum_fusion.refs_3_.refs_6_), channel_id=1, source_target_pairs={{0,1},{1,0},{2,3},{3,2},{4,5},{5,4},{6,7},{7,6},{8,9},{9,8},{10,11... | collective-permute-start | bytes 3080 | tf_op jit(solution)/shard_map/ppermute | solution.py:653
  25.9 0.2 collective-permute-start.8
  26.1 2.3 %collective-permute-start.9 = (f32[2,128]{1,0:T(2,128)S(1)}, f32[2,128]{1,0:T(2,128)S(1)}, u32[]{:S(2)}, u32[]{:S(2)}) collective-permute-start(f32[2,128]{1,0:T(2,128)S(1)} %pad_maximum_fusion.refs_3_.refs_6_), channel_id=1, source_target_pairs={{0,3},{1,2},{2,1},{3,0},{4,7},{5,6},{6,5},{7,4},{8,11},{9,10},{10,... | collective-permute-start | bytes 3080 | tf_op jit(solution)/shard_map/ppermute | solution.py:653
  28.3 2.1 %fine_part.5.refs_17_ = f32[2,512,128]{2,1,0:T(8,128)S(1)} custom-call(s32[8,6]{1,0:T(8,128)S(1)} %get-tuple-element.46.refs_0_.refs_1_, bf16[8,512,128]{2,1,0:T(8,128)(2,1)S(1)} %get-tuple-element.71.refs_1_.refs_13_, bf16[27,128,128]{2,1,0:T(8,128)(2,1)S(1)} %get-tuple-element.72.refs_2_, f32[2,128]{1,0:T(2,128)S(1)} %pad_maximum_fusion.refs_3_.refs_6_), custom_call_target="tpu_custom_call" | custom-call | flops 905969664 | bytes 524288 | tf_op jit(solution)/shard_map/fine_part/pallas_call | solution.py:500
  30.4 0.0 collective-permute-done.7.refs_7_
  30.4 0.0 collective-permute-done.8.refs_8_
  30.4 1.0 %collective-permute-done.9.refs_9_ = f32[2,128]{1,0:T(2,128)S(1)} collective-permute-done((f32[2,128]{1,0:T(2,128)S(1)}, f32[2,128]{1,0:T(2,128)S(1)}, u32[]{:S(2)}, u32[]{:S(2)}) %collective-permute-start.9) | collective-permute-done | bytes 1056 | tf_op jit(solution)/shard_map/ppermute | solution.py:653
  31.4 0.0 copy-done.1
  31.4 0.0 copy-done.2
  31.4 0.0 copy-done.3
  31.4 3.5 %final.1 = bf16[8,512,128]{2,1,0:T(8,128)(2,1)} custom-call(s32[3,8]{1,0:T(4,128)S(1)} %get-tuple-element.45.refs_0_, s32[8,6]{1,0:T(8,128)S(1)} %get-tuple-element.46.refs_0_.refs_1_, bf16[144,128]{1,0:T(8,128)(2,1)S(1)} %get-tuple-element.67.refs_3_.refs_2_, bf16[144,128]{1,0:T(8,128)(2,1)S(1)} %collective-permute-done.4.refs_3_, ...), custom_call_target="tpu_custom_call" | custom-call | tf_op jit(solution)/shard_map/final/pallas_call | solution.py:660
  (10 shorter events, 0.1 us)
Async XLA Ops:
  1.0 1.6 %collective-permute-start = (bf16[33,16,128]{2,1,0:T(8,128)(2,1)S(1)}, bf16[33,16,128]{2,1,0:T(8,128)(2,1)S(1)}, u32[]{:S(2)}, u32[]{:S(2)}) collective-permute-start(bf16[33,16,128]{2,1,0:T(8,128)(2,1)S(1)} %get-tuple-element.47.refs_1_), channel_id=1, source_target_pairs={{0,4},{4,0},{8,12},{12,8},{1,5},{5,1},{9,13},{13,9},{2,6},{6,2},{1... | collective-permute-start | bytes 405512 | tf_op jit(solution)/shard_map/ppermute | solution.py:552
  2.6 7.6 %collective-permute-start.1 = (bf16[34,16,128]{2,1,0:T(8,128)(2,1)S(1)}, bf16[34,16,128]{2,1,0:T(8,128)(2,1)S(1)}, u32[]{:S(2)}, u32[]{:S(2)}) collective-permute-start(bf16[34,16,128]{2,1,0:T(8,128)(2,1)S(1)} %relay.1.refs_3_), channel_id=1, source_target_pairs={{0,12},{4,8},{8,4},{12,0},{1,13},{5,9},{9,5},{13,1},{2,14},{6,10},... | collective-permute-start | bytes 417800 | tf_op jit(solution)/shard_map/ppermute | solution.py:563
  5.2 7.3 %copy-start = (bf16[27,128,128]{2,1,0:T(8,128)(2,1)S(1)}, bf16[27,128,128]{2,1,0:T(8,128)(2,1)}, u32[]{:S(2)}) copy-start(bf16[27,128,128]{2,1,0:T(8,128)(2,1)} %refs_5_.3) | copy-start | bytes 2654212
  10.2 5.4 %collective-permute-start.2 = (bf16[6,16,128]{2,1,0:T(8,128)(2,1)S(1)}, bf16[6,16,128]{2,1,0:T(8,128)(2,1)S(1)}, u32[]{:S(2)}, u32[]{:S(2)}) collective-permute-start(bf16[6,16,128]{2,1,0:T(8,128)(2,1)S(1)} %get-tuple-element.58.refs_6_), channel_id=1, source_target_pairs={{0,1},{1,0},{2,3},{3,2},{4,5},{5,4},{6,7},{7,6},{8,9},{9,8},{10,11... | collective-permute-start | bytes 73736 | tf_op jit(solution)/shard_map/ppermute | solution.py:591
  11.9 3.8 %collective-permute-start.3 = (bf16[6,16,128]{2,1,0:T(8,128)(2,1)S(1)}, bf16[6,16,128]{2,1,0:T(8,128)(2,1)S(1)}, u32[]{:S(2)}, u32[]{:S(2)}) collective-permute-start(bf16[6,16,128]{2,1,0:T(8,128)(2,1)S(1)} %get-tuple-element.62), channel_id=1, source_target_pairs={{1,2},{2,1},{5,6},{6,5},{9,10},{10,9},{13,14},{14,13},{17,18},{18,... | collective-permute-start | bytes 73736 | tf_op jit(solution)/shard_map/ppermute | solution.py:592
  16.5 4.7 %collective-permute-start.4 = (bf16[144,128]{1,0:T(8,128)(2,1)S(1)}, bf16[144,128]{1,0:T(8,128)(2,1)S(1)}, u32[]{:S(2)}, u32[]{:S(2)}) collective-permute-start(bf16[144,128]{1,0:T(8,128)(2,1)S(1)} %get-tuple-element.68), channel_id=1, source_target_pairs={{0,4},{4,0},{8,12},{12,8},{1,5},{5,1},{9,13},{13,9},{2,6},{6,2},{1... | collective-permute-start | bytes 110600 | tf_op jit(solution)/shard_map/ppermute | solution.py:640
  16.8 4.4 %collective-permute-start.5 = (bf16[144,128]{1,0:T(8,128)(2,1)S(1)}, bf16[144,128]{1,0:T(8,128)(2,1)S(1)}, u32[]{:S(2)}, u32[]{:S(2)}) collective-permute-start(bf16[144,128]{1,0:T(8,128)(2,1)S(1)} %get-tuple-element.69), channel_id=1, source_target_pairs={{0,8},{4,12},{8,0},{12,4},{1,9},{5,13},{9,1},{13,5},{2,10},{6,14},... | collective-permute-start | bytes 110600 | tf_op jit(solution)/shard_map/ppermute | solution.py:640
  17.7 3.6 %collective-permute-start.6 = (bf16[144,128]{1,0:T(8,128)(2,1)S(1)}, bf16[144,128]{1,0:T(8,128)(2,1)S(1)}, u32[]{:S(2)}, u32[]{:S(2)}) collective-permute-start(bf16[144,128]{1,0:T(8,128)(2,1)S(1)} %get-tuple-element.70), channel_id=1, source_target_pairs={{0,12},{4,8},{8,4},{12,0},{1,13},{5,9},{9,5},{13,1},{2,14},{6,10},... | collective-permute-start | bytes 110600 | tf_op jit(solution)/shard_map/ppermute | solution.py:640
  21.2 10.2 %copy-start.1 = (bf16[128,128]{1,0:T(8,128)(2,1)S(1)}, bf16[128,128]{1,0:T(8,128)(2,1)}, u32[]{:S(2)}) copy-start(bf16[128,128]{1,0:T(8,128)(2,1)} %refs_12_.1) | copy-start | bytes 98308
  21.2 10.2 %copy-start.2 = (f32[128]{0:T(128)S(1)}, f32[128]{0:T(128)}, u32[]{:S(2)}) copy-start(f32[128]{0:T(128)} %param.11) | copy-start | bytes 1540
  21.2 10.2 %copy-start.3 = (f32[128]{0:T(128)S(1)}, f32[128]{0:T(128)}, u32[]{:S(2)}) copy-start(f32[128]{0:T(128)} %param.12) | copy-start | bytes 1540
  21.4 9.0 %collective-permute-start.7 = (f32[2,128]{1,0:T(2,128)S(1)}, f32[2,128]{1,0:T(2,128)S(1)}, u32[]{:S(2)}, u32[]{:S(2)}) collective-permute-start(f32[2,128]{1,0:T(2,128)S(1)} %pad_maximum_fusion.refs_3_.refs_6_), channel_id=1, source_target_pairs={{0,1},{1,0},{2,3},{3,2},{4,5},{5,4},{6,7},{7,6},{8,9},{9,8},{10,11... | collective-permute-start | bytes 3080 | tf_op jit(solution)/shard_map/ppermute | solution.py:653
  25.9 4.5 %collective-permute-start.8 = (f32[2,128]{1,0:T(2,128)S(1)}, f32[2,128]{1,0:T(2,128)S(1)}, u32[]{:S(2)}, u32[]{:S(2)}) collective-permute-start(f32[2,128]{1,0:T(2,128)S(1)} %pad_maximum_fusion.refs_3_.refs_6_), channel_id=1, source_target_pairs={{0,2},{1,3},{2,0},{3,1},{4,6},{5,7},{6,4},{7,5},{8,10},{9,11},{10,... | collective-permute-start | bytes 3080 | tf_op jit(solution)/shard_map/ppermute | solution.py:653
  26.1 5.4 %collective-permute-start.9 = (f32[2,128]{1,0:T(2,128)S(1)}, f32[2,128]{1,0:T(2,128)S(1)}, u32[]{:S(2)}, u32[]{:S(2)}) collective-permute-start(f32[2,128]{1,0:T(2,128)S(1)} %pad_maximum_fusion.refs_3_.refs_6_), channel_id=1, source_target_pairs={{0,3},{1,2},{2,1},{3,0},{4,7},{5,6},{6,5},{7,4},{8,11},{9,10},{10,... | collective-permute-start | bytes 3080 | tf_op jit(solution)/shard_map/ppermute | solution.py:653

commit v4 on v3

--- a/solution.py
+++ b/solution.py
@@ -30,16 +30,6 @@
     return [(i, i ^ distance) for i in range(count)]
 
 
-def wide_weight(weight):
-    return jnp.concatenate(
-        [
-            jnp.concatenate([weight[3 * ab + c] for c in range(3)], axis=1)
-            for ab in range(9)
-        ],
-        axis=0,
-    )
-
-
 def shifted_sum(sums, depth, channels):
     rows = sums.shape[0]
     place = lax.broadcasted_iota(jnp.int32, (rows, channels), 0) % depth
@@ -49,6 +39,61 @@
         sums[:, channels : 2 * channels]
         + jnp.where(place == 0, 0.0, below)
         + jnp.where(place == depth - 1, 0.0, above)
+    )
+
+
+def convolved(get, weight, outer, depth):
+    channels = weight.shape[1]
+    taken = jnp.concatenate(
+        [
+            jnp.concatenate([get(i + a, b) for i in range(outer)], axis=0)
+            for a in range(3)
+            for b in range(3)
+        ],
+        axis=1,
+    )
+    taps = jnp.concatenate(
+        [jnp.concatenate([weight[3 * ab], weight[3 * ab + 1]], axis=1) for ab in range(9)], axis=0
+    )
+    sums = jnp.dot(taken, taps, preferred_element_type=F32)
+    zero = jnp.zeros((channels, channels), BF16)
+    taken = jnp.concatenate(
+        [
+            jnp.concatenate([get(i + a, b) for i in range(0, outer, 2)], axis=0)
+            for a in range(4)
+            for b in range(3)
+        ],
+        axis=1,
+    )
+    taps = jnp.concatenate(
+        [
+            jnp.concatenate(
+                [
+                    weight[3 * (3 * a + b) + 2] if a < 3 else zero,
+                    weight[3 * (3 * a - 3 + b) + 2] if a else zero,
+                ],
+                axis=1,
+            )
+            for a in range(4)
+            for b in range(3)
+        ],
+        axis=0,
+    )
+    above = jnp.dot(taken, taps, preferred_element_type=F32)
+    rows = sums.shape[0]
+    plane = rows // outer
+    above = jnp.concatenate(
+        [
+            above[i // 2 * plane : (i // 2 + 1) * plane, i % 2 * channels : (i % 2 + 1) * channels]
+            for i in range(outer)
+        ],
+        axis=0,
+    )
+    place = lax.broadcasted_iota(jnp.int32, (rows, channels), 0) % depth
+    return (
+        sums[:, channels:]
+        + jnp.where(place == 0, 0.0, pltpu.roll(sums[:, :channels], 1, 0))
+        + jnp.where(place == depth - 1, 0.0, pltpu.roll(above, rows - 1, 0))
     )
 
 
@@ -180,18 +225,15 @@
                 ).astype(BF16)
         if role == "load" and slot == 0:
             loads[1].wait()
-        taken = []
-        for a in range(3):
-            for b in range(3):
-                if b == 1:
-                    part = even[slot, pl.ds(a, FB)]
-                else:
-                    part = odd[slot, pl.ds(a, FB), pl.ds(b // 2, lines)]
-                taken.append(part.reshape(FB**3, channels))
-        sums = jnp.dot(
-            jnp.concatenate(taken, axis=1), wide_weight(weight), preferred_element_type=F32
-        )
-        out[slot] = shifted_sum(sums, FB, channels)
+
+        def get(plane_index, b, slot=slot):
+            if b == 1:
+                part = even[slot, plane_index]
+            else:
+                part = odd[slot, plane_index, pl.ds(b // 2, lines)]
+            return part.reshape(FB * FB, channels)
+
+        out[slot] = convolved(get, weight, FB, FB)
     if role == "load":
         fold_weights(weight, folded)
     for load in loads[2:]:
@@ -257,15 +299,13 @@
     first.wait()
     means, squares = [], []
     for x in range(dx):
-        taken = [
-            padded[x + a, pl.ds(b, dy)].reshape(dy * dz, channels)
-            for a in range(3)
-            for b in range(3)
-        ]
-        sums = jnp.dot(
-            jnp.concatenate(taken, axis=1), wide_weight(weight), preferred_element_type=F32
-        )
-        value = shifted_sum(sums, dz, channels).reshape(dy, dz, channels)
+        if x % 2 == 0:
+
+            def get(plane_index, b, x=x):
+                return padded[x + plane_index, pl.ds(b, dy)].reshape(dy * dz, channels)
+
+            both = convolved(get, weight, 2, dz).reshape(2, dy, dz, channels)
+        value = both[x % 2]
         conv[x] = value
         if x == 0:
             picks[...] = choose([note.astype(F32) for note in asked], dy // EDGE)

time: 35.2 us -> 34.9 us (level)
  Pallas kernels: 18.4 us -> 16.9 us
  waiting for transfers between devices: 2.06 us -> 3.19 us
    pallas_call x3, Pallas kernels: 9.76 us -> 8.74 us  [fine_part(): pl.pallas_call(functools.partial(fine_kernel, first, count, role), out_sh...]
    ppermute x3, waiting for transfers between devices: 0.05 us -> 0.71 us  [body(): lax.ppermute(sent[distance], 'slab', xor_links(slabs, distance))]
    ppermute x3, waiting for transfers between devices: 1.01 us -> 1.48 us  [body(): lax.ppermute(merged, 'sub', xor_links(subs, distance))]
    pallas_call x1, Pallas kernels: 3.1 us -> 2.69 us  [body(): pl.pallas_call(functools.partial(coarse_kernel, slabs, xor, (dx, dy, dz))...]
  transfers between devices with their start and end apart: 10 -> 10, of which waited for: 2 -> 4; matrix products, arithmetic and copies ran while one was open for 0% -> 0% of each run, Pallas kernels for 37% -> 33%
where the time goes in v4:
time: 34.9 us; the launch traced here: 34.7 us
  Pallas kernels  16.9 us (48%)
  starting transfers between devices  14.3 us (41%)
  waiting for transfers between devices  3.19 us (9%)
    pallas_call x3, Pallas kernels, fine_part(): pl.pallas_call(functools.partial(fine_kernel, first, count, role), out_sh...  8.74 us
    ppermute x3, starting transfers between devices, body(): lax.ppermute(merged, 'sub', xor_links(subs, distance))  6.91 us
    pallas_call x1, Pallas kernels, body(): pl.pallas_call(functools.partial(final_kernel, len(replies), len(lines),...  3.54 us
    pallas_call x1, Pallas kernels, body(): pl.pallas_call(functools.partial(coarse_kernel, slabs, xor, (dx, dy, dz))...  2.69 us
    ppermute x1, starting transfers between devices, body(): far = x_second = lax.ppermute(send_b, 'slab', xor_links(slabs, 3))  2.62 us
    ppermute x3, starting transfers between devices, body(): lax.ppermute(sent[distance], 'slab', xor_links(slabs, distance))  1.93 us
    ppermute x1, starting transfers between devices, body(): y_first = lax.ppermute(line_a, 'sub', pairs(subs, 0))  1.64 us
    ppermute x3, waiting for transfers between devices, body(): lax.ppermute(merged, 'sub', xor_links(subs, distance))  1.48 us
  transfers between devices with their start and end apart: 10, of which 4 were waited for; matrix products, arithmetic and copies ran while one was open for 0% of the time, Pallas kernels for 33%

profile of v4, /device:TPU:0, one launch (start us, length us, event | category | flops | bytes accessed | tf_op | source)
XLA Modules:
  0.0 34.7 jit_solution(7778777174719271050)
XLA Ops:
  0.0 1.0 %send.1 = (bf16[33,16,128]{2,1,0:T(8,128)(2,1)S(1)}, bf16[34,16,128]{2,1,0:T(8,128)(2,1)S(1)}, bf16[4,16,128]{2,1,0:T(8,128)(2,1)S(1)}, bf16[4,16,128]{2,1,0:T(8...) custom-call(bf16[4,32,16,128]{3,2,1,0:T(8,128)(2,1)} %refs_4_.1, s32[3,8]{1,0:T(4,128)} %bitcast.43, s32[8,6]{1,0:T(8,128)} %links.1), custom_call_target="tpu_custom_call" | custom-call | tf_op jit(solution)/shard_map/send/pallas_call | solution.py:576
  1.0 0.6 %collective-permute-start = (bf16[33,16,128]{2,1,0:T(8,128)(2,1)S(1)}, bf16[33,16,128]{2,1,0:T(8,128)(2,1)S(1)}, u32[]{:S(2)}, u32[]{:S(2)}) collective-permute-start(bf16[33,16,128]{2,1,0:T(8,128)(2,1)S(1)} %get-tuple-element.47.refs_1_), channel_id=1, source_target_pairs={{0,4},{4,0},{8,12},{12,8},{1,5},{5,1},{9,13},{13,9},{2,6},{6,2},{1... | collective-permute-start | bytes 405512 | tf_op jit(solution)/shard_map/ppermute | solution.py:592
  1.6 1.0 %collective-permute-done.x_first.refs_3_ = bf16[33,16,128]{2,1,0:T(8,128)(2,1)S(1)} collective-permute-done((bf16[33,16,128]{2,1,0:T(8,128)(2,1)S(1)}, bf16[33,16,128]{2,1,0:T(8,128)(2,1)S(1)}, u32[]{:S(2)}, u32[]{:S(2)}) %collective-permute-start) | collective-permute-done | bytes 135200 | tf_op jit(solution)/shard_map/ppermute | solution.py:592
  2.6 2.6 %collective-permute-start.1 = (bf16[34,16,128]{2,1,0:T(8,128)(2,1)S(1)}, bf16[34,16,128]{2,1,0:T(8,128)(2,1)S(1)}, u32[]{:S(2)}, u32[]{:S(2)}) collective-permute-start(bf16[34,16,128]{2,1,0:T(8,128)(2,1)S(1)} %relay.1.refs_3_), channel_id=1, source_target_pairs={{0,12},{4,8},{8,4},{12,0},{1,13},{5,9},{9,5},{13,1},{2,14},{6,10},... | collective-permute-start | bytes 417800 | tf_op jit(solution)/shard_map/ppermute | solution.py:603
  5.2 0.0 copy-start
  5.2 4.4 %fine_part.3 = (f32[3,512,128]{2,1,0:T(8,128)S(1)}, bf16[8,512,128]{2,1,0:T(8,128)(2,1)S(1)}, bf16[27,128,128]{2,1,0:T(8,128)(2,1)S(1)}, bf16[6,34,16,128]{3,2,1,0:T(8,128)(2,1)S(1)}, bf16[4,512,512]{2,1,0:T(8,128)(2,1)S(1)}) custom-call(s32[8,6]{1,0:T(8,128)S(1)} %get-tuple-element.46.refs_0_.refs_1_, bf16[8,512,128]{2,1,0:T(8,128)(2,1)} %refs_1_.1, ...), custom_call_target="tpu_custom_call" | custom-call | flops 1358954496 | bytes 786432 | tf_op jit(solution)/shard_map/fine_part/pallas_call | solution.py:540
  9.7 0.0 collective-permute-done.1.x_second.refs_2_.refs_4_
  9.7 1.6 %collective-permute-start.2 = (bf16[6,16,128]{2,1,0:T(8,128)(2,1)S(1)}, bf16[6,16,128]{2,1,0:T(8,128)(2,1)S(1)}, u32[]{:S(2)}, u32[]{:S(2)}) collective-permute-start(bf16[6,16,128]{2,1,0:T(8,128)(2,1)S(1)} %get-tuple-element.58.refs_6_), channel_id=1, source_target_pairs={{0,1},{1,0},{2,3},{3,2},{4,5},{5,4},{6,7},{7,6},{8,9},{9,8},{10,11... | collective-permute-start | bytes 73736 | tf_op jit(solution)/shard_map/ppermute | solution.py:631
  11.3 0.7 %collective-permute-start.3 = (bf16[6,16,128]{2,1,0:T(8,128)(2,1)S(1)}, bf16[6,16,128]{2,1,0:T(8,128)(2,1)S(1)}, u32[]{:S(2)}, u32[]{:S(2)}) collective-permute-start(bf16[6,16,128]{2,1,0:T(8,128)(2,1)S(1)} %get-tuple-element.62), channel_id=1, source_target_pairs={{1,2},{2,1},{5,6},{6,5},{9,10},{10,9},{13,14},{14,13},{17,18},{18,... | collective-permute-start | bytes 73736 | tf_op jit(solution)/shard_map/ppermute | solution.py:632
  12.0 0.0 copy-done
  12.0 2.7 %coarse.1 = (bf16[6,34,16,128]{3,2,1,0:T(8,128)(2,1)S(1)}, f32[4,32,16,128]{3,2,1,0:T(8,128)S(1)}, f32[8,128]{1,0:T(8,128)S(1)}, s32[4,128]{1,0:T(4,128)S(1)}) custom-call(bf16[6,34,16,128]{3,2,1,0:T(8,128)(2,1)S(1)} %get-tuple-element.54.refs_0_, bf16[33,16,128]{2,1,0:T(8,128)(2,1)S(1)} %get-tuple-element.47.refs_1_, ...), custom_call_target="tpu_custom_call", output_to_operand_aliasing={{0}: (0, {})} | custom-call | flops 1811939328 | bytes 1048576 | tf_op jit(solution)/shard_map/coarse/pallas_call | solution.py:634
  14.7 0.0 collective-permute-done.2.refs_3_
  14.7 0.0 collective-permute-done.3.refs_4_
  14.7 0.9 %edge.1 = (bf16[144,128]{1,0:T(8,128)(2,1)S(1)}, bf16[144,128]{1,0:T(8,128)(2,1)S(1)}, bf16[144,128]{1,0:T(8,128)(2,1)S(1)}, bf16[144,128]{1,0:T(8,128)(2,1)S(1)}, f32[4,32,16,128]{3,2,1,0:T(8,128)S(1)}) custom-call(s32[4,128]{1,0:T(4,128)S(1)} %get-tuple-element.59.refs_0_, ...), custom_call_target="tpu_custom_call", output_to_operand_aliasing={{4}: (1, {})} | custom-call | tf_op jit(solution)/shard_map/edge/pallas_call | solution.py:662
  15.6 0.3 collective-permute-start.4
  15.9 1.4 %collective-permute-start.5 = (bf16[144,128]{1,0:T(8,128)(2,1)S(1)}, bf16[144,128]{1,0:T(8,128)(2,1)S(1)}, u32[]{:S(2)}, u32[]{:S(2)}) collective-permute-start(bf16[144,128]{1,0:T(8,128)(2,1)S(1)} %get-tuple-element.69), channel_id=1, source_target_pairs={{0,8},{4,12},{8,0},{12,4},{1,9},{5,13},{9,1},{13,5},{2,10},{6,14},... | collective-permute-start | bytes 110600 | tf_op jit(solution)/shard_map/ppermute | solution.py:680
  17.3 0.2 collective-permute-start.6
  17.5 2.4 %fine_part.4.refs_16_ = f32[3,512,128]{2,1,0:T(8,128)S(1)} custom-call(s32[8,6]{1,0:T(8,128)S(1)} %get-tuple-element.46.refs_0_.refs_1_, bf16[8,512,128]{2,1,0:T(8,128)(2,1)S(1)} %get-tuple-element.71.refs_1_.refs_13_, bf16[27,128,128]{2,1,0:T(8,128)(2,1)S(1)} %get-tuple-element.72.refs_2_, bf16[144,128]{1,0:T(8,128)(2,1)S(1)} %get-tuple-element.67.refs_3_.refs_2_), custom_call_target="tpu_custom_call" | custom-call | flops 1358954496 | bytes 786432 | tf_op jit(solution)/shard_map/fine_part/pallas_call | solution.py:540
  20.0 0.0 copy-start.1
  20.0 0.0 copy-start.2
  20.0 0.0 copy-start.3
  20.0 0.0 collective-permute-done.4.refs_3_
  20.0 0.0 collective-permute-done.5.refs_4_
  20.1 0.7 %collective-permute-done.6.refs_5_ = bf16[144,128]{1,0:T(8,128)(2,1)S(1)} collective-permute-done((bf16[144,128]{1,0:T(8,128)(2,1)S(1)}, bf16[144,128]{1,0:T(8,128)(2,1)S(1)}, u32[]{:S(2)}, u32[]{:S(2)}) %collective-permute-start.6) | collective-permute-done | bytes 36896 | tf_op jit(solution)/shard_map/ppermute | solution.py:680
  20.9 4.5 %collective-permute-start.7 = (f32[2,128]{1,0:T(2,128)S(1)}, f32[2,128]{1,0:T(2,128)S(1)}, u32[]{:S(2)}, u32[]{:S(2)}) collective-permute-start(f32[2,128]{1,0:T(2,128)S(1)} %pad_maximum_fusion.refs_3_.refs_6_), channel_id=1, source_target_pairs={{0,1},{1,0},{2,3},{3,2},{4,5},{5,4},{6,7},{7,6},{8,9},{9,8},{10,11... | collective-permute-start | bytes 3080 | tf_op jit(solution)/shard_map/ppermute | solution.py:693
  25.3 0.4 %collective-permute-start.8 = (f32[2,128]{1,0:T(2,128)S(1)}, f32[2,128]{1,0:T(2,128)S(1)}, u32[]{:S(2)}, u32[]{:S(2)}) collective-permute-start(f32[2,128]{1,0:T(2,128)S(1)} %pad_maximum_fusion.refs_3_.refs_6_), channel_id=1, source_target_pairs={{0,2},{1,3},{2,0},{3,1},{4,6},{5,7},{6,4},{7,5},{8,10},{9,11},{10,... | collective-permute-start | bytes 3080 | tf_op jit(solution)/shard_map/ppermute | solution.py:693
  25.8 2.0 %collective-permute-start.9 = (f32[2,128]{1,0:T(2,128)S(1)}, f32[2,128]{1,0:T(2,128)S(1)}, u32[]{:S(2)}, u32[]{:S(2)}) collective-permute-start(f32[2,128]{1,0:T(2,128)S(1)} %pad_maximum_fusion.refs_3_.refs_6_), channel_id=1, source_target_pairs={{0,3},{1,2},{2,1},{3,0},{4,7},{5,6},{6,5},{7,4},{8,11},{9,10},{10,... | collective-permute-start | bytes 3080 | tf_op jit(solution)/shard_map/ppermute | solution.py:693
  27.8 1.9 %fine_part.5.refs_17_ = f32[2,512,128]{2,1,0:T(8,128)S(1)} custom-call(s32[8,6]{1,0:T(8,128)S(1)} %get-tuple-element.46.refs_0_.refs_1_, bf16[8,512,128]{2,1,0:T(8,128)(2,1)S(1)} %get-tuple-element.71.refs_1_.refs_13_, bf16[27,128,128]{2,1,0:T(8,128)(2,1)S(1)} %get-tuple-element.72.refs_2_, f32[2,128]{1,0:T(2,128)S(1)} %pad_maximum_fusion.refs_3_.refs_6_), custom_call_target="tpu_custom_call" | custom-call | flops 905969664 | bytes 524288 | tf_op jit(solution)/shard_map/fine_part/pallas_call | solution.py:540
  29.6 0.0 collective-permute-done.7.refs_7_
  29.7 0.1 collective-permute-done.8.refs_8_
  29.8 1.3 %collective-permute-done.9.refs_9_ = f32[2,128]{1,0:T(2,128)S(1)} collective-permute-done((f32[2,128]{1,0:T(2,128)S(1)}, f32[2,128]{1,0:T(2,128)S(1)}, u32[]{:S(2)}, u32[]{:S(2)}) %collective-permute-start.9) | collective-permute-done | bytes 1056 | tf_op jit(solution)/shard_map/ppermute | solution.py:693
  31.1 0.0 copy-done.1
  31.1 0.0 copy-done.2
  31.1 0.0 copy-done.3
  31.1 3.5 %final.1 = bf16[8,512,128]{2,1,0:T(8,128)(2,1)} custom-call(s32[3,8]{1,0:T(4,128)S(1)} %get-tuple-element.45.refs_0_, s32[8,6]{1,0:T(8,128)S(1)} %get-tuple-element.46.refs_0_.refs_1_, bf16[144,128]{1,0:T(8,128)(2,1)S(1)} %get-tuple-element.67.refs_3_.refs_2_, bf16[144,128]{1,0:T(8,128)(2,1)S(1)} %collective-permute-done.4.refs_3_, ...), custom_call_target="tpu_custom_call" | custom-call | tf_op jit(solution)/shard_map/final/pallas_call | solution.py:700
  (10 shorter events, 0.1 us)
Async XLA Ops:
  1.0 1.6 %collective-permute-start = (bf16[33,16,128]{2,1,0:T(8,128)(2,1)S(1)}, bf16[33,16,128]{2,1,0:T(8,128)(2,1)S(1)}, u32[]{:S(2)}, u32[]{:S(2)}) collective-permute-start(bf16[33,16,128]{2,1,0:T(8,128)(2,1)S(1)} %get-tuple-element.47.refs_1_), channel_id=1, source_target_pairs={{0,4},{4,0},{8,12},{12,8},{1,5},{5,1},{9,13},{13,9},{2,6},{6,2},{1... | collective-permute-start | bytes 405512 | tf_op jit(solution)/shard_map/ppermute | solution.py:592
  2.6 7.1 %collective-permute-start.1 = (bf16[34,16,128]{2,1,0:T(8,128)(2,1)S(1)}, bf16[34,16,128]{2,1,0:T(8,128)(2,1)S(1)}, u32[]{:S(2)}, u32[]{:S(2)}) collective-permute-start(bf16[34,16,128]{2,1,0:T(8,128)(2,1)S(1)} %relay.1.refs_3_), channel_id=1, source_target_pairs={{0,12},{4,8},{8,4},{12,0},{1,13},{5,9},{9,5},{13,1},{2,14},{6,10},... | collective-permute-start | bytes 417800 | tf_op jit(solution)/shard_map/ppermute | solution.py:603
  5.2 6.8 %copy-start = (bf16[27,128,128]{2,1,0:T(8,128)(2,1)S(1)}, bf16[27,128,128]{2,1,0:T(8,128)(2,1)}, u32[]{:S(2)}) copy-start(bf16[27,128,128]{2,1,0:T(8,128)(2,1)} %refs_5_.3) | copy-start | bytes 2654212
  9.7 5.0 %collective-permute-start.2 = (bf16[6,16,128]{2,1,0:T(8,128)(2,1)S(1)}, bf16[6,16,128]{2,1,0:T(8,128)(2,1)S(1)}, u32[]{:S(2)}, u32[]{:S(2)}) collective-permute-start(bf16[6,16,128]{2,1,0:T(8,128)(2,1)S(1)} %get-tuple-element.58.refs_6_), channel_id=1, source_target_pairs={{0,1},{1,0},{2,3},{3,2},{4,5},{5,4},{6,7},{7,6},{8,9},{9,8},{10,11... | collective-permute-start | bytes 73736 | tf_op jit(solution)/shard_map/ppermute | solution.py:631
  11.3 3.4 %collective-permute-start.3 = (bf16[6,16,128]{2,1,0:T(8,128)(2,1)S(1)}, bf16[6,16,128]{2,1,0:T(8,128)(2,1)S(1)}, u32[]{:S(2)}, u32[]{:S(2)}) collective-permute-start(bf16[6,16,128]{2,1,0:T(8,128)(2,1)S(1)} %get-tuple-element.62), channel_id=1, source_target_pairs={{1,2},{2,1},{5,6},{6,5},{9,10},{10,9},{13,14},{14,13},{17,18},{18,... | collective-permute-start | bytes 73736 | tf_op jit(solution)/shard_map/ppermute | solution.py:632
  15.6 4.4 %collective-permute-start.4 = (bf16[144,128]{1,0:T(8,128)(2,1)S(1)}, bf16[144,128]{1,0:T(8,128)(2,1)S(1)}, u32[]{:S(2)}, u32[]{:S(2)}) collective-permute-start(bf16[144,128]{1,0:T(8,128)(2,1)S(1)} %get-tuple-element.68), channel_id=1, source_target_pairs={{0,4},{4,0},{8,12},{12,8},{1,5},{5,1},{9,13},{13,9},{2,6},{6,2},{1... | collective-permute-start | bytes 110600 | tf_op jit(solution)/shard_map/ppermute | solution.py:680
  15.9 4.1 %collective-permute-start.5 = (bf16[144,128]{1,0:T(8,128)(2,1)S(1)}, bf16[144,128]{1,0:T(8,128)(2,1)S(1)}, u32[]{:S(2)}, u32[]{:S(2)}) collective-permute-start(bf16[144,128]{1,0:T(8,128)(2,1)S(1)} %get-tuple-element.69), channel_id=1, source_target_pairs={{0,8},{4,12},{8,0},{12,4},{1,9},{5,13},{9,1},{13,5},{2,10},{6,14},... | collective-permute-start | bytes 110600 | tf_op jit(solution)/shard_map/ppermute | solution.py:680
  17.3 3.4 %collective-permute-start.6 = (bf16[144,128]{1,0:T(8,128)(2,1)S(1)}, bf16[144,128]{1,0:T(8,128)(2,1)S(1)}, u32[]{:S(2)}, u32[]{:S(2)}) collective-permute-start(bf16[144,128]{1,0:T(8,128)(2,1)S(1)} %get-tuple-element.70), channel_id=1, source_target_pairs={{0,12},{4,8},{8,4},{12,0},{1,13},{5,9},{9,5},{13,1},{2,14},{6,10},... | collective-permute-start | bytes 110600 | tf_op jit(solution)/shard_map/ppermute | solution.py:680
  20.0 11.2 %copy-start.1 = (bf16[128,128]{1,0:T(8,128)(2,1)S(1)}, bf16[128,128]{1,0:T(8,128)(2,1)}, u32[]{:S(2)}) copy-start(bf16[128,128]{1,0:T(8,128)(2,1)} %refs_12_.1) | copy-start | bytes 98308
  20.0 11.1 %copy-start.2 = (f32[128]{0:T(128)S(1)}, f32[128]{0:T(128)}, u32[]{:S(2)}) copy-start(f32[128]{0:T(128)} %param.11) | copy-start | bytes 1540
  20.0 11.1 %copy-start.3 = (f32[128]{0:T(128)S(1)}, f32[128]{0:T(128)}, u32[]{:S(2)}) copy-start(f32[128]{0:T(128)} %param.12) | copy-start | bytes 1540
  20.9 8.8 %collective-permute-start.7 = (f32[2,128]{1,0:T(2,128)S(1)}, f32[2,128]{1,0:T(2,128)S(1)}, u32[]{:S(2)}, u32[]{:S(2)}) collective-permute-start(f32[2,128]{1,0:T(2,128)S(1)} %pad_maximum_fusion.refs_3_.refs_6_), channel_id=1, source_target_pairs={{0,1},{1,0},{2,3},{3,2},{4,5},{5,4},{6,7},{7,6},{8,9},{9,8},{10,11... | collective-permute-start | bytes 3080 | tf_op jit(solution)/shard_map/ppermute | solution.py:693
  25.3 4.5 %collective-permute-start.8 = (f32[2,128]{1,0:T(2,128)S(1)}, f32[2,128]{1,0:T(2,128)S(1)}, u32[]{:S(2)}, u32[]{:S(2)}) collective-permute-start(f32[2,128]{1,0:T(2,128)S(1)} %pad_maximum_fusion.refs_3_.refs_6_), channel_id=1, source_target_pairs={{0,2},{1,3},{2,0},{3,1},{4,6},{5,7},{6,4},{7,5},{8,10},{9,11},{10,... | collective-permute-start | bytes 3080 | tf_op jit(solution)/shard_map/ppermute | solution.py:693
  25.8 5.4 %collective-permute-start.9 = (f32[2,128]{1,0:T(2,128)S(1)}, f32[2,128]{1,0:T(2,128)S(1)}, u32[]{:S(2)}, u32[]{:S(2)}) collective-permute-start(f32[2,128]{1,0:T(2,128)S(1)} %pad_maximum_fusion.refs_3_.refs_6_), channel_id=1, source_target_pairs={{0,3},{1,2},{2,1},{3,0},{4,7},{5,6},{6,5},{7,4},{8,11},{9,10},{10,... | collective-permute-start | bytes 3080 | tf_op jit(solution)/shard_map/ppermute | solution.py:693

commit v5 on v4

--- a/solution.py
+++ b/solution.py
@@ -676,10 +676,9 @@
     cells = dx * dy * dz
     row = MOST * EDGE**3
     if xor:
-        replies = [sent[0]] + [
-            lax.ppermute(sent[distance], "slab", xor_links(slabs, distance))
-            for distance in range(1, slabs)
-        ]
+        replies = [sent[0]]
+        for distance in range(1, slabs):
+            replies.append(lax.ppermute(sent[distance], "slab", xor_links(slabs, distance)))
         parts = [r[row : row + 6] for r in replies]
     else:
         replies = [lax.all_to_all(sent[0], "slab", split_axis=0, concat_axis=0, tiled=True)]
@@ -689,9 +688,9 @@
     cells = cells * slabs
     merged = jnp.concatenate([mean, square])
     if subs == 4:
-        lines = [merged] + [
-            lax.ppermute(merged, "sub", xor_links(subs, distance)) for distance in range(1, subs)
-        ]
+        lines = [merged]
+        for distance in range(1, subs):
+            lines.append(lax.ppermute(merged, "sub", xor_links(subs, distance)))
     else:
         lines = list(lax.all_gather(merged, "sub", axis=0))
     _, lines = fill(2, merged, lines)

time: 34.9 us -> 34.9 us (level)
  no operation moved by 1% of the time
where the time goes in v5:
time: 34.9 us; the launch traced here: 34.7 us
  Pallas kernels  16.9 us (48%)
  starting transfers between devices  14.3 us (41%)
  waiting for transfers between devices  3.19 us (9%)
    pallas_call x3, Pallas kernels, fine_part(): pl.pallas_call(functools.partial(fine_kernel, first, count, role), out_sh...  8.74 us
    ppermute x3, starting transfers between devices, body(): lines.append(lax.ppermute(merged, 'sub', xor_links(subs, distance)))  6.91 us
    pallas_call x1, Pallas kernels, body(): pl.pallas_call(functools.partial(final_kernel, len(replies), len(lines),...  3.54 us
    pallas_call x1, Pallas kernels, body(): pl.pallas_call(functools.partial(coarse_kernel, slabs, xor, (dx, dy, dz))...  2.69 us
    ppermute x1, starting transfers between devices, body(): far = x_second = lax.ppermute(send_b, 'slab', xor_links(slabs, 3))  2.62 us
    ppermute x3, starting transfers between devices, body(): lax.ppermute(sent[distance], 'slab', xor_links(slabs, distance))  1.93 us
    ppermute x1, starting transfers between devices, body(): y_first = lax.ppermute(line_a, 'sub', pairs(subs, 0))  1.64 us
    ppermute x3, waiting for transfers between devices, body(): lines.append(lax.ppermute(merged, 'sub', xor_links(subs, distance)))  1.48 us
  transfers between devices with their start and end apart: 10, of which 4 were waited for; matrix products, arithmetic and copies ran while one was open for 0% of the time, Pallas kernels for 33%

profile of v5, /device:TPU:0, one launch (start us, length us, event | category | flops | bytes accessed | tf_op | source)
XLA Modules:
  0.0 34.7 jit_solution(7778777174719271050)
XLA Ops:
  0.0 1.0 %send.1 = (bf16[33,16,128]{2,1,0:T(8,128)(2,1)S(1)}, bf16[34,16,128]{2,1,0:T(8,128)(2,1)S(1)}, bf16[4,16,128]{2,1,0:T(8,128)(2,1)S(1)}, bf16[4,16,128]{2,1,0:T(8...) custom-call(bf16[4,32,16,128]{3,2,1,0:T(8,128)(2,1)} %refs_4_.1, s32[3,8]{1,0:T(4,128)} %bitcast.43, s32[8,6]{1,0:T(8,128)} %links.1), custom_call_target="tpu_custom_call" | custom-call | tf_op jit(solution)/shard_map/send/pallas_call | solution.py:576
  1.0 0.6 %collective-permute-start = (bf16[33,16,128]{2,1,0:T(8,128)(2,1)S(1)}, bf16[33,16,128]{2,1,0:T(8,128)(2,1)S(1)}, u32[]{:S(2)}, u32[]{:S(2)}) collective-permute-start(bf16[33,16,128]{2,1,0:T(8,128)(2,1)S(1)} %get-tuple-element.47.refs_1_), channel_id=1, source_target_pairs={{0,4},{4,0},{8,12},{12,8},{1,5},{5,1},{9,13},{13,9},{2,6},{6,2},{1... | collective-permute-start | bytes 405512 | tf_op jit(solution)/shard_map/ppermute | solution.py:592
  1.6 1.0 %collective-permute-done.x_first.refs_3_ = bf16[33,16,128]{2,1,0:T(8,128)(2,1)S(1)} collective-permute-done((bf16[33,16,128]{2,1,0:T(8,128)(2,1)S(1)}, bf16[33,16,128]{2,1,0:T(8,128)(2,1)S(1)}, u32[]{:S(2)}, u32[]{:S(2)}) %collective-permute-start) | collective-permute-done | bytes 135200 | tf_op jit(solution)/shard_map/ppermute | solution.py:592
  2.6 2.6 %collective-permute-start.1 = (bf16[34,16,128]{2,1,0:T(8,128)(2,1)S(1)}, bf16[34,16,128]{2,1,0:T(8,128)(2,1)S(1)}, u32[]{:S(2)}, u32[]{:S(2)}) collective-permute-start(bf16[34,16,128]{2,1,0:T(8,128)(2,1)S(1)} %relay.1.refs_3_), channel_id=1, source_target_pairs={{0,12},{4,8},{8,4},{12,0},{1,13},{5,9},{9,5},{13,1},{2,14},{6,10},... | collective-permute-start | bytes 417800 | tf_op jit(solution)/shard_map/ppermute | solution.py:603
  5.2 0.0 copy-start
  5.2 4.4 %fine_part.3 = (f32[3,512,128]{2,1,0:T(8,128)S(1)}, bf16[8,512,128]{2,1,0:T(8,128)(2,1)S(1)}, bf16[27,128,128]{2,1,0:T(8,128)(2,1)S(1)}, bf16[6,34,16,128]{3,2,1,0:T(8,128)(2,1)S(1)}, bf16[4,512,512]{2,1,0:T(8,128)(2,1)S(1)}) custom-call(s32[8,6]{1,0:T(8,128)S(1)} %get-tuple-element.46.refs_0_.refs_1_, bf16[8,512,128]{2,1,0:T(8,128)(2,1)} %refs_1_.1, ...), custom_call_target="tpu_custom_call" | custom-call | flops 1358954496 | bytes 786432 | tf_op jit(solution)/shard_map/fine_part/pallas_call | solution.py:540
  9.7 0.0 collective-permute-done.1.x_second.refs_2_.refs_4_
  9.7 1.6 %collective-permute-start.2 = (bf16[6,16,128]{2,1,0:T(8,128)(2,1)S(1)}, bf16[6,16,128]{2,1,0:T(8,128)(2,1)S(1)}, u32[]{:S(2)}, u32[]{:S(2)}) collective-permute-start(bf16[6,16,128]{2,1,0:T(8,128)(2,1)S(1)} %get-tuple-element.58.refs_6_), channel_id=1, source_target_pairs={{0,1},{1,0},{2,3},{3,2},{4,5},{5,4},{6,7},{7,6},{8,9},{9,8},{10,11... | collective-permute-start | bytes 73736 | tf_op jit(solution)/shard_map/ppermute | solution.py:631
  11.3 0.7 %collective-permute-start.3 = (bf16[6,16,128]{2,1,0:T(8,128)(2,1)S(1)}, bf16[6,16,128]{2,1,0:T(8,128)(2,1)S(1)}, u32[]{:S(2)}, u32[]{:S(2)}) collective-permute-start(bf16[6,16,128]{2,1,0:T(8,128)(2,1)S(1)} %get-tuple-element.62), channel_id=1, source_target_pairs={{1,2},{2,1},{5,6},{6,5},{9,10},{10,9},{13,14},{14,13},{17,18},{18,... | collective-permute-start | bytes 73736 | tf_op jit(solution)/shard_map/ppermute | solution.py:632
  12.0 0.0 copy-done
  12.0 2.7 %coarse.1 = (bf16[6,34,16,128]{3,2,1,0:T(8,128)(2,1)S(1)}, f32[4,32,16,128]{3,2,1,0:T(8,128)S(1)}, f32[8,128]{1,0:T(8,128)S(1)}, s32[4,128]{1,0:T(4,128)S(1)}) custom-call(bf16[6,34,16,128]{3,2,1,0:T(8,128)(2,1)S(1)} %get-tuple-element.54.refs_0_, bf16[33,16,128]{2,1,0:T(8,128)(2,1)S(1)} %get-tuple-element.47.refs_1_, ...), custom_call_target="tpu_custom_call", output_to_operand_aliasing={{0}: (0, {})} | custom-call | flops 1811939328 | bytes 1048576 | tf_op jit(solution)/shard_map/coarse/pallas_call | solution.py:634
  14.7 0.0 collective-permute-done.2.refs_3_
  14.7 0.0 collective-permute-done.3.refs_4_
  14.7 0.9 %edge.1 = (bf16[144,128]{1,0:T(8,128)(2,1)S(1)}, bf16[144,128]{1,0:T(8,128)(2,1)S(1)}, bf16[144,128]{1,0:T(8,128)(2,1)S(1)}, bf16[144,128]{1,0:T(8,128)(2,1)S(1)}, f32[4,32,16,128]{3,2,1,0:T(8,128)S(1)}) custom-call(s32[4,128]{1,0:T(4,128)S(1)} %get-tuple-element.59.refs_0_, ...), custom_call_target="tpu_custom_call", output_to_operand_aliasing={{4}: (1, {})} | custom-call | tf_op jit(solution)/shard_map/edge/pallas_call | solution.py:662
  15.6 0.3 collective-permute-start.4
  15.9 1.4 %collective-permute-start.5 = (bf16[144,128]{1,0:T(8,128)(2,1)S(1)}, bf16[144,128]{1,0:T(8,128)(2,1)S(1)}, u32[]{:S(2)}, u32[]{:S(2)}) collective-permute-start(bf16[144,128]{1,0:T(8,128)(2,1)S(1)} %get-tuple-element.69), channel_id=1, source_target_pairs={{0,8},{4,12},{8,0},{12,4},{1,9},{5,13},{9,1},{13,5},{2,10},{6,14},... | collective-permute-start | bytes 110600 | tf_op jit(solution)/shard_map/ppermute | solution.py:681
  17.3 0.2 collective-permute-start.6
  17.5 2.4 %fine_part.4.refs_16_ = f32[3,512,128]{2,1,0:T(8,128)S(1)} custom-call(s32[8,6]{1,0:T(8,128)S(1)} %get-tuple-element.46.refs_0_.refs_1_, bf16[8,512,128]{2,1,0:T(8,128)(2,1)S(1)} %get-tuple-element.71.refs_1_.refs_13_, bf16[27,128,128]{2,1,0:T(8,128)(2,1)S(1)} %get-tuple-element.72.refs_2_, bf16[144,128]{1,0:T(8,128)(2,1)S(1)} %get-tuple-element.67.refs_3_.refs_2_), custom_call_target="tpu_custom_call" | custom-call | flops 1358954496 | bytes 786432 | tf_op jit(solution)/shard_map/fine_part/pallas_call | solution.py:540
  20.0 0.0 copy-start.1
  20.0 0.0 copy-start.2
  20.0 0.0 copy-start.3
  20.0 0.0 collective-permute-done.4.refs_3_
  20.0 0.0 collective-permute-done.5.refs_4_
  20.1 0.7 %collective-permute-done.6.refs_5_ = bf16[144,128]{1,0:T(8,128)(2,1)S(1)} collective-permute-done((bf16[144,128]{1,0:T(8,128)(2,1)S(1)}, bf16[144,128]{1,0:T(8,128)(2,1)S(1)}, u32[]{:S(2)}, u32[]{:S(2)}) %collective-permute-start.6) | collective-permute-done | bytes 36896 | tf_op jit(solution)/shard_map/ppermute | solution.py:681
  20.9 4.5 %collective-permute-start.7 = (f32[2,128]{1,0:T(2,128)S(1)}, f32[2,128]{1,0:T(2,128)S(1)}, u32[]{:S(2)}, u32[]{:S(2)}) collective-permute-start(f32[2,128]{1,0:T(2,128)S(1)} %pad_maximum_fusion.refs_3_.refs_6_), channel_id=1, source_target_pairs={{0,1},{1,0},{2,3},{3,2},{4,5},{5,4},{6,7},{7,6},{8,9},{9,8},{10,11... | collective-permute-start | bytes 3080 | tf_op jit(solution)/shard_map/ppermute | solution.py:693
  25.3 0.4 %collective-permute-start.8 = (f32[2,128]{1,0:T(2,128)S(1)}, f32[2,128]{1,0:T(2,128)S(1)}, u32[]{:S(2)}, u32[]{:S(2)}) collective-permute-start(f32[2,128]{1,0:T(2,128)S(1)} %pad_maximum_fusion.refs_3_.refs_6_), channel_id=1, source_target_pairs={{0,2},{1,3},{2,0},{3,1},{4,6},{5,7},{6,4},{7,5},{8,10},{9,11},{10,... | collective-permute-start | bytes 3080 | tf_op jit(solution)/shard_map/ppermute | solution.py:693
  25.8 2.0 %collective-permute-start.9 = (f32[2,128]{1,0:T(2,128)S(1)}, f32[2,128]{1,0:T(2,128)S(1)}, u32[]{:S(2)}, u32[]{:S(2)}) collective-permute-start(f32[2,128]{1,0:T(2,128)S(1)} %pad_maximum_fusion.refs_3_.refs_6_), channel_id=1, source_target_pairs={{0,3},{1,2},{2,1},{3,0},{4,7},{5,6},{6,5},{7,4},{8,11},{9,10},{10,... | collective-permute-start | bytes 3080 | tf_op jit(solution)/shard_map/ppermute | solution.py:693
  27.8 1.9 %fine_part.5.refs_17_ = f32[2,512,128]{2,1,0:T(8,128)S(1)} custom-call(s32[8,6]{1,0:T(8,128)S(1)} %get-tuple-element.46.refs_0_.refs_1_, bf16[8,512,128]{2,1,0:T(8,128)(2,1)S(1)} %get-tuple-element.71.refs_1_.refs_13_, bf16[27,128,128]{2,1,0:T(8,128)(2,1)S(1)} %get-tuple-element.72.refs_2_, f32[2,128]{1,0:T(2,128)S(1)} %pad_maximum_fusion.refs_3_.refs_6_), custom_call_target="tpu_custom_call" | custom-call | flops 905969664 | bytes 524288 | tf_op jit(solution)/shard_map/fine_part/pallas_call | solution.py:540
  29.6 0.0 collective-permute-done.7.refs_7_
  29.7 0.1 collective-permute-done.8.refs_8_
  29.8 1.3 %collective-permute-done.9.refs_9_ = f32[2,128]{1,0:T(2,128)S(1)} collective-permute-done((f32[2,128]{1,0:T(2,128)S(1)}, f32[2,128]{1,0:T(2,128)S(1)}, u32[]{:S(2)}, u32[]{:S(2)}) %collective-permute-start.9) | collective-permute-done | bytes 1056 | tf_op jit(solution)/shard_map/ppermute | solution.py:693
  31.1 0.0 copy-done.1
  31.1 0.0 copy-done.2
  31.1 0.0 copy-done.3
  31.1 3.5 %final.1 = bf16[8,512,128]{2,1,0:T(8,128)(2,1)} custom-call(s32[3,8]{1,0:T(4,128)S(1)} %get-tuple-element.45.refs_0_, s32[8,6]{1,0:T(8,128)S(1)} %get-tuple-element.46.refs_0_.refs_1_, bf16[144,128]{1,0:T(8,128)(2,1)S(1)} %get-tuple-element.67.refs_3_.refs_2_, bf16[144,128]{1,0:T(8,128)(2,1)S(1)} %collective-permute-done.4.refs_3_, ...), custom_call_target="tpu_custom_call" | custom-call | tf_op jit(solution)/shard_map/final/pallas_call | solution.py:699
  (10 shorter events, 0.1 us)
Async XLA Ops:
  1.0 1.6 %collective-permute-start = (bf16[33,16,128]{2,1,0:T(8,128)(2,1)S(1)}, bf16[33,16,128]{2,1,0:T(8,128)(2,1)S(1)}, u32[]{:S(2)}, u32[]{:S(2)}) collective-permute-start(bf16[33,16,128]{2,1,0:T(8,128)(2,1)S(1)} %get-tuple-element.47.refs_1_), channel_id=1, source_target_pairs={{0,4},{4,0},{8,12},{12,8},{1,5},{5,1},{9,13},{13,9},{2,6},{6,2},{1... | collective-permute-start | bytes 405512 | tf_op jit(solution)/shard_map/ppermute | solution.py:592
  2.6 7.1 %collective-permute-start.1 = (bf16[34,16,128]{2,1,0:T(8,128)(2,1)S(1)}, bf16[34,16,128]{2,1,0:T(8,128)(2,1)S(1)}, u32[]{:S(2)}, u32[]{:S(2)}) collective-permute-start(bf16[34,16,128]{2,1,0:T(8,128)(2,1)S(1)} %relay.1.refs_3_), channel_id=1, source_target_pairs={{0,12},{4,8},{8,4},{12,0},{1,13},{5,9},{9,5},{13,1},{2,14},{6,10},... | collective-permute-start | bytes 417800 | tf_op jit(solution)/shard_map/ppermute | solution.py:603
  5.2 6.8 %copy-start = (bf16[27,128,128]{2,1,0:T(8,128)(2,1)S(1)}, bf16[27,128,128]{2,1,0:T(8,128)(2,1)}, u32[]{:S(2)}) copy-start(bf16[27,128,128]{2,1,0:T(8,128)(2,1)} %refs_5_.3) | copy-start | bytes 2654212
  9.7 5.0 %collective-permute-start.2 = (bf16[6,16,128]{2,1,0:T(8,128)(2,1)S(1)}, bf16[6,16,128]{2,1,0:T(8,128)(2,1)S(1)}, u32[]{:S(2)}, u32[]{:S(2)}) collective-permute-start(bf16[6,16,128]{2,1,0:T(8,128)(2,1)S(1)} %get-tuple-element.58.refs_6_), channel_id=1, source_target_pairs={{0,1},{1,0},{2,3},{3,2},{4,5},{5,4},{6,7},{7,6},{8,9},{9,8},{10,11... | collective-permute-start | bytes 73736 | tf_op jit(solution)/shard_map/ppermute | solution.py:631
  11.3 3.4 %collective-permute-start.3 = (bf16[6,16,128]{2,1,0:T(8,128)(2,1)S(1)}, bf16[6,16,128]{2,1,0:T(8,128)(2,1)S(1)}, u32[]{:S(2)}, u32[]{:S(2)}) collective-permute-start(bf16[6,16,128]{2,1,0:T(8,128)(2,1)S(1)} %get-tuple-element.62), channel_id=1, source_target_pairs={{1,2},{2,1},{5,6},{6,5},{9,10},{10,9},{13,14},{14,13},{17,18},{18,... | collective-permute-start | bytes 73736 | tf_op jit(solution)/shard_map/ppermute | solution.py:632
  15.6 4.4 %collective-permute-start.4 = (bf16[144,128]{1,0:T(8,128)(2,1)S(1)}, bf16[144,128]{1,0:T(8,128)(2,1)S(1)}, u32[]{:S(2)}, u32[]{:S(2)}) collective-permute-start(bf16[144,128]{1,0:T(8,128)(2,1)S(1)} %get-tuple-element.68), channel_id=1, source_target_pairs={{0,4},{4,0},{8,12},{12,8},{1,5},{5,1},{9,13},{13,9},{2,6},{6,2},{1... | collective-permute-start | bytes 110600 | tf_op jit(solution)/shard_map/ppermute | solution.py:681
  15.9 4.1 %collective-permute-start.5 = (bf16[144,128]{1,0:T(8,128)(2,1)S(1)}, bf16[144,128]{1,0:T(8,128)(2,1)S(1)}, u32[]{:S(2)}, u32[]{:S(2)}) collective-permute-start(bf16[144,128]{1,0:T(8,128)(2,1)S(1)} %get-tuple-element.69), channel_id=1, source_target_pairs={{0,8},{4,12},{8,0},{12,4},{1,9},{5,13},{9,1},{13,5},{2,10},{6,14},... | collective-permute-start | bytes 110600 | tf_op jit(solution)/shard_map/ppermute | solution.py:681
  17.3 3.4 %collective-permute-start.6 = (bf16[144,128]{1,0:T(8,128)(2,1)S(1)}, bf16[144,128]{1,0:T(8,128)(2,1)S(1)}, u32[]{:S(2)}, u32[]{:S(2)}) collective-permute-start(bf16[144,128]{1,0:T(8,128)(2,1)S(1)} %get-tuple-element.70), channel_id=1, source_target_pairs={{0,12},{4,8},{8,4},{12,0},{1,13},{5,9},{9,5},{13,1},{2,14},{6,10},... | collective-permute-start | bytes 110600 | tf_op jit(solution)/shard_map/ppermute | solution.py:681
  20.0 11.2 %copy-start.1 = (bf16[128,128]{1,0:T(8,128)(2,1)S(1)}, bf16[128,128]{1,0:T(8,128)(2,1)}, u32[]{:S(2)}) copy-start(bf16[128,128]{1,0:T(8,128)(2,1)} %refs_12_.1) | copy-start | bytes 98308
  20.0 11.1 %copy-start.2 = (f32[128]{0:T(128)S(1)}, f32[128]{0:T(128)}, u32[]{:S(2)}) copy-start(f32[128]{0:T(128)} %param.11) | copy-start | bytes 1540
  20.0 11.1 %copy-start.3 = (f32[128]{0:T(128)S(1)}, f32[128]{0:T(128)}, u32[]{:S(2)}) copy-start(f32[128]{0:T(128)} %param.12) | copy-start | bytes 1540
  20.9 8.8 %collective-permute-start.7 = (f32[2,128]{1,0:T(2,128)S(1)}, f32[2,128]{1,0:T(2,128)S(1)}, u32[]{:S(2)}, u32[]{:S(2)}) collective-permute-start(f32[2,128]{1,0:T(2,128)S(1)} %pad_maximum_fusion.refs_3_.refs_6_), channel_id=1, source_target_pairs={{0,1},{1,0},{2,3},{3,2},{4,5},{5,4},{6,7},{7,6},{8,9},{9,8},{10,11... | collective-permute-start | bytes 3080 | tf_op jit(solution)/shard_map/ppermute | solution.py:693
  25.3 4.5 %collective-permute-start.8 = (f32[2,128]{1,0:T(2,128)S(1)}, f32[2,128]{1,0:T(2,128)S(1)}, u32[]{:S(2)}, u32[]{:S(2)}) collective-permute-start(f32[2,128]{1,0:T(2,128)S(1)} %pad_maximum_fusion.refs_3_.refs_6_), channel_id=1, source_target_pairs={{0,2},{1,3},{2,0},{3,1},{4,6},{5,7},{6,4},{7,5},{8,10},{9,11},{10,... | collective-permute-start | bytes 3080 | tf_op jit(solution)/shard_map/ppermute | solution.py:693
  25.8 5.4 %collective-permute-start.9 = (f32[2,128]{1,0:T(2,128)S(1)}, f32[2,128]{1,0:T(2,128)S(1)}, u32[]{:S(2)}, u32[]{:S(2)}) collective-permute-start(f32[2,128]{1,0:T(2,128)S(1)} %pad_maximum_fusion.refs_3_.refs_6_), channel_id=1, source_target_pairs={{0,3},{1,2},{2,1},{3,0},{4,7},{5,6},{6,5},{7,4},{8,11},{9,10},{10,... | collective-permute-start | bytes 3080 | tf_op jit(solution)/shard_map/ppermute | solution.py:693
